TPU v7x, 32 devices: a whole 2x2x4 slice. The times are simulated.
32 devices in a mesh: rep: 2 (over x), shard: 16 (over z, y, core).
Axes of the slice: x: 2, y: 2, z: 4, core: 2. Of those that a mesh axis runs over, the one named last changes fastest.
Arguments:
- block_input: bfloat16 [4096, 2048], P(('rep', 'shard')), may hold values from -6 to 6
- out_grad: bfloat16 [4096, 2048], P(('rep', 'shard')), may hold values from -6 to 6
- segments: int32 [32, 128], P(('rep', 'shard')), may hold values from 0 to 2, as said below
- positions: int32 [32, 128], P(('rep', 'shard')), may hold values from 0 to 1023, as said below
- attn_gain: float32 [2048], replicated, may hold values from 0.5 to 1.5
- mlp_gain: float32 [2048], replicated, may hold values from 0.5 to 1.5
- q_gain: float32 [128], replicated, may hold values from 0.5 to 2
- k_gain: float32 [128], replicated, may hold values from 0.5 to 2
- w_q: bfloat16 [2048, 2048], P('shard'), may hold values from -0.125 to 0.125
- key_matrix: bfloat16 [2048, 1024], P('shard'), may hold values from -0.125 to 0.125
- value_matrix: bfloat16 [2048, 1024], P('shard'), may hold values from -0.125 to 0.125
- w_o: bfloat16 [2048, 2048], P('shard'), may hold values from -0.75 to 0.75
- w_gate: bfloat16 [2048, 6144], P('shard'), may hold values from -0.125 to 0.125
- w_up: bfloat16 [2048, 6144], P('shard'), may hold values from -0.125 to 0.125
- w_down: bfloat16 [2048, 6144], P('shard'), may hold values from -0.078125 to 0.078125
Outputs:
- output: bfloat16 [4096, 2048], P(('rep', 'shard'))
- grad_input: float32 [4096, 2048], P(('rep', 'shard'))
- grad_w_q: float32 [2048, 2048], P('shard')
- grad_w_k: float32 [2048, 1024], P('shard')
- grad_w_v: float32 [2048, 1024], P('shard')
- grad_w_o: float32 [2048, 2048], P('shard')
- grad_w_gate: float32 [2048, 6144], P('shard')
- grad_w_up: float32 [2048, 6144], P('shard')
- grad_w_down: float32 [2048, 6144], P('shard')
- grad_attn_gain: float32 [2048], replicated
- grad_mlp_gain: float32 [2048], replicated
- grad_q_gain: float32 [128], replicated
- grad_k_gain: float32 [128], replicated
Inputs may be any that keep to these rules, and one draw needn't show every extreme that they name: `segments`: in each sequence the segment numbers never fall, the first token has 0 and the last has 2. Within a segment the positions rise by one from token to token; segments 1 and 2 start at position 0.
All inputs are finite; a program needn't handle non-finite values.
Results may differ from a plain program's by a relative error of at most 0.015.
Values may be sent and summed in bfloat16 or wider, within the bound.
No kernel may reach another device: no remote copies, remote signals or barrier semaphores. Data moves between devices by JAX's collectives and lax.ppermute only.
A program may use at most 768 MiB of HBM per device.

v0:
```python
import math

import jax
import jax.numpy as jnp
from jax import lax
from jax.sharding import PartitionSpec as P

EPSILON = 1e-06
ROPE_BASE = 1000000.0
NEG_FILL = -1e30


def rope_tables(positions, half):
    freq = jnp.exp(jnp.arange(half, dtype=jnp.float32) * (-math.log(ROPE_BASE) / half))
    angles = positions.reshape(-1).astype(jnp.float32)[:, None, None] * freq
    return (jnp.cos(angles), jnp.sin(angles))


def rotate(vectors, cosine, sine):
    half = vectors.shape[-1] // 2
    first, second = (vectors[..., :half], vectors[..., half:])
    return jnp.concatenate([first * cosine - second * sine, second * cosine + first * sine], -1)


def unrotate(grads, cosine, sine):
    half = grads.shape[-1] // 2
    first, second = (grads[..., :half], grads[..., half:])
    return jnp.concatenate([first * cosine + second * sine, second * cosine - first * sine], -1)


def head_norm(heads, gain):
    recip = lax.rsqrt(jnp.mean(heads * heads, -1, keepdims=True) + EPSILON)
    return (heads * recip * gain, recip)


def norm_back(grads, inputs, recip, gain, axes):
    normal = inputs * recip
    scaled = grads * gain
    gain_grad = jnp.sum(grads * normal, axis=axes)
    input_grad = recip * (scaled - normal * jnp.mean(scaled * normal, -1, keepdims=True))
    return (input_grad, gain_grad)


def attention_mask(segments):
    packed_length = segments.shape[1]
    same = segments[:, :, None] == segments[:, None, :]
    places = jnp.arange(packed_length)
    causal = places[None, :] <= places[:, None]
    return same & causal[None]


def contract_rows(left, right):
    return lax.dot_general(
        left, right, (((0,), (0,)), ((), ())), preferred_element_type=jnp.float32
    )


def contract_cols(left, right):
    return lax.dot_general(
        left, right, (((1,), (1,)), ((), ())), preferred_element_type=jnp.float32
    )


def head_scores(rotated_query_rows, rotated_key_rows, mask, kv_heads, head):
    sequence_list, packed_length = (mask.shape[0], mask.shape[1])
    groups = rotated_query_rows.shape[1] // kv_heads
    query_rows = rotated_query_rows.reshape(sequence_list, packed_length, kv_heads, groups, head)
    every_key_row = rotated_key_rows.reshape(sequence_list, packed_length, kv_heads, head)
    scores = jnp.einsum(
        "slkgd,smkd->skglm", query_rows, every_key_row, preferred_element_type=jnp.float32
    ) * head ** (-0.5)
    return (jnp.where(mask[:, None, None], scores, NEG_FILL), query_rows, every_key_row)


def attend_forward(rotated_query_rows, rotated_key_rows, value_rows, mask):
    sequence_list, packed_length = (mask.shape[0], mask.shape[1])
    kv_heads, head = (value_rows.shape[1], value_rows.shape[2])
    scores, query_rows, every_key_row = head_scores(
        rotated_query_rows, rotated_key_rows, mask, kv_heads, head
    )
    top = jnp.max(scores, -1, keepdims=True)
    expo = jnp.exp(scores - top)
    total = jnp.sum(expo, -1, keepdims=True)
    probs = (expo / total).astype(jnp.bfloat16)
    log_total = top + jnp.log(total)
    value_heads = value_rows.reshape(sequence_list, packed_length, kv_heads, head)
    attended_rows = jnp.einsum(
        "skglm,smkd->slkgd", probs, value_heads, preferred_element_type=jnp.float32
    )
    return (
        attended_rows.reshape(
            sequence_list * packed_length, rotated_query_rows.shape[1] * head
        ).astype(jnp.bfloat16),
        log_total,
    )


def attend_backward(
    rotated_query_rows,
    rotated_key_rows,
    value_rows,
    attended_rows,
    attended_gradient,
    log_total,
    mask,
):
    sequence_list, packed_length = (mask.shape[0], mask.shape[1])
    kv_heads, head = (value_rows.shape[1], value_rows.shape[2])
    groups = rotated_query_rows.shape[1] // kv_heads
    scores, query_rows, every_key_row = head_scores(
        rotated_query_rows, rotated_key_rows, mask, kv_heads, head
    )
    probs_back = jnp.where(mask[:, None, None], jnp.exp(scores - log_total), 0.0)
    output_gradient = attended_gradient.reshape(
        sequence_list, packed_length, kv_heads, groups, head
    )
    value_heads = value_rows.reshape(sequence_list, packed_length, kv_heads, head)
    value_rows_gradient = jnp.einsum(
        "skglm,slkgd->smkd",
        probs_back.astype(jnp.bfloat16),
        output_gradient,
        preferred_element_type=jnp.float32,
    )
    grad_probs = jnp.einsum(
        "slkgd,smkd->skglm", output_gradient, value_heads, preferred_element_type=jnp.float32
    )
    complete_output = attended_rows.reshape(
        sequence_list, packed_length, kv_heads, groups, head
    ).astype(jnp.float32)
    delta = jnp.transpose(
        jnp.sum(output_gradient.astype(jnp.float32) * complete_output, -1), (0, 2, 3, 1)
    )[..., None]
    grad_scores = (probs_back * (grad_probs - delta)).astype(jnp.bfloat16)
    rotated_query_gradient = jnp.einsum(
        "skglm,smkd->slkgd", grad_scores, every_key_row, preferred_element_type=jnp.float32
    ) * head ** (-0.5)
    rotated_key_gradient = jnp.einsum(
        "skglm,slkgd->smkd", grad_scores, query_rows, preferred_element_type=jnp.float32
    ) * head ** (-0.5)
    token_rows = sequence_list * packed_length
    return (
        rotated_query_gradient.reshape(token_rows, rotated_query_rows.shape[1], head),
        rotated_key_gradient.reshape(token_rows, kv_heads, head),
        value_rows_gradient.reshape(token_rows, kv_heads, head),
    )


def on_device(
    block_input,
    out_grad,
    segments,
    positions,
    attn_gain,
    mlp_gain,
    q_gain,
    k_gain,
    w_q,
    key_matrix,
    value_matrix,
    w_o,
    w_gate,
    w_up,
    w_down,
):
    tokens, width = block_input.shape
    head = q_gain.shape[0]
    heads = w_q.shape[1] // head
    kv_heads = key_matrix.shape[1] // head
    hidden = w_gate.shape[1]
    mask = attention_mask(segments)
    cosine, sine = rope_tables(positions, head // 2)
    inputs = block_input.astype(jnp.float32)
    recip_attn = lax.rsqrt(jnp.mean(inputs * inputs, -1, keepdims=True) + EPSILON)
    normed_rows = (inputs * recip_attn * attn_gain).astype(jnp.bfloat16)
    pieces = (
        lax.all_gather(w_q, "shard", axis=0, tiled=True),
        lax.all_gather(key_matrix, "shard", axis=0, tiled=True),
        lax.all_gather(value_matrix, "shard", axis=0, tiled=True),
    )
    columns = normed_rows
    q_proj, k_proj, v_proj = tuple(
        (
            jnp.dot(columns, weight_piece, preferred_element_type=jnp.float32)
            for weight_piece in pieces
        )
    )
    q_heads = q_proj.reshape(tokens, heads, head)
    key_head_rows = k_proj.reshape(tokens, kv_heads, head)
    q_normed, q_recip = head_norm(q_heads, q_gain)
    k_normed, k_recip = head_norm(key_head_rows, k_gain)
    rotated_query_rows = rotate(q_normed, cosine, sine).astype(jnp.bfloat16)
    rotated_key_rows = rotate(k_normed, cosine, sine).astype(jnp.bfloat16)
    value_rows = v_proj.astype(jnp.bfloat16).reshape(tokens, kv_heads, head)
    attended_rows, log_total = attend_forward(
        rotated_query_rows, rotated_key_rows, value_rows, mask
    )
    attn_out = contract_cols(attended_rows, lax.all_gather(w_o, "shard", axis=0, tiled=True))
    mid = inputs + attn_out
    recip_mlp = lax.rsqrt(jnp.mean(mid * mid, -1, keepdims=True) + EPSILON)
    mlp_in = (mid * recip_mlp * mlp_gain).astype(jnp.bfloat16)
    pieces = (
        lax.all_gather(w_gate, "shard", axis=0, tiled=True),
        lax.all_gather(w_up, "shard", axis=0, tiled=True),
    )
    columns = mlp_in
    gate_pre = jnp.dot(columns, pieces[0], preferred_element_type=jnp.float32)
    up_pre = jnp.dot(columns, pieces[1], preferred_element_type=jnp.float32)
    sigma = jax.nn.sigmoid(gate_pre)
    silu_gate = gate_pre * sigma
    act = (silu_gate * up_pre).astype(jnp.bfloat16)
    mlp_out = contract_cols(act, lax.all_gather(w_down, "shard", axis=0, tiled=True))
    output = (mid + mlp_out).astype(jnp.bfloat16)
    grad_top = out_grad.astype(jnp.float32)
    columns = out_grad
    grad_act = jnp.dot(
        columns,
        lax.all_gather(w_down, "shard", axis=0, tiled=True),
        preferred_element_type=jnp.float32,
    )
    grad_gate = (grad_act * up_pre * sigma * (1.0 + gate_pre * (1.0 - sigma))).astype(jnp.bfloat16)
    grad_up = (grad_act * silu_gate).astype(jnp.bfloat16)
    pieces = (
        lax.all_gather(w_gate, "shard", axis=0, tiled=True),
        lax.all_gather(w_up, "shard", axis=0, tiled=True),
    )
    part = contract_cols(grad_gate, pieces[0]) + contract_cols(grad_up, pieces[1])
    grad_mlp_in = part
    mlp_right = jnp.concatenate([grad_gate, grad_up], 1)
    left_in = mlp_in
    left_grad = out_grad
    mlp_grads = lax.psum_scatter(
        jnp.concatenate([contract_rows(left_in, mlp_right), contract_rows(left_grad, act)], 1),
        "shard",
        scatter_dimension=0,
        tiled=True,
    )
    grad_mid_part, mlp_gain_part = norm_back(grad_mlp_in, mid, recip_mlp, mlp_gain, 0)
    grad_mid = grad_top + grad_mid_part
    grad_mid_b = grad_mid.astype(jnp.bfloat16)
    columns = grad_mid_b
    attended_gradient = jnp.dot(
        columns,
        lax.all_gather(w_o, "shard", axis=0, tiled=True),
        preferred_element_type=jnp.float32,
    ).astype(jnp.bfloat16)
    rotated_query_gradient, rotated_key_gradient, value_rows_gradient = attend_backward(
        rotated_query_rows,
        rotated_key_rows,
        value_rows,
        attended_rows,
        attended_gradient,
        log_total,
        mask,
    )
    grad_qh, q_gain_part = norm_back(
        unrotate(rotated_query_gradient, cosine, sine), q_heads, q_recip, q_gain, (0, 1)
    )
    key_heads_gradient, k_gain_part = norm_back(
        unrotate(rotated_key_gradient, cosine, sine), key_head_rows, k_recip, k_gain, (0, 1)
    )
    grad_q = grad_qh.reshape(tokens, heads * head).astype(jnp.bfloat16)
    key_gradient = key_heads_gradient.reshape(tokens, kv_heads * head).astype(jnp.bfloat16)
    value_gradient = value_rows_gradient.reshape(tokens, kv_heads * head).astype(jnp.bfloat16)
    pieces = (
        lax.all_gather(w_q, "shard", axis=0, tiled=True),
        lax.all_gather(key_matrix, "shard", axis=0, tiled=True),
        lax.all_gather(value_matrix, "shard", axis=0, tiled=True),
    )
    part = (
        contract_cols(grad_q, pieces[0])
        + contract_cols(key_gradient, pieces[1])
        + contract_cols(value_gradient, pieces[2])
    )
    attn_right = jnp.concatenate([grad_q, key_gradient, value_gradient], 1)
    left_in = normed_rows
    left_grad = grad_mid_b
    attn_grads = lax.psum_scatter(
        jnp.concatenate(
            [contract_rows(left_in, attn_right), contract_rows(left_grad, attended_rows)], 1
        ),
        "shard",
        scatter_dimension=0,
        tiled=True,
    )
    grad_in_part, attn_gain_part = norm_back(part, inputs, recip_attn, attn_gain, 0)
    grad_input = grad_mid + grad_in_part
    gain_totals = lax.psum(
        (attn_gain_part, mlp_gain_part, q_gain_part, k_gain_part), ("rep", "shard")
    )
    attn_total, mlp_total = (
        lax.psum(attn_grads.astype(jnp.bfloat16), "rep").astype(jnp.float32),
        lax.psum(mlp_grads.astype(jnp.bfloat16), "rep").astype(jnp.float32),
    )
    q_cols = heads * head
    k_cols = kv_heads * head
    grad_w_q = attn_total[:, :q_cols]
    grad_w_k = attn_total[:, q_cols : q_cols + k_cols]
    grad_w_v = attn_total[:, q_cols + k_cols : q_cols + 2 * k_cols]
    grad_w_o = attn_total[:, q_cols + 2 * k_cols :]
    grad_w_gate = mlp_total[:, :hidden]
    grad_w_up = mlp_total[:, hidden : 2 * hidden]
    grad_w_down = mlp_total[:, 2 * hidden :]
    return (
        output,
        grad_input,
        grad_w_q,
        grad_w_k,
        grad_w_v,
        grad_w_o,
        grad_w_gate,
        grad_w_up,
        grad_w_down,
        gain_totals[0],
        gain_totals[1],
        gain_totals[2],
        gain_totals[3],
    )


def solution(mesh):
    placed = (
        P(("rep", "shard"), None),
        P(("rep", "shard"), None),
        P(("rep", "shard"), None),
        P(("rep", "shard"), None),
        P(),
        P(),
        P(),
        P(),
        P("shard", None),
        P("shard", None),
        P("shard", None),
        P("shard", None),
        P("shard", None),
        P("shard", None),
        P("shard", None),
    )
    return jax.shard_map(
        on_device,
        mesh=mesh,
        in_specs=placed,
        out_specs=(
            P(("rep", "shard"), None),
            P(("rep", "shard"), None),
            P("shard", None),
            P("shard", None),
            P("shard", None),
            P("shard", None),
            P("shard", None),
            P("shard", None),
            P("shard", None),
            P(),
            P(),
            P(),
            P(),
        ),
        check_vma=False,
    )
```

profile of v0, /device:TPU:0, one launch (start us, length us, event | category | flops | bytes accessed | tf_op | source)
XLA Modules:
  0.0 2806.3 jit_solution(15419628978582923309)
XLA Ops:
  14.5 49.1 %all-gather.8.cloned.1.call-done = bf16[2048,1024]{1,0:T(8,128)(2,1)} async-done(((bf16[128,1024]{1,0:T(8,128)(2,1)}), bf16[2048,1024]{1,0:T(8,128)(2,1)}) %all-gather.8.cloned.1.call-update) | async-done | bytes 4194320 | tf_op jit(solution)/shard_map/all_gather | solution.py:178
  63.5 2.9 fusion.19
  66.6 48.2 %all-gather.10.cloned.1.call-done = bf16[2048,1024]{1,0:T(8,128)(2,1)} async-done(((bf16[128,1024]{1,0:T(8,128)(2,1)}), bf16[2048,1024]{1,0:T(8,128)(2,1)}) %all-gather.10.cloned.1.call-update) | async-done | bytes 4194320 | tf_op jit(solution)/shard_map/all_gather | solution.py:177
  114.8 2.9 fusion.66
  119.3 71.0 %all-gather.12.cloned.1.call-done = bf16[2048,2048]{1,0:T(8,128)(2,1)} async-done(((bf16[128,2048]{1,0:T(8,128)(2,1)}), bf16[2048,2048]{1,0:T(8,128)(2,1)}) %all-gather.12.cloned.1.call-update) | async-done | bytes 8388624 | tf_op jit(solution)/shard_map/all_gather | solution.py:176
  190.4 4.7 fusion.64
  200.2 65.4 %all-gather.14.cloned.1.call-done = bf16[2048,2048]{1,0:T(8,128)(2,1)} async-done(((bf16[128,2048]{1,0:T(8,128)(2,1)}), bf16[2048,2048]{1,0:T(8,128)(2,1)}) %all-gather.14.cloned.1.call-update) | async-done | bytes 8388624 | tf_op jit(solution)/shard_map/all_gather | solution.py:197
  265.6 6.4 multiply_reduce_fusion.4
  272.8 121.1 %all-gather.18.cloned.1.call-done = bf16[2048,6144]{1,0:T(8,128)(2,1)} async-done(((bf16[128,6144]{1,0:T(8,128)(2,1)}), bf16[2048,6144]{1,0:T(8,128)(2,1)}) %all-gather.18.cloned.1.call-update) | async-done | bytes 25165840 | tf_op jit(solution)/shard_map/all_gather | solution.py:203
  393.9 13.7 fusion.75
  407.6 116.4 %all-gather.16.cloned.1.call-done = bf16[2048,6144]{1,0:T(8,128)(2,1)} async-done(((bf16[128,6144]{1,0:T(8,128)(2,1)}), bf16[2048,6144]{1,0:T(8,128)(2,1)}) %all-gather.16.cloned.1.call-update) | async-done | bytes 25165840 | tf_op jit(solution)/shard_map/all_gather | solution.py:202
  524.0 13.2 fusion.74
  537.2 117.0 %all-gather.20.cloned.1.call-done = bf16[2048,6144]{1,0:T(8,128)(2,1)} async-done(((bf16[128,6144]{1,0:T(8,128)(2,1)}), bf16[2048,6144]{1,0:T(8,128)(2,1)}) %all-gather.20.cloned.1.call-update) | async-done | bytes 25165840 | tf_op jit(solution)/shard_map/all_gather | solution.py:211
  654.2 14.8 multiply_convert_fusion
  668.9 13.5 fusion.76
  682.5 15.2 multiply_reduce_fusion
  700.0 5.8 convolution_convert_fusion
  717.4 8.1 fusion.50
  740.5 13.6 fusion.31
  754.1 33.6 %pad_maximum_fusion.1 = f32[2048,6144]{1,0:T(8,128)} fusion(f32[2048,2048]{1,0:T(8,128)} %fusion.50, f32[2048,4096]{1,0:T(8,128)} %fusion.31), kind=kLoop, calls=%fused_computation.1 | loop fusion | flops 12582912 | bytes 100663296 | tf_op jit(solution)/shard_map/concatenate | solution.py:278
  789.1 32.8 %convolution_bitcast_fusion = f32[2048,6144]{1,0:T(8,128)} fusion(bf16[128,6144]{1,0:T(8,128)(2,1)S(1)} %copy-done.13, bf16[128,2048]{1,0:T(8,128)(2,1)} %param.16), kind=kOutput, calls=%fused_computation.2 | convolution fusion | flops 3221225472 | bytes 52428800 | tf_op jit(solution)/shard_map/dot_general | solution.py:53
  822.0 48.1 %fusion = f32[2048,12288]{1,0:T(8,128)} fusion(bf16[128,2048]{1,0:T(8,128)(2,1)} %copy-done.15, bf16[128,6144]{1,0:T(8,128)(2,1)} %get-tuple-element.25, bf16[128,6144]{1,0:T(8,128)(2,1)S(1)} %copy-done.14), kind=kOutput, calls=%fused_computation.3 | convolution fusion | flops 6448742400 | bytes 104333312 | tf_op jit(solution)/shard_map/dot_general | solution.py:53
  870.1 100.2 %pad_maximum_fusion = f32[2048,18432]{1,0:T(8,128)} fusion(f32[2048,6144]{1,0:T(8,128)} %convolution_bitcast_fusion, f32[2048,12288]{1,0:T(8,128)} %fusion), kind=kLoop, calls=%fused_computation | loop fusion | flops 37748736 | bytes 301989888 | tf_op jit(solution)/shard_map/concatenate | solution.py:232
  970.6 285.1 %reduce-scatter.3.cloned.1.call-done = f32[128,6144]{1,0:T(8,128)} async-done(((f32[2048,6144]{1,0:T(8,128)}), f32[128,6144]{1,0:T(8,128)}) %reduce-scatter.3.cloned.1.call-update) | async-done | bytes 3145744 | tf_op jit(solution)/shard_map/reduce_scatter | solution.py:277
  1255.7 3.2 convert_element_type.156
  1258.9 1370.2 %reduce-scatter.5.cloned.1.call-done = f32[128,18432]{1,0:T(8,128)} async-done(((f32[2048,18432]{1,0:T(8,128)}), f32[128,18432]{1,0:T(8,128)}) %reduce-scatter.5.cloned.1.call-update) | async-done | bytes 9437200 | tf_op jit(solution)/shard_map/reduce_scatter | solution.py:231
  2629.1 6.5 convert_element_type.158
  2636.7 6.4 fusion.77
  2648.2 40.2 %all-reduce = (f32[2048]{0:T(1024)}, f32[2048]{0:T(1024)}, f32[128]{0:T(128)}, f32[128]{0:T(128)}) all-reduce(f32[2048]{0:T(1024)S(1)} %get-tuple-element.15, f32[2048]{0:T(1024)S(1)} %copy-done.50, f32[128]{0:T(128)S(1)} %bitcast_reduce_fusion, f32[128]{0:T(128)S(1)} %bitcast_reduce_fusion.1), channel_id=1, replica_groups=mesh['rep'=2,'shard'=16] {'rep','shard'}, use_global_device_ids=true, to_apply=%region_16.17 | all-reduce | flops 4352 | bytes 34816 | tf_op jit(solution)/shard_map/psum | solution.py:287
  2691.0 14.2 fusion.5
  2705.2 84.7 %all-reduce.4.cloned.1.call-done = (bf16[128,6144]{1,0:T(8,128)(2,1)}, bf16[128,18432]{1,0:T(8,128)(2,1)}) async-done(((bf16[128,6144]{1,0:T(8,128)(2,1)}, bf16[128,18432]{1,0:T(8,128)(2,1)}), (bf16[128,6144]{1,0:T(8,128)(2,1)}, bf16[128,18432]{1,0:T(8,128)(2,1)})) %all-reduce.4.cloned.1.call-update) | async-done | bytes 6291472 | tf_op jit(solution)/shard_map/psum | solution.py:291
  2795.0 4.0 fusion.69
  (203 shorter events, 58.5 us)
Async XLA Ops:
  7.2 6.2 copy-start.58
  7.2 56.3 %copy-start.37 = (f32[2048]{0:T(1024)S(1)}, f32[2048]{0:T(1024)}, u32[]{:S(2)}) copy-start(f32[2048]{0:T(1024)} %param.19) | copy-start | bytes 24580
  7.2 56.3 %all-gather.8.cloned.1.call-start = ((), (), s32[]{:S(2)}) async-start(), calls=%async_computation.2 | async-start | bytes 4456448 | tf_op jit(solution)/shard_map/all_gather | solution.py:178
  8.0 106.8 %all-gather.10.cloned.1.call-start = ((), (), s32[]{:S(2)}) async-start(), calls=%async_computation.3 | async-start | bytes 4456448 | tf_op jit(solution)/shard_map/all_gather | solution.py:177
  8.7 181.6 %all-gather.12.cloned.1.call-start = ((), (), s32[]{:S(2)}) async-start(), calls=%async_computation.4 | async-start | bytes 8912896 | tf_op jit(solution)/shard_map/all_gather | solution.py:176
  9.5 256.1 %all-gather.14.cloned.1.call-start = ((), (), s32[]{:S(2)}) async-start(), calls=%async_computation.5 | async-start | bytes 8912896 | tf_op jit(solution)/shard_map/all_gather | solution.py:197
  10.0 383.8 %all-gather.18.cloned.1.call-start = ((), (), s32[]{:S(2)}) async-start(), calls=%async_computation.7 | async-start | bytes 26738688 | tf_op jit(solution)/shard_map/all_gather | solution.py:203
  10.6 513.3 %all-gather.16.cloned.1.call-start = ((), (), s32[]{:S(2)}) async-start(), calls=%async_computation.6 | async-start | bytes 26738688 | tf_op jit(solution)/shard_map/all_gather | solution.py:202
  11.2 643.0 %all-gather.20.cloned.1.call-start = ((), (), s32[]{:S(2)}) async-start(), calls=%async_computation.8 | async-start | bytes 26738688 | tf_op jit(solution)/shard_map/all_gather | solution.py:211
  12.0 1243.7 %reduce-scatter.3.cloned.1.call-start = ((), (), s32[]{:S(2)}) async-start(), calls=%async_computation.9 | async-start | bytes 53477376 | tf_op jit(solution)/shard_map/reduce_scatter | solution.py:277
  12.2 178.1 %copy-start.46 = (f32[128]{0:T(128)}, f32[128]{0:T(128)S(1)}, u32[]{:S(2)}) copy-start(f32[128]{0:T(128)S(1)} %add_rsqrt_fusion.3) | copy-start | bytes 1540
  66.5 132.4 %copy-start.36 = (bf16[16,8,8,128]{3,2,1,0:T(8,128)(2,1)}, bf16[16,8,8,128]{3,2,1,0:T(8,128)(2,1)S(1)}, u32[]{:S(2)}) copy-start(bf16[16,8,8,128]{3,2,1,0:T(8,128)(2,1)S(1)} %copy.175) | copy-start | bytes 786436
  119.3 78.8 %copy-start.28 = (bf16[128,8,64]{2,0,1:T(8,128)(2,1)}, bf16[128,8,64]{2,0,1:T(8,128)(2,1)S(1)}, u32[]{:S(2)}) copy-start(bf16[128,8,64]{2,0,1:T(8,128)(2,1)S(1)} %get-tuple-element.50) | copy-start | bytes 393220
  198.2 67.4 %copy-start.22 = (bf16[128,16,64]{2,0,1:T(8,128)(2,1)}, bf16[128,16,64]{2,0,1:T(8,128)(2,1)S(1)}, u32[]{:S(2)}) copy-start(bf16[128,16,64]{2,0,1:T(8,128)(2,1)S(1)} %copy.127) | copy-start | bytes 786436
  200.1 71.8 %copy-start.24 = (bf16[8,128,2,128]{3,1,2,0:T(8,128)(2,1)}, bf16[8,128,2,128]{3,1,2,0:T(8,128)(2,1)S(1)}, u32[]{:S(2)}) copy-start(bf16[8,128,2,128]{3,1,2,0:T(8,128)(2,1)S(1)} %convolution_convert_fusion.1) | copy-start | bytes 1572868
  265.6 7.1 copy-start.42
  271.9 426.4 %copy-start.2 = (f32[128,2048]{1,0:T(8,128)}, f32[128,2048]{1,0:T(8,128)S(1)}, u32[]{:S(2)}) copy-start(f32[128,2048]{1,0:T(8,128)S(1)} %get-tuple-element.56) | copy-start | bytes 3145732
  272.0 121.9 %copy-start.54 = (f32[128]{0:T(128)}, f32[128]{0:T(128)S(1)}, u32[]{:S(2)}) copy-start(f32[128]{0:T(128)S(1)} %add_rsqrt_fusion.2) | copy-start | bytes 1540
  272.8 251.1 %copy-start.15 = (bf16[128,2048]{1,0:T(8,128)(2,1)}, bf16[128,2048]{1,0:T(8,128)(2,1)S(1)}, u32[]{:S(2)}) copy-start(bf16[128,2048]{1,0:T(8,128)(2,1)S(1)} %multiply_convert_fusion.3) | copy-start | bytes 1572868
  407.6 246.6 %copy-start.32 = (bf16[128,2048]{1,0:T(8,128)(2,1)S(1)}, bf16[128,2048]{1,0:T(8,128)(2,1)}, u32[]{:S(2)}) copy-start(bf16[128,2048]{1,0:T(8,128)(2,1)} %param.16) | copy-start | bytes 1572868
  700.0 17.4 copy-start.4
  705.8 6.0 copy-start.43
  717.4 8.1 copy-start.30
  737.6 16.4 copy-start.26
  740.5 13.6 copy-start.18
  787.7 1841.4 %reduce-scatter.5.cloned.1.call-start = ((), (), s32[]{:S(2)}) async-start(), calls=%async_computation.10 | async-start | bytes 160432128 | tf_op jit(solution)/shard_map/reduce_scatter | solution.py:231
  789.1 32.8 %copy-start.14 = (bf16[128,6144]{1,0:T(8,128)(2,1)S(1)}, bf16[128,6144]{1,0:T(8,128)(2,1)}, u32[]{:S(2)}) copy-start(bf16[128,6144]{1,0:T(8,128)(2,1)} %get-tuple-element.26) | copy-start | bytes 4718596
  970.3 1819.6 %all-reduce.4.cloned.1.call-start = ((), (), s32[]{:S(2)}) async-start(), calls=%async_computation.11 | async-start | bytes 12582912 | tf_op jit(solution)/shard_map/psum | solution.py:291
  2636.7 6.4 copy-start.12
  2636.7 6.4 copy-start.27
  2645.5 42.9 %copy-start.5 = (f32[128,2048]{1,0:T(8,128)S(1)}, f32[128,2048]{1,0:T(8,128)}, u32[]{:S(2)}) copy-start(f32[128,2048]{1,0:T(8,128)} %copy-done.4) | copy-start | bytes 3145732
  2645.5 45.5 %copy-start.3 = (f32[128,2048]{1,0:T(8,128)S(1)}, f32[128,2048]{1,0:T(8,128)}, u32[]{:S(2)}) copy-start(f32[128,2048]{1,0:T(8,128)} %copy-done.2) | copy-start | bytes 3145732
  (38 other events, 120.0 us)
Sparse Core Ops, SparseCore 0:
  10.2 53.2 all-gather.7
  65.7 49.0 all-gather.9
  116.9 73.3 all-gather.11
  192.4 73.1 all-gather.13
  267.0 126.8 all-gather.17
  395.3 128.5 all-gather.15
  525.5 128.5 all-gather.19
  787.9 467.7 reduce-scatter.2
  1259.9 1369.1 reduce-scatter.4
  2635.8 154.1 all-reduce.3
where the time goes:
time: 2820 us; the launch traced here: 2810 us
  waiting for transfers between devices  2330 us (83%)
  matrix products  227 us (8%)
  other arithmetic  162 us (6%)
  blocking collectives  40.2 us (1%)
  local copies, waits for them, and re-layouts  28.5 us (1%)
    reduce_scatter x1, waiting for transfers between devices, on_device(): lax.psum_scatter(jnp.concatenate([contract_rows(left_in, mlp_right), cont...  1370 us
    reduce_scatter x1, waiting for transfers between devices, on_device(): lax.psum_scatter(jnp.concatenate([contract_rows(left_in, attn_right), con...  285 us
    all_gather x1, waiting for transfers between devices, on_device(): lax.all_gather(w_up, 'shard', axis=0, tiled=True)  121 us
    all_gather x1, waiting for transfers between devices, on_device(): lax.all_gather(w_down, 'shard', axis=0, tiled=True)  117 us
    all_gather x1, waiting for transfers between devices, on_device(): lax.all_gather(w_gate, 'shard', axis=0, tiled=True)  116 us
    dot_general x4, matrix products, contract_rows(): lax.dot_general(left, right, (((0,), (0,)), ((), ())), preferred_element_...  103 us
    concatenate x1, other arithmetic, on_device(): jnp.concatenate([contract_rows(left_in, mlp_right), contract_rows(left_gr...  100 us
    psum x1, waiting for transfers between devices, on_device(): lax.psum(attn_grads.astype(jnp.bfloat16), 'rep').astype(jnp.float32)  84.7 us
  transfers between devices with their start and end apart: 10, of which 10 were waited for; matrix products, arithmetic and copies ran while one was open for 9% of the time, Pallas kernels for 0%

commit v1 on v0

v1 whole, which is shorter than its diff:
```python
import math

import jax
import jax.numpy as jnp
from jax import lax
from jax.sharding import Mesh
from jax.sharding import PartitionSpec as P

EPSILON = 1e-06
ROPE_BASE = 1000000.0
NEG_FILL = -1e30
F32 = jnp.float32
BF16 = jnp.bfloat16
SWAP = [(0, 1), (1, 0)]
CHUNK = 2048


def over_rep(v):
    return lax.ppermute(v, "rep", SWAP)


def over_mid(v):
    return lax.ppermute(v, "mid", SWAP)


def over_near(v):
    return lax.ppermute(v, "near", SWAP)


def plane_gather(own):
    half = own.shape[0] // 2
    from_rep = over_rep(own)
    from_mid = over_mid(own)
    top = over_mid(from_rep[:half])
    bottom = over_rep(from_mid[half:])
    mine = jnp.concatenate([own, from_rep, from_mid, top, bottom], 0)
    return jnp.concatenate([mine, over_near(mine)], 0)


def plane_scatter(left, contract):
    middle = left.shape[0] // 2
    rows = middle // 4
    half = rows // 2
    near = over_near(contract(left[middle:]).astype(BF16))
    part = contract(left[:middle]) + near.astype(F32)
    own, rep, mid, both = (part[i * rows : (i + 1) * rows] for i in range(4))
    first_rep = over_rep(jnp.concatenate([both[:half], rep[:half]], 0).astype(BF16))
    first_mid = over_mid(jnp.concatenate([both[half:], mid[half:]], 0).astype(BF16))
    last_mid = over_mid((mid[:half] + first_rep[:half].astype(F32)).astype(BF16))
    last_rep = over_rep((rep[half:] + first_mid[:half].astype(F32)).astype(BF16))
    top = own[:half] + first_rep[half:].astype(F32) + last_mid.astype(F32)
    bottom = own[half:] + last_rep.astype(F32) + first_mid[half:].astype(F32)
    return jnp.concatenate([top, bottom], 0)


def line_gather(block, size):
    m, rows, n = block.shape
    if size > 4:
        return lax.all_gather(block, "far", axis=1, tiled=True)
    place = lax.axis_index("far")
    right, left = [block], [block]
    for k in range(1, size):
        right.append(lax.ppermute(right[-1], "far", [(i, i + 1) for i in range(k - 1, size - 1)]))
        left.append(lax.ppermute(left[-1], "far", [(i, i - 1) for i in range(1, size - k + 1)]))
    out = jnp.zeros((m, size * rows, n), block.dtype)
    out = lax.dynamic_update_slice(out, block, (0, place * rows, 0))
    for k in range(1, size):
        piece = jnp.where(place >= k, right[k], left[size - k])
        out = lax.dynamic_update_slice(out, piece, (0, (place - k) % size * rows, 0))
    return out


def line_scatter(parts, size):
    m, full, n = parts.shape
    rows = full // size
    if size > 4:
        return lax.psum_scatter(parts, "far", scatter_dimension=1, tiled=True)
    place = lax.axis_index("far")

    def block(index):
        return lax.dynamic_slice(parts, (0, index % size * rows, 0), (m, rows, n))

    right = left = None
    for k in range(size - 1, 0, -1):
        onward, back = block(place + k), block(place - k)
        if right is not None:
            onward = (onward.astype(F32) + right.astype(F32)).astype(parts.dtype)
            back = (back.astype(F32) + left.astype(F32)).astype(parts.dtype)
        right = lax.ppermute(onward, "far", [(i, i + 1) for i in range(0, size - k)])
        left = lax.ppermute(back, "far", [(i, i - 1) for i in range(k, size)])
    out = block(place).astype(F32)
    if right is not None:
        out = out + right.astype(F32) + left.astype(F32)
    return out.astype(parts.dtype)


def fetch_columns(pieces, size):
    side = lax.axis_index("rep")
    stacked = jnp.stack([p.reshape(p.shape[0], 2, 4, -1) for p in pieces])
    mine = lax.dynamic_index_in_dim(stacked, side, 2, keepdims=False)
    ready = jnp.transpose(mine, (2, 0, 1, 3))
    swapped = lax.all_to_all(ready, ("mid", "near"), 0, 0)
    m, rows, n = mine.shape[0], mine.shape[1], mine.shape[3]
    block = jnp.transpose(swapped, (1, 0, 2, 3)).reshape(m, 4 * rows, n)
    return line_gather(block, size)


def return_rows(grads, size):
    mine = line_scatter(grads, size)
    m, four, n = mine.shape
    rows = four // 4
    ready = jnp.transpose(mine.reshape(m, 4, rows, n), (1, 0, 2, 3))
    swapped = lax.all_to_all(ready, ("mid", "near"), 0, 0)
    other = over_rep(swapped)
    side = lax.axis_index("rep")
    low = jnp.where(side == 0, swapped, other)
    high = jnp.where(side == 0, other, swapped)
    both = jnp.stack([low, high])
    return jnp.transpose(both, (2, 3, 0, 1, 4)).reshape(m, rows, 8 * n).astype(F32)


def sum_everywhere(v, size):
    for axis in ("near", "mid", "rep"):
        v = v + lax.ppermute(v, axis, SWAP)
    if size & (size - 1):
        return lax.psum(v, "far")
    step = 1
    while step < size:
        v = v + lax.ppermute(v, "far", [(i, i ^ step) for i in range(size)])
        step *= 2
    return v


def rope_tables(positions, half):
    freq = jnp.exp(jnp.arange(half, dtype=F32) * (-math.log(ROPE_BASE) / half))
    angles = positions.reshape(-1).astype(F32)[:, None, None] * freq
    return (jnp.cos(angles), jnp.sin(angles))


def rotate(vectors, cosine, sine):
    half = vectors.shape[-1] // 2
    first, second = (vectors[..., :half], vectors[..., half:])
    return jnp.concatenate([first * cosine - second * sine, second * cosine + first * sine], -1)


def unrotate(grads, cosine, sine):
    half = grads.shape[-1] // 2
    first, second = (grads[..., :half], grads[..., half:])
    return jnp.concatenate([first * cosine + second * sine, second * cosine - first * sine], -1)


def head_norm(heads, gain):
    recip = lax.rsqrt(jnp.mean(heads * heads, -1, keepdims=True) + EPSILON)
    return (heads * recip * gain, recip)


def norm_back(grads, inputs, recip, gain, axes):
    normal = inputs * recip
    scaled = grads * gain
    gain_grad = jnp.sum(grads * normal, axis=axes)
    input_grad = recip * (scaled - normal * jnp.mean(scaled * normal, -1, keepdims=True))
    return (input_grad, gain_grad)


def attention_mask(segments):
    packed_length = segments.shape[1]
    same = segments[:, :, None] == segments[:, None, :]
    places = jnp.arange(packed_length)
    causal = places[None, :] <= places[:, None]
    return same & causal[None]


def dot(left, right):
    return jnp.dot(left, right, preferred_element_type=F32)


def contract_rows(left, right):
    return lax.dot_general(left, right, (((0,), (0,)), ((), ())), preferred_element_type=F32)


def contract_cols(left, right):
    return lax.dot_general(left, right, (((1,), (1,)), ((), ())), preferred_element_type=F32)


def head_scores(rotated_query_rows, rotated_key_rows, mask):
    sequences, length = (mask.shape[0], mask.shape[1])
    kv_heads, head = rotated_key_rows.shape[1:]
    groups = rotated_query_rows.shape[1] // kv_heads
    query_rows = rotated_query_rows.reshape(sequences, length, kv_heads, groups, head)
    key_rows = rotated_key_rows.reshape(sequences, length, kv_heads, head)
    scores = jnp.einsum("slkgd,smkd->skglm", query_rows, key_rows, preferred_element_type=F32) * head ** (-0.5)
    return (jnp.where(mask[:, None, None], scores, NEG_FILL), query_rows, key_rows)


def attend_forward(rotated_query_rows, rotated_key_rows, value_rows, mask):
    sequences, length = (mask.shape[0], mask.shape[1])
    kv_heads, head = (value_rows.shape[1], value_rows.shape[2])
    scores, _, _ = head_scores(rotated_query_rows, rotated_key_rows, mask)
    top = jnp.max(scores, -1, keepdims=True)
    expo = jnp.exp(scores - top)
    total = jnp.sum(expo, -1, keepdims=True)
    probs = (expo / total).astype(BF16)
    log_total = top + jnp.log(total)
    value_heads = value_rows.reshape(sequences, length, kv_heads, head)
    attended = jnp.einsum("skglm,smkd->slkgd", probs, value_heads, preferred_element_type=F32)
    return (attended.reshape(sequences * length, -1).astype(BF16), log_total)


def attend_backward(rotated_query_rows, rotated_key_rows, value_rows, attended_rows, attended_gradient, log_total, mask):
    sequences, length = (mask.shape[0], mask.shape[1])
    kv_heads, head = (value_rows.shape[1], value_rows.shape[2])
    groups = rotated_query_rows.shape[1] // kv_heads
    scores, query_rows, key_rows = head_scores(rotated_query_rows, rotated_key_rows, mask)
    probs_back = jnp.where(mask[:, None, None], jnp.exp(scores - log_total), 0.0)
    output_gradient = attended_gradient.reshape(sequences, length, kv_heads, groups, head)
    value_heads = value_rows.reshape(sequences, length, kv_heads, head)
    value_gradient = jnp.einsum(
        "skglm,slkgd->smkd", probs_back.astype(BF16), output_gradient, preferred_element_type=F32
    )
    grad_probs = jnp.einsum("slkgd,smkd->skglm", output_gradient, value_heads, preferred_element_type=F32)
    complete = attended_rows.reshape(sequences, length, kv_heads, groups, head).astype(F32)
    delta = jnp.transpose(jnp.sum(output_gradient.astype(F32) * complete, -1), (0, 2, 3, 1))[..., None]
    grad_scores = (probs_back * (grad_probs - delta)).astype(BF16)
    query_gradient = jnp.einsum("skglm,smkd->slkgd", grad_scores, key_rows, preferred_element_type=F32)
    key_gradient = jnp.einsum("skglm,slkgd->smkd", grad_scores, query_rows, preferred_element_type=F32)
    tokens = sequences * length
    return (
        query_gradient.reshape(tokens, kv_heads * groups, head) * head ** (-0.5),
        key_gradient.reshape(tokens, kv_heads, head) * head ** (-0.5),
        value_gradient.reshape(tokens, kv_heads, head),
    )


def gather_inputs(normed_rows, segments, positions):
    tokens, width = normed_rows.shape
    digits = jnp.concatenate(
        [segments >> 7, segments & 127, positions >> 7, positions & 127], 0
    ).astype(BF16)
    note = jnp.zeros((16, width), BF16).at[:4, : digits.shape[1]].set(digits)
    half = tokens // 2
    sent = jnp.concatenate([normed_rows[:half], note, normed_rows[half:], note], 0)
    every = plane_gather(sent).reshape(8, 2, half + 16, width)
    rows = every[:, :, :half].reshape(8 * tokens, width)
    notes = every[:, 0, half : half + 4, : digits.shape[1]].astype(jnp.int32)
    return (rows, notes[:, 0] * 128 + notes[:, 1], notes[:, 2] * 128 + notes[:, 3])


def build(far):
    def on_device(
        block_input,
        out_grad,
        segments,
        positions,
        attn_gain,
        mlp_gain,
        q_gain,
        k_gain,
        w_q,
        key_matrix,
        value_matrix,
        w_o,
        w_gate,
        w_up,
        w_down,
    ):
        head = q_gain.shape[0]
        heads = w_q.shape[1] // head // 8
        kv_heads = key_matrix.shape[1] // head // 8
        hidden = w_gate.shape[1]
        rows = w_q.shape[0]
        inputs = block_input.astype(F32)
        recip_attn = lax.rsqrt(jnp.mean(inputs * inputs, -1, keepdims=True) + EPSILON)
        normed_own = (inputs * recip_attn * attn_gain).astype(BF16)
        normed_rows, every_segment, every_position = gather_inputs(normed_own, segments, positions)
        tokens = normed_rows.shape[0]
        mask = attention_mask(every_segment)
        cosine, sine = rope_tables(every_position, head // 2)

        qkv_own = jnp.concatenate(
            [w.reshape(rows, 8, -1) for w in (w_q, key_matrix, value_matrix)], 2
        ).reshape(rows, -1)
        qkv = fetch_columns([qkv_own], far)[0]
        w_o_cols = fetch_columns([w_o], far)[0]
        q_cols = heads * head
        k_cols = kv_heads * head
        proj = dot(normed_rows, qkv)
        q_heads = proj[:, :q_cols].reshape(tokens, heads, head)
        key_head_rows = proj[:, q_cols : q_cols + k_cols].reshape(tokens, kv_heads, head)
        value_rows = proj[:, q_cols + k_cols :].astype(BF16).reshape(tokens, kv_heads, head)
        q_normed, q_recip = head_norm(q_heads, q_gain)
        k_normed, k_recip = head_norm(key_head_rows, k_gain)
        rotated_query_rows = rotate(q_normed, cosine, sine).astype(BF16)
        rotated_key_rows = rotate(k_normed, cosine, sine).astype(BF16)
        attended_rows, log_total = attend_forward(rotated_query_rows, rotated_key_rows, value_rows, mask)
        mid = inputs + plane_scatter(attended_rows, lambda left: contract_cols(left, w_o_cols))
        recip_mlp = lax.rsqrt(jnp.mean(mid * mid, -1, keepdims=True) + EPSILON)
        mlp_in = plane_gather((mid * recip_mlp * mlp_gain).astype(BF16))
        grad_top = plane_gather(out_grad)

        chunks = range(hidden // CHUNK)
        acts, downs, sides, side_weights, mlp_grads = [], [], [], [], []
        for j in chunks:
            span = slice(j * CHUNK, (j + 1) * CHUNK)
            three = fetch_columns([w_gate[:, span], w_up[:, span], w_down[:, span]], far)
            gate_pre = dot(mlp_in, three[0])
            up_pre = dot(mlp_in, three[1])
            sigma = jax.nn.sigmoid(gate_pre)
            silu_gate = gate_pre * sigma
            act = (silu_gate * up_pre).astype(BF16)
            grad_act = dot(grad_top, three[2])
            grad_gate = (grad_act * up_pre * sigma * (1.0 + gate_pre * (1.0 - sigma))).astype(BF16)
            grad_up = (grad_act * silu_gate).astype(BF16)
            own = jnp.stack(
                [
                    contract_rows(mlp_in, grad_gate).astype(BF16),
                    contract_rows(mlp_in, grad_up).astype(BF16),
                    contract_rows(grad_top, act).astype(BF16),
                ]
            )
            mlp_grads.append(return_rows(own, far))
            acts.append(act)
            downs.append(three[2])
            sides += [grad_gate, grad_up]
            side_weights += [three[0], three[1]]
        down = jnp.concatenate(downs, 1)
        sideways = jnp.concatenate(side_weights, 1)
        grad_mlp_in = plane_scatter(jnp.concatenate(sides, 1), lambda left: contract_cols(left, sideways))
        mlp_out = plane_scatter(jnp.concatenate(acts, 1), lambda left: contract_cols(left, down))
        output = (mid + mlp_out).astype(BF16)
        grad_mid_part, mlp_gain_part = norm_back(grad_mlp_in, mid, recip_mlp, mlp_gain, 0)
        grad_mid = out_grad.astype(F32) + grad_mid_part
        grad_mid_b = plane_gather(grad_mid.astype(BF16))
        attended_gradient = dot(grad_mid_b, w_o_cols).astype(BF16)
        own_o = contract_rows(grad_mid_b, attended_rows).astype(BF16)
        grad_w_o = return_rows(own_o[None], far)[0]
        query_gradient, key_gradient, value_gradient = attend_backward(
            rotated_query_rows,
            rotated_key_rows,
            value_rows,
            attended_rows,
            attended_gradient,
            log_total,
            mask,
        )
        grad_qh, q_gain_part = norm_back(unrotate(query_gradient, cosine, sine), q_heads, q_recip, q_gain, (0, 1))
        grad_kh, k_gain_part = norm_back(
            unrotate(key_gradient, cosine, sine), key_head_rows, k_recip, k_gain, (0, 1)
        )
        grad_qkv = jnp.concatenate(
            [g.reshape(tokens, -1).astype(BF16) for g in (grad_qh, grad_kh, value_gradient)], 1
        )
        own_qkv = contract_rows(normed_rows, grad_qkv).astype(BF16)
        every_qkv = return_rows(own_qkv[None], far)[0].reshape(rows, 8, -1)
        grad_normed = plane_scatter(grad_qkv, lambda left: contract_cols(left, qkv))
        grad_in_part, attn_gain_part = norm_back(grad_normed, inputs, recip_attn, attn_gain, 0)
        grad_input = grad_mid + grad_in_part
        width = inputs.shape[1]
        sums = sum_everywhere(
            jnp.concatenate([attn_gain_part, mlp_gain_part, q_gain_part, k_gain_part]).reshape(1, -1), far
        )[0]
        grad_gate_w, grad_up_w, grad_down_w = (
            jnp.concatenate([g[i] for g in mlp_grads], 1) for i in range(3)
        )
        return (
            output,
            grad_input,
            every_qkv[:, :, :q_cols].reshape(rows, -1),
            every_qkv[:, :, q_cols : q_cols + k_cols].reshape(rows, -1),
            every_qkv[:, :, q_cols + k_cols :].reshape(rows, -1),
            grad_w_o,
            grad_gate_w,
            grad_up_w,
            grad_down_w,
            sums[:width],
            sums[width : 2 * width],
            sums[2 * width : 2 * width + head],
            sums[2 * width + head :],
        )

    return on_device


def solution(mesh):
    far = mesh.shape["shard"] // 4
    split = Mesh(mesh.devices.reshape(mesh.shape["rep"], far, 2, 2), ("rep", "far", "mid", "near"))
    tokens = P(("rep", "far", "mid", "near"), None)
    weights = P(("far", "mid", "near"), None)
    return jax.shard_map(
        build(far),
        mesh=split,
        in_specs=(tokens,) * 4 + (P(),) * 4 + (weights,) * 7,
        out_specs=(tokens,) * 2 + (weights,) * 7 + (P(),) * 4,
        check_vma=False,
    )
```

time: 2820 us -> 903 us (0.32)
  waiting for transfers between devices: 2330 us -> 369 us
  starting transfers between devices: 0.64 us -> 227 us
  matrix products: 227 us -> 77.4 us
  local copies, waits for them, and re-layouts: 28.5 us -> 133 us
  other arithmetic: 162 us -> 79 us
  blocking collectives: 40.2 us -> 0 us
    reduce_scatter x2 -> x0, waiting for transfers between devices: 1660 us -> none  [the longest x1 1370 us: on_device(): lax.psum_scatter(jnp.concatenate([contract_rows(left_in, mlp_right), cont...]
    all_gather x7 -> x0, waiting for transfers between devices: 588 us -> none  [the longest x1 121 us: on_device(): lax.all_gather(w_up, 'shard', axis=0, tiled=True)]
    ppermute x0 -> x110, waiting for transfers between devices: none -> 352 us  [the longest x15 136 us: line_gather(): lax.ppermute(left[-1], 'far', [(i, i - 1) for i in range(1, size - k + 1)])]
    ppermute x0 -> x110, starting transfers between devices: none -> 188 us  [the longest x15 62.7 us: line_scatter(): lax.ppermute(onward, 'far', [(i, i + 1) for i in range(0, size - k)])]
    concatenate x2 -> x17, other arithmetic: 134 us -> 9.56 us  [the longest x3 5.61 us: on_device(): jnp.concatenate([g[i] for g in mlp_grads], 1)]
    psum x1 -> x0, waiting for transfers between devices: 84.7 us -> none  [on_device(): lax.psum(attn_grads.astype(jnp.bfloat16), 'rep').astype(jnp.float32)]
    dot_general x4 -> x11, matrix products: 103 us -> 18.3 us  [contract_rows(): lax.dot_general(left, right, (((0,), (0,)), ((), ())), preferred_element_...]
    dot_general x10 -> x14, matrix products: 62.3 us -> 21.5 us  [the longest x11 20.2 us: dot(): return jnp.dot(left, right, preferred_element_type=F32)]
  transfers between devices with their start and end apart: 10 -> 120, of which waited for: 10 -> 52; matrix products, arithmetic and copies ran while one was open for 9% -> 26% of each run, Pallas kernels for 0% -> 0%
where the time goes in v1:
time: 903 us; the launch traced here: 890 us
  waiting for transfers between devices  369 us (41%)
  starting transfers between devices  227 us (25%)
  local copies, waits for them, and re-layouts  133 us (15%)
  other arithmetic  79 us (9%)
  matrix products  77.4 us (9%)
    ppermute x15, waiting for transfers between devices, line_gather(): lax.ppermute(left[-1], 'far', [(i, i - 1) for i in range(1, size - k + 1)])  136 us
    ppermute x21, waiting for transfers between devices, over_rep(): return lax.ppermute(v, 'rep', SWAP)  105 us
    ppermute x15, waiting for transfers between devices, line_scatter(): lax.ppermute(onward, 'far', [(i, i + 1) for i in range(0, size - k)])  68 us
    ppermute x15, starting transfers between devices, line_scatter(): lax.ppermute(onward, 'far', [(i, i + 1) for i in range(0, size - k)])  62.7 us
    unnamed x272, local copies, waits for them, and re-layouts  49.6 us
    ppermute x15, starting transfers between devices, line_gather(): lax.ppermute(right[-1], 'far', [(i, i + 1) for i in range(k - 1, size - 1)])  36.6 us
    dot_general x8, matrix products, contract_cols(): lax.dot_general(left, right, (((1,), (1,)), ((), ())), preferred_element_...  34.8 us
    ppermute x21, starting transfers between devices, over_rep(): return lax.ppermute(v, 'rep', SWAP)  23.3 us
  transfers between devices with their start and end apart: 120, of which 52 were waited for; matrix products, arithmetic and copies ran while one was open for 26% of the time, Pallas kernels for 0%

profile of v1, /device:TPU:0, one launch (start us, length us, event | category | flops | bytes accessed | tf_op | source)
XLA Modules:
  0.0 890.4 jit_solution(6878371324382605307)
XLA Ops:
  31.4 8.6 all-to-all-done
  99.4 7.6 collective-permute-start.5
  148.3 15.3 %collective-permute-done.34 = bf16[3,512,256]{2,1,0:T(8,128)(2,1)S(1)} collective-permute-done((bf16[3,512,256]{2,1,0:T(8,128)(2,1)S(1)}, bf16[3,512,256]{2,1,0:T(8,128)(2,1)S(1)}, u32[]{:S(2)}, u32[]{:S(2)}) %collective-permute-start.34) | collective-permute-done | bytes 786464 | tf_op jit(solution)/shard_map/ppermute | solution.py:64
  167.9 12.6 %collective-permute-done.40 = bf16[3,512,256]{2,1,0:T(8,128)(2,1)S(1)} collective-permute-done((bf16[3,512,256]{2,1,0:T(8,128)(2,1)S(1)}, bf16[3,512,256]{2,1,0:T(8,128)(2,1)S(1)}, u32[]{:S(2)}, u32[]{:S(2)}) %collective-permute-start.40) | collective-permute-done | bytes 786464 | tf_op jit(solution)/shard_map/ppermute | solution.py:64
  181.9 9.8 %collective-permute-done.7 = bf16[1,512,512]{2,1,0:T(8,128)(2,1)S(1)} collective-permute-done((bf16[1,512,512]{2,1,0:T(8,128)(2,1)}, bf16[1,512,512]{2,1,0:T(8,128)(2,1)S(1)}, u32[]{:S(2)}, u32[]{:S(2)}) %collective-permute-start.7) | collective-permute-done | bytes 524320 | tf_op jit(solution)/shard_map/ppermute | solution.py:64
  199.8 18.0 %collective-permute-done.8 = bf16[1,512,512]{2,1,0:T(8,128)(2,1)S(1)} collective-permute-done((bf16[1,512,512]{2,1,0:T(8,128)(2,1)S(1)}, bf16[1,512,512]{2,1,0:T(8,128)(2,1)S(1)}, u32[]{:S(2)}, u32[]{:S(2)}) %collective-permute-start.8) | collective-permute-done | bytes 524320 | tf_op jit(solution)/shard_map/ppermute | solution.py:64
  223.3 16.8 %collective-permute-done.35 = bf16[3,512,256]{2,1,0:T(8,128)(2,1)S(1)} collective-permute-done((bf16[3,512,256]{2,1,0:T(8,128)(2,1)S(1)}, bf16[3,512,256]{2,1,0:T(8,128)(2,1)S(1)}, u32[]{:S(2)}, u32[]{:S(2)}) %collective-permute-start.35) | collective-permute-done | bytes 786464 | tf_op jit(solution)/shard_map/ppermute | solution.py:64
  243.3 13.7 %collective-permute-done.30 = bf16[3,512,256]{2,1,0:T(8,128)(2,1)S(1)} collective-permute-done((bf16[3,512,256]{2,1,0:T(8,128)(2,1)S(1)}, bf16[3,512,256]{2,1,0:T(8,128)(2,1)S(1)}, u32[]{:S(2)}, u32[]{:S(2)}) %collective-permute-start.30) | collective-permute-done | bytes 786464 | tf_op jit(solution)/shard_map/ppermute | solution.py:64
  258.6 15.2 %collective-permute-done.41 = bf16[3,512,256]{2,1,0:T(8,128)(2,1)S(1)} collective-permute-done((bf16[3,512,256]{2,1,0:T(8,128)(2,1)S(1)}, bf16[3,512,256]{2,1,0:T(8,128)(2,1)S(1)}, u32[]{:S(2)}, u32[]{:S(2)}) %collective-permute-start.41) | collective-permute-done | bytes 786464 | tf_op jit(solution)/shard_map/ppermute | solution.py:64
  278.8 11.8 %collective-permute-done.36 = bf16[3,512,256]{2,1,0:T(8,128)(2,1)S(1)} collective-permute-done((bf16[3,512,256]{2,1,0:T(8,128)(2,1)S(1)}, bf16[3,512,256]{2,1,0:T(8,128)(2,1)S(1)}, u32[]{:S(2)}, u32[]{:S(2)}) %collective-permute-start.36) | collective-permute-done | bytes 786464 | tf_op jit(solution)/shard_map/ppermute | solution.py:64
  292.7 14.4 %collective-permute-done.42 = bf16[3,512,256]{2,1,0:T(8,128)(2,1)S(1)} collective-permute-done((bf16[3,512,256]{2,1,0:T(8,128)(2,1)S(1)}, bf16[3,512,256]{2,1,0:T(8,128)(2,1)S(1)}, u32[]{:S(2)}, u32[]{:S(2)}) %collective-permute-start.42) | collective-permute-done | bytes 786464 | tf_op jit(solution)/shard_map/ppermute | solution.py:64
  342.4 10.2 %collective-permute-done.18 = bf16[128,2048]{1,0:T(8,128)(2,1)S(1)} collective-permute-done((bf16[128,2048]{1,0:T(8,128)(2,1)S(1)}, bf16[128,2048]{1,0:T(8,128)(2,1)S(1)}, u32[]{:S(2)}, u32[]{:S(2)}) %collective-permute-start.18) | collective-permute-done | bytes 524320 | tf_op jit(solution)/shard_map/ppermute | solution.py:19
  354.5 5.6 collective-permute-done.19
  372.8 6.4 collective-permute-done.22
  431.8 8.3 collective-permute-done.84
  444.7 12.2 %collective-permute-done.91 = bf16[3,512,256]{2,1,0:T(8,128)(2,1)S(1)} collective-permute-done((bf16[3,512,256]{2,1,0:T(8,128)(2,1)S(1)}, bf16[3,512,256]{2,1,0:T(8,128)(2,1)S(1)}, u32[]{:S(2)}, u32[]{:S(2)}) %collective-permute-start.91) | collective-permute-done | bytes 786464 | tf_op jit(solution)/shard_map/ppermute | solution.py:89
  461.4 7.5 convolution_convert_fusion.3
  479.3 11.4 %collective-permute-done.85 = bf16[3,512,256]{2,1,0:T(8,128)(2,1)S(1)} collective-permute-done((bf16[3,512,256]{2,1,0:T(8,128)(2,1)S(1)}, bf16[3,512,256]{2,1,0:T(8,128)(2,1)S(1)}, u32[]{:S(2)}, u32[]{:S(2)}) %collective-permute-start.85) | collective-permute-done | bytes 786464 | tf_op jit(solution)/shard_map/ppermute | solution.py:89
  496.1 11.4 %collective-permute-done.92 = bf16[3,512,256]{2,1,0:T(8,128)(2,1)S(1)} collective-permute-done((bf16[3,512,256]{2,1,0:T(8,128)(2,1)S(1)}, bf16[3,512,256]{2,1,0:T(8,128)(2,1)S(1)}, u32[]{:S(2)}, u32[]{:S(2)}) %collective-permute-start.92) | collective-permute-done | bytes 786464 | tf_op jit(solution)/shard_map/ppermute | solution.py:89
  509.5 6.0 collective-permute-start.86
  515.5 8.9 collective-permute-done.99
  526.4 5.9 collective-permute-start.93
  538.7 8.7 fusion.172
  556.2 9.6 %collective-permute-done.46 = bf16[128,2048]{1,0:T(8,128)(2,1)S(1)} collective-permute-done((bf16[128,2048]{1,0:T(8,128)(2,1)S(1)}, bf16[128,2048]{1,0:T(8,128)(2,1)S(1)}, u32[]{:S(2)}, u32[]{:S(2)}) %collective-permute-start.46) | collective-permute-done | bytes 524320 | tf_op jit(solution)/shard_map/ppermute | solution.py:19
  566.1 7.8 collective-permute-done.56
  588.2 7.3 collective-permute-done.49
  615.0 10.9 %collective-permute-done.96 = bf16[3,512,256]{2,1,0:T(8,128)(2,1)} collective-permute-done((bf16[3,512,256]{2,1,0:T(8,128)(2,1)}, bf16[3,512,256]{2,1,0:T(8,128)(2,1)}, u32[]{:S(2)}, u32[]{:S(2)}) %collective-permute-start.96) | collective-permute-done | bytes 786464 | tf_op jit(solution)/shard_map/ppermute | solution.py:90
  672.6 11.8 %collective-permute-done.90 = bf16[4,3,128,256]{2,3,0,1:T(8,128)(2,1)} collective-permute-done((bf16[4,3,128,256]{2,3,0,1:T(8,128)(2,1)S(1)}, bf16[4,3,128,256]{2,3,0,1:T(8,128)(2,1)}, u32[]{:S(2)}, u32[]{:S(2)}) %collective-permute-start.90) | collective-permute-done | bytes 786464 | tf_op jit(solution)/shard_map/ppermute | solution.py:19
  685.9 15.4 %collective-permute-done.97 = bf16[4,3,128,256]{2,3,0,1:T(8,128)(2,1)} collective-permute-done((bf16[4,3,128,256]{2,3,0,1:T(8,128)(2,1)S(1)}, bf16[4,3,128,256]{2,3,0,1:T(8,128)(2,1)}, u32[]{:S(2)}, u32[]{:S(2)}) %collective-permute-start.97) | collective-permute-done | bytes 786464 | tf_op jit(solution)/shard_map/ppermute | solution.py:19
  702.5 13.9 %collective-permute-done.104 = bf16[4,3,128,256]{2,3,0,1:T(8,128)(2,1)S(1)} collective-permute-done((bf16[4,3,128,256]{2,3,0,1:T(8,128)(2,1)S(1)}, bf16[4,3,128,256]{2,3,0,1:T(8,128)(2,1)S(1)}, u32[]{:S(2)}, u32[]{:S(2)}) %collective-permute-start.104) | collective-permute-done | bytes 786464 | tf_op jit(solution)/shard_map/ppermute | solution.py:19
  764.1 8.5 collective-permute-done.78
  857.4 7.1 collective-permute-done.76
  (755 shorter events, 547.3 us)
Async XLA Ops:
  45.1 53.0 %collective-permute-start = (bf16[160,2048]{1,0:T(8,128)(2,1)}, bf16[160,2048]{1,0:T(8,128)(2,1)}, u32[]{:S(2)}, u32[]{:S(2)}) collective-permute-start(bf16[160,2048]{1,0:T(8,128)(2,1)} %pad_maximum_fusion.16), channel_id=1, source_target_pairs={{0,16},{16,0},{1,17},{17,1},{2,18},{18,2},{3,19},{19,3},{4,20},{20... | collective-permute-start | bytes 1966088 | tf_op jit(solution)/shard_map/ppermute | solution.py:19
  47.4 52.0 %collective-permute-start.1 = (bf16[160,2048]{1,0:T(8,128)(2,1)}, bf16[160,2048]{1,0:T(8,128)(2,1)}, u32[]{:S(2)}, u32[]{:S(2)}) collective-permute-start(bf16[160,2048]{1,0:T(8,128)(2,1)} %pad_maximum_fusion.16), channel_id=1, source_target_pairs={{0,2},{2,0},{1,3},{3,1},{4,6},{6,4},{5,7},{7,5},{8,10},{10,8},{9,1... | collective-permute-start | bytes 1966088 | tf_op jit(solution)/shard_map/ppermute | solution.py:23
  49.3 34.3 %collective-permute-start.50 = (bf16[128,2048]{1,0:T(8,128)(2,1)}, bf16[128,2048]{1,0:T(8,128)(2,1)}, u32[]{:S(2)}, u32[]{:S(2)}) collective-permute-start(bf16[128,2048]{1,0:T(8,128)(2,1)} %param.18), channel_id=1, source_target_pairs={{0,16},{16,0},{1,17},{17,1},{2,18},{18,2},{3,19},{19,3},{4,20},{20... | collective-permute-start | bytes 1572872 | tf_op jit(solution)/shard_map/ppermute | solution.py:19
  49.3 43.7 %collective-permute-start.51 = (bf16[128,2048]{1,0:T(8,128)(2,1)}, bf16[128,2048]{1,0:T(8,128)(2,1)}, u32[]{:S(2)}, u32[]{:S(2)}) collective-permute-start(bf16[128,2048]{1,0:T(8,128)(2,1)} %param.18), channel_id=1, source_target_pairs={{0,2},{2,0},{1,3},{3,1},{4,6},{6,4},{5,7},{7,5},{8,10},{10,8},{9,1... | collective-permute-start | bytes 1572872 | tf_op jit(solution)/shard_map/ppermute | solution.py:23
  127.3 36.3 %collective-permute-start.34 = (bf16[3,512,256]{2,1,0:T(8,128)(2,1)S(1)}, bf16[3,512,256]{2,1,0:T(8,128)(2,1)S(1)}, u32[]{:S(2)}, u32[]{:S(2)}) collective-permute-start(bf16[3,512,256]{2,1,0:T(8,128)(2,1)S(1)} %bitcast.454), channel_id=1, source_target_pairs={{4,0},{8,4},{12,8},{5,1},{9,5},{13,9},{6,2},{10,6},{14,10},{7,3},{... | collective-permute-start | bytes 2359304 | tf_op jit(solution)/shard_map/ppermute | solution.py:64
  128.6 36.3 %collective-permute-start.33 = (bf16[3,512,256]{2,1,0:T(8,128)(2,1)S(1)}, bf16[3,512,256]{2,1,0:T(8,128)(2,1)S(1)}, u32[]{:S(2)}, u32[]{:S(2)}) collective-permute-start(bf16[3,512,256]{2,1,0:T(8,128)(2,1)S(1)} %bitcast.455), channel_id=1, source_target_pairs={{0,4},{4,8},{8,12},{1,5},{5,9},{9,13},{2,6},{6,10},{10,14},{3,7},{... | collective-permute-start | bytes 2359304 | tf_op jit(solution)/shard_map/ppermute | solution.py:63
  139.5 41.0 %collective-permute-start.40 = (bf16[3,512,256]{2,1,0:T(8,128)(2,1)S(1)}, bf16[3,512,256]{2,1,0:T(8,128)(2,1)S(1)}, u32[]{:S(2)}, u32[]{:S(2)}) collective-permute-start(bf16[3,512,256]{2,1,0:T(8,128)(2,1)S(1)} %bitcast.451), channel_id=1, source_target_pairs={{4,0},{8,4},{12,8},{5,1},{9,5},{13,9},{6,2},{10,6},{14,10},{7,3},{... | collective-permute-start | bytes 2359304 | tf_op jit(solution)/shard_map/ppermute | solution.py:64
  146.8 48.7 %collective-permute-start.39 = (bf16[3,512,256]{2,1,0:T(8,128)(2,1)S(1)}, bf16[3,512,256]{2,1,0:T(8,128)(2,1)S(1)}, u32[]{:S(2)}, u32[]{:S(2)}) collective-permute-start(bf16[3,512,256]{2,1,0:T(8,128)(2,1)S(1)} %bitcast.452), channel_id=1, source_target_pairs={{0,4},{4,8},{8,12},{1,5},{5,9},{9,13},{2,6},{6,10},{10,14},{3,7},{... | collective-permute-start | bytes 2359304 | tf_op jit(solution)/shard_map/ppermute | solution.py:63
  148.3 93.4 %collective-permute-start.54 = (bf16[512,2048]{1,0:T(8,128)(2,1)S(1)}, bf16[512,2048]{1,0:T(8,128)(2,1)S(1)}, u32[]{:S(2)}, u32[]{:S(2)}) collective-permute-start(bf16[512,2048]{1,0:T(8,128)(2,1)S(1)} %get-tuple-element.195), channel_id=1, source_target_pairs={{0,1},{1,0},{2,3},{3,2},{4,5},{5,4},{6,7},{7,6},{8,9},{9,8},{10,11... | collective-permute-start | bytes 6291464 | tf_op jit(solution)/shard_map/ppermute | solution.py:27
  180.5 38.7 %collective-permute-start.29 = (bf16[3,512,256]{2,1,0:T(8,128)(2,1)S(1)}, bf16[3,512,256]{2,1,0:T(8,128)(2,1)S(1)}, u32[]{:S(2)}, u32[]{:S(2)}) collective-permute-start(bf16[3,512,256]{2,1,0:T(8,128)(2,1)S(1)} %collective-permute-done.28), channel_id=1, source_target_pairs={{4,0},{8,4},{5,1},{9,5},{6,2},{10,6},{7,3},{11,7},{20,16},{24,20},... | collective-permute-start | bytes 2359304 | tf_op jit(solution)/shard_map/ppermute | solution.py:64
  217.8 91.5 %collective-permute-start.4 = (bf16[640,2048]{1,0:T(8,128)(2,1)}, bf16[640,2048]{1,0:T(8,128)(2,1)S(1)}, u32[]{:S(2)}, u32[]{:S(2)}) collective-permute-start(bf16[640,2048]{1,0:T(8,128)(2,1)} %get-tuple-element.187), channel_id=1, source_target_pairs={{0,1},{1,0},{2,3},{3,2},{4,5},{5,4},{6,7},{7,6},{8,9},{9,8},{10,11... | collective-permute-start | bytes 7864328 | tf_op jit(solution)/shard_map/ppermute | solution.py:27
  219.1 37.8 %collective-permute-start.30 = (bf16[3,512,256]{2,1,0:T(8,128)(2,1)S(1)}, bf16[3,512,256]{2,1,0:T(8,128)(2,1)S(1)}, u32[]{:S(2)}, u32[]{:S(2)}) collective-permute-start(bf16[3,512,256]{2,1,0:T(8,128)(2,1)S(1)} %collective-permute-done.29), channel_id=1, source_target_pairs={{4,0},{5,1},{6,2},{7,3},{20,16},{21,17},{22,18},{23,19}} | collective-permute-start | bytes 2359304 | tf_op jit(solution)/shard_map/ppermute | solution.py:64
  220.8 53.0 %collective-permute-start.41 = (bf16[3,512,256]{2,1,0:T(8,128)(2,1)S(1)}, bf16[3,512,256]{2,1,0:T(8,128)(2,1)S(1)}, u32[]{:S(2)}, u32[]{:S(2)}) collective-permute-start(bf16[3,512,256]{2,1,0:T(8,128)(2,1)S(1)} %collective-permute-done.40), channel_id=1, source_target_pairs={{4,0},{8,4},{5,1},{9,5},{6,2},{10,6},{7,3},{11,7},{20,16},{24,20},... | collective-permute-start | bytes 2359304 | tf_op jit(solution)/shard_map/ppermute | solution.py:64
  240.1 35.3 %collective-permute-start.37 = (bf16[3,512,256]{2,1,0:T(8,128)(2,1)S(1)}, bf16[3,512,256]{2,1,0:T(8,128)(2,1)}, u32[]{:S(2)}, u32[]{:S(2)}) collective-permute-start(bf16[3,512,256]{2,1,0:T(8,128)(2,1)S(1)} %collective-permute-done.33), channel_id=1, source_target_pairs={{4,8},{8,12},{5,9},{9,13},{6,10},{10,14},{7,11},{11,15},{20,24},{2... | collective-permute-start | bytes 2359304 | tf_op jit(solution)/shard_map/ppermute | solution.py:63
  241.7 35.6 %collective-permute-start.43 = (bf16[3,512,256]{2,1,0:T(8,128)(2,1)S(1)}, bf16[3,512,256]{2,1,0:T(8,128)(2,1)}, u32[]{:S(2)}, u32[]{:S(2)}) collective-permute-start(bf16[3,512,256]{2,1,0:T(8,128)(2,1)S(1)} %collective-permute-done.39), channel_id=1, source_target_pairs={{4,8},{8,12},{5,9},{9,13},{6,10},{10,14},{7,11},{11,15},{20,24},{2... | collective-permute-start | bytes 2359304 | tf_op jit(solution)/shard_map/ppermute | solution.py:63
  275.3 53.8 %collective-permute-start.32 = (bf16[3,512,256]{2,1,0:T(8,128)(2,1)}, bf16[3,512,256]{2,1,0:T(8,128)(2,1)}, u32[]{:S(2)}, u32[]{:S(2)}) collective-permute-start(bf16[3,512,256]{2,1,0:T(8,128)(2,1)} %collective-permute-done.31), channel_id=1, source_target_pairs={{8,12},{9,13},{10,14},{11,15},{24,28},{25,29},{26,30},{27,31}} | collective-permute-start | bytes 2359304 | tf_op jit(solution)/shard_map/ppermute | solution.py:63
  277.2 52.3 %collective-permute-start.38 = (bf16[3,512,256]{2,1,0:T(8,128)(2,1)}, bf16[3,512,256]{2,1,0:T(8,128)(2,1)}, u32[]{:S(2)}, u32[]{:S(2)}) collective-permute-start(bf16[3,512,256]{2,1,0:T(8,128)(2,1)} %collective-permute-done.37), channel_id=1, source_target_pairs={{8,12},{9,13},{10,14},{11,15},{24,28},{25,29},{26,30},{27,31}} | collective-permute-start | bytes 2359304 | tf_op jit(solution)/shard_map/ppermute | solution.py:63
  290.6 40.7 %collective-permute-start.44 = (bf16[3,512,256]{2,1,0:T(8,128)(2,1)}, bf16[3,512,256]{2,1,0:T(8,128)(2,1)}, u32[]{:S(2)}, u32[]{:S(2)}) collective-permute-start(bf16[3,512,256]{2,1,0:T(8,128)(2,1)} %collective-permute-done.43), channel_id=1, source_target_pairs={{8,12},{9,13},{10,14},{11,15},{24,28},{25,29},{26,30},{27,31}} | collective-permute-start | bytes 2359304 | tf_op jit(solution)/shard_map/ppermute | solution.py:63
  416.4 109.9 %collective-permute-start.45 = (bf16[512,2048]{1,0:T(8,128)(2,1)}, bf16[512,2048]{1,0:T(8,128)(2,1)}, u32[]{:S(2)}, u32[]{:S(2)}) collective-permute-start(bf16[512,2048]{1,0:T(8,128)(2,1)} %convolution_convert_fusion.4), channel_id=1, source_target_pairs={{0,1},{1,0},{2,3},{3,2},{4,5},{5,4},{6,7},{7,6},{8,9},{9,8},{10,11... | collective-permute-start | bytes 6291464 | tf_op jit(solution)/shard_map/ppermute | solution.py:27
  422.3 56.2 %collective-permute-start.87 = (bf16[3,512,256]{2,1,0:T(8,128)(2,1)S(1)}, bf16[3,512,256]{2,1,0:T(8,128)(2,1)S(1)}, u32[]{:S(2)}, u32[]{:S(2)}) collective-permute-start(bf16[3,512,256]{2,1,0:T(8,128)(2,1)S(1)} %get-tuple-element.100), channel_id=1, source_target_pairs={{12,8},{13,9},{14,10},{15,11},{28,24},{29,25},{30,26},{31,27}} | collective-permute-start | bytes 2359304 | tf_op jit(solution)/shard_map/ppermute | solution.py:90
  427.5 51.0 %collective-permute-start.94 = (bf16[3,512,256]{2,1,0:T(8,128)(2,1)S(1)}, bf16[3,512,256]{2,1,0:T(8,128)(2,1)S(1)}, u32[]{:S(2)}, u32[]{:S(2)}) collective-permute-start(bf16[3,512,256]{2,1,0:T(8,128)(2,1)S(1)} %get-tuple-element.104), channel_id=1, source_target_pairs={{12,8},{13,9},{14,10},{15,11},{28,24},{29,25},{30,26},{31,27}} | collective-permute-start | bytes 2359304 | tf_op jit(solution)/shard_map/ppermute | solution.py:90
  478.5 57.2 %collective-permute-start.55 = (bf16[512,2048]{1,0:T(8,128)(2,1)S(1)}, bf16[512,2048]{1,0:T(8,128)(2,1)S(1)}, u32[]{:S(2)}, u32[]{:S(2)}) collective-permute-start(bf16[512,2048]{1,0:T(8,128)(2,1)S(1)} %copy-done.115), channel_id=1, source_target_pairs={{0,1},{1,0},{2,3},{3,2},{4,5},{5,4},{6,7},{7,6},{8,9},{9,8},{10,11... | collective-permute-start | bytes 6291464 | tf_op jit(solution)/shard_map/ppermute | solution.py:27
  490.7 33.7 %collective-permute-start.99 = (bf16[3,512,256]{2,1,0:T(8,128)(2,1)S(1)}, bf16[3,512,256]{2,1,0:T(8,128)(2,1)S(1)}, u32[]{:S(2)}, u32[]{:S(2)}) collective-permute-start(bf16[3,512,256]{2,1,0:T(8,128)(2,1)S(1)} %add_convert_fusion.4), channel_id=1, source_target_pairs={{0,4},{4,8},{1,5},{5,9},{2,6},{6,10},{3,7},{7,11},{16,20},{20,24},... | collective-permute-start | bytes 2359304 | tf_op jit(solution)/shard_map/ppermute | solution.py:89
  507.5 41.3 %collective-permute-start.88 = (bf16[3,512,256]{2,1,0:T(8,128)(2,1)S(1)}, bf16[3,512,256]{2,1,0:T(8,128)(2,1)S(1)}, u32[]{:S(2)}, u32[]{:S(2)}) collective-permute-start(bf16[3,512,256]{2,1,0:T(8,128)(2,1)S(1)} %get-tuple-element.98), channel_id=1, source_target_pairs={{8,4},{12,8},{9,5},{13,9},{10,6},{14,10},{11,7},{15,11},{24,20},{2... | collective-permute-start | bytes 2359304 | tf_op jit(solution)/shard_map/ppermute | solution.py:90
  509.5 94.5 %collective-permute-start.86 = (bf16[3,512,256]{2,1,0:T(8,128)(2,1)S(1)}, bf16[3,512,256]{2,1,0:T(8,128)(2,1)}, u32[]{:S(2)}, u32[]{:S(2)}) collective-permute-start(bf16[3,512,256]{2,1,0:T(8,128)(2,1)S(1)} %get-tuple-element.97), channel_id=1, source_target_pairs={{0,4},{4,8},{8,12},{1,5},{5,9},{9,13},{2,6},{6,10},{10,14},{3,7},{... | collective-permute-start | bytes 2359304 | tf_op jit(solution)/shard_map/ppermute | solution.py:89
  526.4 88.6 %collective-permute-start.93 = (bf16[3,512,256]{2,1,0:T(8,128)(2,1)}, bf16[3,512,256]{2,1,0:T(8,128)(2,1)}, u32[]{:S(2)}, u32[]{:S(2)}) collective-permute-start(bf16[3,512,256]{2,1,0:T(8,128)(2,1)} %get-tuple-element.101), channel_id=1, source_target_pairs={{0,4},{4,8},{8,12},{1,5},{5,9},{9,13},{2,6},{6,10},{10,14},{3,7},{... | collective-permute-start | bytes 2359304 | tf_op jit(solution)/shard_map/ppermute | solution.py:89
  574.3 67.2 %collective-permute-start.100 = (bf16[3,512,256]{2,1,0:T(8,128)(2,1)}, bf16[3,512,256]{2,1,0:T(8,128)(2,1)}, u32[]{:S(2)}, u32[]{:S(2)}) collective-permute-start(bf16[3,512,256]{2,1,0:T(8,128)(2,1)} %get-tuple-element.105), channel_id=1, source_target_pairs={{0,4},{4,8},{8,12},{1,5},{5,9},{9,13},{2,6},{6,10},{10,14},{3,7},{... | collective-permute-start | bytes 2359304 | tf_op jit(solution)/shard_map/ppermute | solution.py:89
  604.1 37.4 %collective-permute-start.103 = (bf16[3,512,256]{2,1,0:T(8,128)(2,1)}, bf16[3,512,256]{2,1,0:T(8,128)(2,1)}, u32[]{:S(2)}, u32[]{:S(2)}) collective-permute-start(bf16[3,512,256]{2,1,0:T(8,128)(2,1)} %add_convert_fusion.1), channel_id=1, source_target_pairs={{4,0},{8,4},{12,8},{5,1},{9,5},{13,9},{6,2},{10,6},{14,10},{7,3},{... | collective-permute-start | bytes 2359304 | tf_op jit(solution)/shard_map/ppermute | solution.py:90
  667.4 33.9 %collective-permute-start.97 = (bf16[4,3,128,256]{2,3,0,1:T(8,128)(2,1)S(1)}, bf16[4,3,128,256]{2,3,0,1:T(8,128)(2,1)}, u32[]{:S(2)}, u32[]{:S(2)}) collective-permute-start(bf16[4,3,128,256]{2,3,0,1:T(8,128)(2,1)S(1)} %copy.283), channel_id=1, source_target_pairs={{0,16},{16,0},{1,17},{17,1},{2,18},{18,2},{3,19},{19,3},{4,20},{20... | collective-permute-start | bytes 2359304 | tf_op jit(solution)/shard_map/ppermute | solution.py:19
  669.9 46.6 %collective-permute-start.104 = (bf16[4,3,128,256]{2,3,0,1:T(8,128)(2,1)S(1)}, bf16[4,3,128,256]{2,3,0,1:T(8,128)(2,1)S(1)}, u32[]{:S(2)}, u32[]{:S(2)}) collective-permute-start(bf16[4,3,128,256]{2,3,0,1:T(8,128)(2,1)S(1)} %copy.287), channel_id=1, source_target_pairs={{0,16},{16,0},{1,17},{17,1},{2,18},{18,2},{3,19},{19,3},{4,20},{20... | collective-permute-start | bytes 2359304 | tf_op jit(solution)/shard_map/ppermute | solution.py:19
  672.6 50.9 %collective-permute-start.64 = (bf16[512,2048]{1,0:T(8,128)(2,1)}, bf16[512,2048]{1,0:T(8,128)(2,1)S(1)}, u32[]{:S(2)}, u32[]{:S(2)}) collective-permute-start(bf16[512,2048]{1,0:T(8,128)(2,1)} %get-tuple-element.191), channel_id=1, source_target_pairs={{0,1},{1,0},{2,3},{3,2},{4,5},{5,4},{6,7},{7,6},{8,9},{9,8},{10,11... | collective-permute-start | bytes 6291464 | tf_op jit(solution)/shard_map/ppermute | solution.py:27
  763.2 55.6 %collective-permute-start.65 = (bf16[512,2048]{1,0:T(8,128)(2,1)}, bf16[512,2048]{1,0:T(8,128)(2,1)}, u32[]{:S(2)}, u32[]{:S(2)}) collective-permute-start(bf16[512,2048]{1,0:T(8,128)(2,1)} %convolution_convert_fusion.2), channel_id=1, source_target_pairs={{0,1},{1,0},{2,3},{3,2},{4,5},{5,4},{6,7},{7,6},{8,9},{9,8},{10,11... | collective-permute-start | bytes 6291464 | tf_op jit(solution)/shard_map/ppermute | solution.py:27
  (207 other events, 3315.6 us)

commit v2 on v1

--- a/solution.py
+++ b/solution.py
@@ -3,6 +3,8 @@
 import jax
 import jax.numpy as jnp
 from jax import lax
+from jax.experimental import pallas as pl
+from jax.experimental.pallas import tpu as pltpu
 from jax.sharding import Mesh
 from jax.sharding import PartitionSpec as P
 
@@ -37,12 +39,10 @@
     return jnp.concatenate([mine, over_near(mine)], 0)
 
 
-def plane_scatter(left, contract):
-    middle = left.shape[0] // 2
-    rows = middle // 4
+def plane_scatter(partial, rows):
     half = rows // 2
-    near = over_near(contract(left[middle:]).astype(BF16))
-    part = contract(left[:middle]) + near.astype(F32)
+    near = over_near(partial(4 * rows, 8 * rows).astype(BF16))
+    part = partial(0, 4 * rows) + near.astype(F32)
     own, rep, mid, both = (part[i * rows : (i + 1) * rows] for i in range(4))
     first_rep = over_rep(jnp.concatenate([both[:half], rep[:half]], 0).astype(BF16))
     first_mid = over_mid(jnp.concatenate([both[half:], mid[half:]], 0).astype(BF16))
@@ -53,70 +53,79 @@
     return jnp.concatenate([top, bottom], 0)
 
 
-def line_gather(block, size):
-    m, rows, n = block.shape
-    if size > 4:
-        return lax.all_gather(block, "far", axis=1, tiled=True)
-    place = lax.axis_index("far")
-    right, left = [block], [block]
-    for k in range(1, size):
-        right.append(lax.ppermute(right[-1], "far", [(i, i + 1) for i in range(k - 1, size - 1)]))
-        left.append(lax.ppermute(left[-1], "far", [(i, i - 1) for i in range(1, size - k + 1)]))
-    out = jnp.zeros((m, size * rows, n), block.dtype)
-    out = lax.dynamic_update_slice(out, block, (0, place * rows, 0))
-    for k in range(1, size):
-        piece = jnp.where(place >= k, right[k], left[size - k])
-        out = lax.dynamic_update_slice(out, piece, (0, (place - k) % size * rows, 0))
-    return out
-
-
-def line_scatter(parts, size):
-    m, full, n = parts.shape
-    rows = full // size
-    if size > 4:
-        return lax.psum_scatter(parts, "far", scatter_dimension=1, tiled=True)
-    place = lax.axis_index("far")
-
-    def block(index):
-        return lax.dynamic_slice(parts, (0, index % size * rows, 0), (m, rows, n))
-
-    right = left = None
-    for k in range(size - 1, 0, -1):
-        onward, back = block(place + k), block(place - k)
-        if right is not None:
-            onward = (onward.astype(F32) + right.astype(F32)).astype(parts.dtype)
-            back = (back.astype(F32) + left.astype(F32)).astype(parts.dtype)
-        right = lax.ppermute(onward, "far", [(i, i + 1) for i in range(0, size - k)])
-        left = lax.ppermute(back, "far", [(i, i - 1) for i in range(k, size)])
-    out = block(place).astype(F32)
-    if right is not None:
-        out = out + right.astype(F32) + left.astype(F32)
-    return out.astype(parts.dtype)
-
-
-def fetch_columns(pieces, size):
-    side = lax.axis_index("rep")
-    stacked = jnp.stack([p.reshape(p.shape[0], 2, 4, -1) for p in pieces])
-    mine = lax.dynamic_index_in_dim(stacked, side, 2, keepdims=False)
-    ready = jnp.transpose(mine, (2, 0, 1, 3))
-    swapped = lax.all_to_all(ready, ("mid", "near"), 0, 0)
-    m, rows, n = mine.shape[0], mine.shape[1], mine.shape[3]
-    block = jnp.transpose(swapped, (1, 0, 2, 3)).reshape(m, 4 * rows, n)
-    return line_gather(block, size)
-
-
-def return_rows(grads, size):
-    mine = line_scatter(grads, size)
-    m, four, n = mine.shape
-    rows = four // 4
-    ready = jnp.transpose(mine.reshape(m, 4, rows, n), (1, 0, 2, 3))
-    swapped = lax.all_to_all(ready, ("mid", "near"), 0, 0)
-    other = over_rep(swapped)
-    side = lax.axis_index("rep")
-    low = jnp.where(side == 0, swapped, other)
-    high = jnp.where(side == 0, other, swapped)
-    both = jnp.stack([low, high])
-    return jnp.transpose(both, (2, 3, 0, 1, 4)).reshape(m, rows, 8 * n).astype(F32)
+def pick_columns(groups):
+    side = lax.axis_index("rep").astype(jnp.int32).reshape(1)
+    members = [m for group in groups for m in group]
+    rows = members[0][0].shape[0]
+    widths = [sum(n for _, _, n in group) for group in groups]
+
+    def kernel(side_ref, *refs):
+        sources = iter(refs[: len(members)])
+        for group, out in zip(groups, refs[len(members) :]):
+            at = 0
+            for _, _, n in group:
+                source = next(sources)
+                for block in range(4):
+                    out[block, :, at : at + n] = source[:, block * n : (block + 1) * n]
+                at += n
+
+    def half(start, n):
+        return pl.BlockSpec((rows, 4 * n), lambda i, side_ref: (0, start // (4 * n) + side_ref[0]))
+
+    return pl.pallas_call(
+        kernel,
+        grid_spec=pltpu.PrefetchScalarGridSpec(
+            num_scalar_prefetch=1,
+            grid=(1,),
+            in_specs=[half(start, n) for _, start, n in members],
+            out_specs=[pl.BlockSpec((4, rows, w), lambda i, side_ref: (0, 0, 0)) for w in widths],
+        ),
+        out_shape=[jax.ShapeDtypeStruct((4, rows, w), BF16) for w in widths],
+        name="pick_columns",
+    )(side, *[m for m, _, _ in members])
+
+
+def trade(blocks):
+    return lax.all_to_all(blocks, ("mid", "near"), 0, 0)
+
+
+def gather_rows(blocks):
+    four, rows, n = blocks.shape
+    return lax.all_gather(blocks.reshape(four * rows, n), "far", axis=0, tiled=True)
+
+
+def scatter_rows(parts):
+    mine = lax.psum_scatter(parts, "far", scatter_dimension=0, tiled=True)
+    mine = trade(mine.reshape(4, mine.shape[0] // 4, -1))
+    return (mine, over_rep(mine))
+
+
+def spread(pairs, outs):
+    side = lax.axis_index("rep").astype(jnp.int32).reshape(1)
+    rows = pairs[0][0].shape[1]
+    columns = [sum(8 * n for _, _, n in pieces) for pieces in outs]
+
+    def kernel(side_ref, *refs):
+        first = side_ref[0] == 0
+        for out, pieces in zip(refs[2 * len(pairs) :], outs):
+            at = 0
+            for pair, start, n in pieces:
+                own, other = refs[2 * pair], refs[2 * pair + 1]
+                for block in range(4):
+                    a = own[block, :, start : start + n].astype(F32)
+                    b = other[block, :, start : start + n].astype(F32)
+                    out[:, at + block * n : at + (block + 1) * n] = jnp.where(first, a, b)
+                    out[:, at + (4 + block) * n : at + (5 + block) * n] = jnp.where(first, b, a)
+                at += 8 * n
+
+    return pl.pallas_call(
+        kernel,
+        in_specs=[pl.BlockSpec(memory_space=pltpu.SMEM)] + [pl.BlockSpec(memory_space=pltpu.VMEM)] * (2 * len(pairs)),
+        out_specs=[pl.BlockSpec(memory_space=pltpu.VMEM)] * len(outs),
+        out_shape=[jax.ShapeDtypeStruct((rows, c), F32) for c in columns],
+        compiler_params=pltpu.CompilerParams(vmem_limit_bytes=40 << 20),
+        name="spread",
+    )(side, *[v for pair in pairs for v in pair])
 
 
 def sum_everywhere(v, size):
@@ -231,18 +240,11 @@
     )
 
 
-def gather_inputs(normed_rows, segments, positions):
-    tokens, width = normed_rows.shape
-    digits = jnp.concatenate(
-        [segments >> 7, segments & 127, positions >> 7, positions & 127], 0
-    ).astype(BF16)
-    note = jnp.zeros((16, width), BF16).at[:4, : digits.shape[1]].set(digits)
-    half = tokens // 2
-    sent = jnp.concatenate([normed_rows[:half], note, normed_rows[half:], note], 0)
-    every = plane_gather(sent).reshape(8, 2, half + 16, width)
-    rows = every[:, :, :half].reshape(8 * tokens, width)
-    notes = every[:, 0, half : half + 4, : digits.shape[1]].astype(jnp.int32)
-    return (rows, notes[:, 0] * 128 + notes[:, 1], notes[:, 2] * 128 + notes[:, 3])
+def plane_notes(own):
+    pair = jnp.concatenate([own, over_near(own)], 0)
+    four = jnp.concatenate([pair, over_mid(pair)], 0)
+    eight = jnp.concatenate([four, over_rep(four)], 0)
+    return jnp.concatenate([eight[i : i + 1] for i in (0, 4, 2, 6, 1, 5, 3, 7)], 0)
 
 
 def build(far):
@@ -268,21 +270,30 @@
         kv_heads = key_matrix.shape[1] // head // 8
         hidden = w_gate.shape[1]
         rows = w_q.shape[0]
+        q_cols = heads * head
+        k_cols = kv_heads * head
+        chunks = list(range(0, hidden, CHUNK))
+
+        q_n, k_n, o_n, block = (n // 8 for n in (w_q.shape[1], key_matrix.shape[1], w_o.shape[1], CHUNK))
+        qkv_slot, o_slot = pick_columns(
+            [[(w_q, 0, q_n), (key_matrix, 0, k_n), (value_matrix, 0, k_n)], [(w_o, 0, o_n)]]
+        )
+        qkv = gather_rows(trade(qkv_slot))
+        w_o_cols = gather_rows(trade(o_slot))
+        mlp_slots = pick_columns([[(w, c, block) for w in (w_gate, w_up, w_down)] for c in chunks])
+        mlp_weights = [gather_rows(trade(slot)) for slot in mlp_slots]
+
         inputs = block_input.astype(F32)
         recip_attn = lax.rsqrt(jnp.mean(inputs * inputs, -1, keepdims=True) + EPSILON)
-        normed_own = (inputs * recip_attn * attn_gain).astype(BF16)
-        normed_rows, every_segment, every_position = gather_inputs(normed_own, segments, positions)
+        normed_rows = plane_gather((inputs * recip_attn * attn_gain).astype(BF16))
+        grad_top = plane_gather(out_grad)
+        notes = plane_notes(jnp.concatenate([segments, positions], 1))
+        length = segments.shape[1]
+        own_tokens = inputs.shape[0]
         tokens = normed_rows.shape[0]
-        mask = attention_mask(every_segment)
-        cosine, sine = rope_tables(every_position, head // 2)
-
-        qkv_own = jnp.concatenate(
-            [w.reshape(rows, 8, -1) for w in (w_q, key_matrix, value_matrix)], 2
-        ).reshape(rows, -1)
-        qkv = fetch_columns([qkv_own], far)[0]
-        w_o_cols = fetch_columns([w_o], far)[0]
-        q_cols = heads * head
-        k_cols = kv_heads * head
+        mask = attention_mask(notes[:, :length])
+        cosine, sine = rope_tables(notes[:, length:], head // 2)
+
         proj = dot(normed_rows, qkv)
         q_heads = proj[:, :q_cols].reshape(tokens, heads, head)
         key_head_rows = proj[:, q_cols : q_cols + k_cols].reshape(tokens, kv_heads, head)
@@ -292,47 +303,45 @@
         rotated_query_rows = rotate(q_normed, cosine, sine).astype(BF16)
         rotated_key_rows = rotate(k_normed, cosine, sine).astype(BF16)
         attended_rows, log_total = attend_forward(rotated_query_rows, rotated_key_rows, value_rows, mask)
-        mid = inputs + plane_scatter(attended_rows, lambda left: contract_cols(left, w_o_cols))
+        attended_rows, grad_top = lax.optimization_barrier((attended_rows, grad_top))
+        mid = inputs + plane_scatter(lambda i, j: contract_cols(attended_rows[i:j], w_o_cols), own_tokens)
         recip_mlp = lax.rsqrt(jnp.mean(mid * mid, -1, keepdims=True) + EPSILON)
         mlp_in = plane_gather((mid * recip_mlp * mlp_gain).astype(BF16))
-        grad_top = plane_gather(out_grad)
-
-        chunks = range(hidden // CHUNK)
-        acts, downs, sides, side_weights, mlp_grads = [], [], [], [], []
-        for j in chunks:
-            span = slice(j * CHUNK, (j + 1) * CHUNK)
-            three = fetch_columns([w_gate[:, span], w_up[:, span], w_down[:, span]], far)
-            gate_pre = dot(mlp_in, three[0])
-            up_pre = dot(mlp_in, three[1])
+
+        acts, downs, mlp_grads = [], [], []
+        before = None
+        for number, three in enumerate(mlp_weights):
+            weight = three[:, : 2 * block]
+            pre = dot(mlp_in, weight)
+            gate_pre, up_pre = pre[:, :block], pre[:, block:]
             sigma = jax.nn.sigmoid(gate_pre)
             silu_gate = gate_pre * sigma
             act = (silu_gate * up_pre).astype(BF16)
-            grad_act = dot(grad_top, three[2])
+            grad_act = dot(grad_top, three[:, 2 * block :])
             grad_gate = (grad_act * up_pre * sigma * (1.0 + gate_pre * (1.0 - sigma))).astype(BF16)
             grad_up = (grad_act * silu_gate).astype(BF16)
-            own = jnp.stack(
-                [
-                    contract_rows(mlp_in, grad_gate).astype(BF16),
-                    contract_rows(mlp_in, grad_up).astype(BF16),
-                    contract_rows(grad_top, act).astype(BF16),
-                ]
-            )
-            mlp_grads.append(return_rows(own, far))
+            both = jnp.concatenate([grad_gate, grad_up], 1)
+            own = jnp.concatenate([contract_rows(mlp_in, both), contract_rows(grad_top, act)], 1).astype(BF16)
+            mlp_grads.append(scatter_rows(own))
             acts.append(act)
-            downs.append(three[2])
-            sides += [grad_gate, grad_up]
-            side_weights += [three[0], three[1]]
-        down = jnp.concatenate(downs, 1)
-        sideways = jnp.concatenate(side_weights, 1)
-        grad_mlp_in = plane_scatter(jnp.concatenate(sides, 1), lambda left: contract_cols(left, sideways))
-        mlp_out = plane_scatter(jnp.concatenate(acts, 1), lambda left: contract_cols(left, down))
-        output = (mid + mlp_out).astype(BF16)
+            downs.append(three[:, 2 * block :])
+            if number < len(mlp_weights) - 1:
+                part = contract_cols(both, weight)
+                before = part if before is None else before + part
+        grad_mlp_in = plane_scatter(
+            lambda i, j: contract_cols(both[i:j], weight) + (0.0 if before is None else before[i:j]), own_tokens
+        )
         grad_mid_part, mlp_gain_part = norm_back(grad_mlp_in, mid, recip_mlp, mlp_gain, 0)
         grad_mid = out_grad.astype(F32) + grad_mid_part
         grad_mid_b = plane_gather(grad_mid.astype(BF16))
+        act = jnp.concatenate(acts, 1)
+        act, grad_mid_b = lax.optimization_barrier((act, grad_mid_b))
+        down = jnp.concatenate(downs, 1)
+        mlp_out = plane_scatter(lambda i, j: contract_cols(act[i:j], down), own_tokens)
+        output = (mid + mlp_out).astype(BF16)
         attended_gradient = dot(grad_mid_b, w_o_cols).astype(BF16)
         own_o = contract_rows(grad_mid_b, attended_rows).astype(BF16)
-        grad_w_o = return_rows(own_o[None], far)[0]
+        o_pair = scatter_rows(own_o)
         query_gradient, key_gradient, value_gradient = attend_backward(
             rotated_query_rows,
             rotated_key_rows,
@@ -350,27 +359,31 @@
             [g.reshape(tokens, -1).astype(BF16) for g in (grad_qh, grad_kh, value_gradient)], 1
         )
         own_qkv = contract_rows(normed_rows, grad_qkv).astype(BF16)
-        every_qkv = return_rows(own_qkv[None], far)[0].reshape(rows, 8, -1)
-        grad_normed = plane_scatter(grad_qkv, lambda left: contract_cols(left, qkv))
+        qkv_pair = scatter_rows(own_qkv)
+        grad_normed = plane_scatter(lambda i, j: contract_cols(grad_qkv[i:j], qkv), own_tokens)
         grad_in_part, attn_gain_part = norm_back(grad_normed, inputs, recip_attn, attn_gain, 0)
         grad_input = grad_mid + grad_in_part
         width = inputs.shape[1]
         sums = sum_everywhere(
             jnp.concatenate([attn_gain_part, mlp_gain_part, q_gain_part, k_gain_part]).reshape(1, -1), far
         )[0]
-        grad_gate_w, grad_up_w, grad_down_w = (
-            jnp.concatenate([g[i] for g in mlp_grads], 1) for i in range(3)
+        by_chunk = range(len(chunks))
+        grad_w_gate, grad_w_up, grad_w_down = spread(
+            mlp_grads, [[(j, m * block, block) for j in by_chunk] for m in range(3)]
+        )
+        grad_w_q, grad_w_k, grad_w_v, grad_w_o = spread(
+            [qkv_pair, o_pair], [[(0, 0, q_n)], [(0, q_n, k_n)], [(0, q_n + k_n, k_n)], [(1, 0, o_n)]]
         )
         return (
             output,
             grad_input,
-            every_qkv[:, :, :q_cols].reshape(rows, -1),
-            every_qkv[:, :, q_cols : q_cols + k_cols].reshape(rows, -1),
-            every_qkv[:, :, q_cols + k_cols :].reshape(rows, -1),
+            grad_w_q,
+            grad_w_k,
+            grad_w_v,
             grad_w_o,
-            grad_gate_w,
-            grad_up_w,
-            grad_down_w,
+            grad_w_gate,
+            grad_w_up,
+            grad_w_down,
             sums[:width],
             sums[width : 2 * width],
             sums[2 * width : 2 * width + head],

time: 903 us -> 669 us (0.74)
  starting transfers between devices: 227 us -> 99.1 us
  waiting for transfers between devices: 369 us -> 287 us
  local copies, waits for them, and re-layouts: 133 us -> 77.5 us
  matrix products: 77.4 us -> 114 us
  other arithmetic: 79 us -> 51.6 us
  Pallas kernels: 0 us -> 12.3 us
  between operations: 4.56 us -> 16.3 us
    ppermute x60 -> x0, waiting for transfers between devices: 222 us -> none  [the longest x15 136 us: line_gather(): lax.ppermute(left[-1], 'far', [(i, i - 1) for i in range(1, size - k + 1)])]
    ppermute x60 -> x0, starting transfers between devices: 134 us -> none  [the longest x15 62.7 us: line_scatter(): lax.ppermute(onward, 'far', [(i, i + 1) for i in range(0, size - k)])]
    all_gather x0 -> x5, waiting for transfers between devices: none -> 60.7 us  [gather_rows(): lax.all_gather(blocks.reshape(four * rows, n), 'far', axis=0, tiled=True)]
    ppermute x16 -> x17, waiting for transfers between devices: 19 us -> 62.3 us  [over_mid(): return lax.ppermute(v, 'mid', SWAP)]
    reduce_scatter x0 -> x5, waiting for transfers between devices: none -> 30 us  [scatter_rows(): mine = lax.psum_scatter(parts, 'far', scatter_dimension=0, tiled=True)]
    convert_element_type x30 -> x1, other arithmetic: 22.8 us -> 0.91 us  [on_device(): output = (mid + mlp_out).astype(BF16)]
    another operation x24 -> x2, local copies, waits for them, and re-layouts: 20.9 us -> 1.83 us  [the longest x19 17.4 us: fetch_columns(): stacked = jnp.stack([p.reshape(p.shape[0], 2, 4, -1) for p in pieces])]
    unnamed x272 -> x202, local copies, waits for them, and re-layouts: 49.6 us -> 30.9 us
  transfers between devices with their start and end apart: 120 -> 73, of which waited for: 52 -> 37; matrix products, arithmetic and copies ran while one was open for 26% -> 35% of each run, Pallas kernels for 0% -> 1%
where the time goes in v2:
time: 669 us; the launch traced here: 658 us
  waiting for transfers between devices  287 us (43%)
  matrix products  114 us (17%)
  starting transfers between devices  99.1 us (15%)
  local copies, waits for them, and re-layouts  77.5 us (12%)
  other arithmetic  51.6 us (8%)
  between operations  16.3 us (2%)
  Pallas kernels  12.3 us (2%)
    ppermute x22, waiting for transfers between devices, over_rep(): return lax.ppermute(v, 'rep', SWAP)  97.3 us
    ppermute x17, waiting for transfers between devices, over_mid(): return lax.ppermute(v, 'mid', SWAP)  62.3 us
    all_gather x5, waiting for transfers between devices, gather_rows(): lax.all_gather(blocks.reshape(four * rows, n), 'far', axis=0, tiled=True)  60.7 us
    dot_general x10, matrix products, contract_cols(): lax.dot_general(left, right, (((1,), (1,)), ((), ())), preferred_element_...  43 us
    dot_general x8, matrix products, dot(): return jnp.dot(left, right, preferred_element_type=F32)  38.3 us
    all_to_all x10, starting transfers between devices, trade(): return lax.all_to_all(blocks, ('mid', 'near'), 0, 0)  37.4 us
    ppermute x22, starting transfers between devices, over_rep(): return lax.ppermute(v, 'rep', SWAP)  34.2 us
    unnamed x202, local copies, waits for them, and re-layouts  30.9 us
  transfers between devices with their start and end apart: 73, of which 37 were waited for; matrix products, arithmetic and copies ran while one was open for 35% of the time, Pallas kernels for 1%

profile of v2, /device:TPU:0, one launch (start us, length us, event | category | flops | bytes accessed | tf_op | source)
XLA Modules:
  0.0 658.0 jit_solution(10060153233439431707)
XLA Ops:
  36.6 9.0 %collective-permute-done.1 = bf16[128,2048]{1,0:T(8,128)(2,1)S(1)} collective-permute-done((bf16[128,2048]{1,0:T(8,128)(2,1)S(1)}, bf16[128,2048]{1,0:T(8,128)(2,1)S(1)}, u32[]{:S(2)}, u32[]{:S(2)}) %collective-permute-start.1) | collective-permute-done | bytes 524320 | tf_op jit(solution)/shard_map/ppermute | solution.py:25
  51.9 7.1 %collective-permute-done.2 = bf16[64,2048]{1,0:T(8,128)(2,1)S(1)} collective-permute-done((bf16[64,2048]{1,0:T(8,128)(2,1)S(1)}, bf16[64,2048]{1,0:T(8,128)(2,1)S(1)}, u32[]{:S(2)}, u32[]{:S(2)}) %collective-permute-start.2) | collective-permute-done | bytes 262176 | tf_op jit(solution)/shard_map/ppermute | solution.py:25
  72.9 8.8 %collective-permute-done.6 = s32[2,256]{1,0:T(2,128)S(1)} collective-permute-done((s32[2,256]{1,0:T(2,128)S(1)}, s32[2,256]{1,0:T(2,128)S(1)}, u32[]{:S(2)}, u32[]{:S(2)}) %collective-permute-start.6) | collective-permute-done | bytes 2080 | tf_op jit(solution)/shard_map/ppermute | solution.py:25
  94.4 5.3 fusion.136
  117.8 4.7 fusion.132
  129.7 8.5 %collective-permute-done.14 = bf16[128,2048]{1,0:T(8,128)(2,1)S(1)} collective-permute-done((bf16[128,2048]{1,0:T(8,128)(2,1)}, bf16[128,2048]{1,0:T(8,128)(2,1)S(1)}, u32[]{:S(2)}, u32[]{:S(2)}) %collective-permute-start.14) | collective-permute-done | bytes 524320 | tf_op jit(solution)/shard_map/ppermute | solution.py:21
  143.6 4.8 collective-permute-done.15
  151.9 5.6 collective-permute-done.17
  168.5 7.2 %collective-permute-done.19 = bf16[128,2048]{1,0:T(8,128)(2,1)} collective-permute-done((bf16[128,2048]{1,0:T(8,128)(2,1)}, bf16[128,2048]{1,0:T(8,128)(2,1)}, u32[]{:S(2)}, u32[]{:S(2)}) %collective-permute-start.19) | collective-permute-done | bytes 524320 | tf_op jit(solution)/shard_map/ppermute | solution.py:25
  198.4 5.3 fusion.11
  216.8 14.2 %all-gather.10.cloned.1.call-done = bf16[2048,768]{1,0:T(8,128)(2,1)} async-done(((bf16[512,768]{1,0:T(8,128)(2,1)}), bf16[2048,768]{1,0:T(8,128)(2,1)}) %all-gather.10.cloned.1.call-update) | async-done | bytes 3145744 | tf_op jit(solution)/shard_map/all_gather | solution.py:94
  231.0 5.4 fusion.7
  236.4 5.0 multiply_convert_fusion.3
  242.3 5.8 fusion.5
  248.1 46.5 %all-gather.12.cloned.1.call-done = bf16[2048,768]{1,0:T(8,128)(2,1)} async-done(((bf16[512,768]{1,0:T(8,128)(2,1)}), bf16[2048,768]{1,0:T(8,128)(2,1)}) %all-gather.12.cloned.1.call-update) | async-done | bytes 3145744 | tf_op jit(solution)/shard_map/all_gather | solution.py:94
  294.6 5.4 fusion.3
  319.1 5.0 fusion.133
  327.0 11.7 %collective-permute-done.24 = bf16[128,2048]{1,0:T(8,128)(2,1)S(1)} collective-permute-done((bf16[128,2048]{1,0:T(8,128)(2,1)S(1)}, bf16[128,2048]{1,0:T(8,128)(2,1)S(1)}, u32[]{:S(2)}, u32[]{:S(2)}) %collective-permute-start.24) | collective-permute-done | bytes 524320 | tf_op jit(solution)/shard_map/ppermute | solution.py:21
  363.0 6.4 collective-permute-done.29
  417.9 4.7 convolution_convert_fusion.10
  437.3 6.9 %all-to-all-done.9.refs_4_ = bf16[4,128,768]{2,1,0:T(8,128)(2,1)S(1)} async-done(((bf16[4,128,768]{2,1,0:T(8,128)(2,1)}), bf16[4,128,768]{2,1,0:T(8,128)(2,1)S(1)}, u32[]{:S(2)}, u32[]{:S(2)}) %all-to-all-start.9) | async-done | bytes 786464 | tf_op jit(solution)/shard_map/all_to_all | solution.py:89
  452.6 30.0 %reduce-scatter.10.cloned.1.call-done = bf16[512,768]{0,1:T(8,128)(2,1)} async-done(((bf16[2048,768]{0,1:T(8,128)(2,1)}), bf16[512,768]{0,1:T(8,128)(2,1)}) %reduce-scatter.10.cloned.1.call-update) | async-done | bytes 786448 | tf_op jit(solution)/shard_map/reduce_scatter | solution.py:98
  501.5 5.4 convolution_convert_fusion.6
  510.9 4.7 collective-permute-done.47.refs_5_
  515.6 17.0 %collective-permute-done.46.refs_3_ = bf16[4,128,768]{2,1,0:T(8,128)(2,1)} collective-permute-done((bf16[4,128,768]{2,1,0:T(8,128)(2,1)S(1)}, bf16[4,128,768]{2,1,0:T(8,128)(2,1)}, u32[]{:S(2)}, u32[]{:S(2)}) %collective-permute-start.46) | collective-permute-done | bytes 786464 | tf_op jit(solution)/shard_map/ppermute | solution.py:21
  532.6 16.4 %collective-permute-done.45.refs_1_ = bf16[4,128,768]{2,1,0:T(8,128)(2,1)} collective-permute-done((bf16[4,128,768]{2,1,0:T(8,128)(2,1)S(1)}, bf16[4,128,768]{2,1,0:T(8,128)(2,1)}, u32[]{:S(2)}, u32[]{:S(2)}) %collective-permute-start.45) | collective-permute-done | bytes 786464 | tf_op jit(solution)/shard_map/ppermute | solution.py:21
  549.0 5.4 spread.3
  565.7 4.6 fusion.134
  570.4 7.5 %collective-permute-done.39 = bf16[128,2048]{1,0:T(8,128)(2,1)S(1)} collective-permute-done((bf16[128,2048]{1,0:T(8,128)(2,1)S(1)}, bf16[128,2048]{1,0:T(8,128)(2,1)S(1)}, u32[]{:S(2)}, u32[]{:S(2)}) %collective-permute-start.39) | collective-permute-done | bytes 524320 | tf_op jit(solution)/shard_map/ppermute | solution.py:21
  597.9 6.5 collective-permute-done.42
  627.6 7.9 %all-to-all-done.5.refs_0_ = bf16[4,128,512]{2,1,0:T(8,128)(2,1)S(1)} async-done(((bf16[4,128,512]{2,1,0:T(8,128)(2,1)}), bf16[4,128,512]{2,1,0:T(8,128)(2,1)S(1)}, u32[]{:S(2)}, u32[]{:S(2)}) %all-to-all-start.5) | async-done | bytes 524320 | tf_op jit(solution)/shard_map/all_to_all | solution.py:89
  637.9 11.0 %collective-permute-done.43.refs_1_ = bf16[4,128,512]{2,1,0:T(8,128)(2,1)S(1)} collective-permute-done((bf16[4,128,512]{2,1,0:T(8,128)(2,1)S(1)}, bf16[4,128,512]{2,1,0:T(8,128)(2,1)S(1)}, u32[]{:S(2)}, u32[]{:S(2)}) %collective-permute-start.43) | collective-permute-done | bytes 524320 | tf_op jit(solution)/shard_map/ppermute | solution.py:21
  (483 shorter events, 342.3 us)
Async XLA Ops:
  13.6 80.7 %all-gather.6.cloned.1.call-start = ((), (), s32[]{:S(2)}) async-start(), calls=%async_computation.15 | async-start | bytes 2621440 | tf_op jit(solution)/shard_map/all_gather | solution.py:94
  13.6 20.7 %collective-permute-start.9 = (bf16[128,2048]{1,0:T(8,128)(2,1)}, bf16[128,2048]{1,0:T(8,128)(2,1)S(1)}, u32[]{:S(2)}, u32[]{:S(2)}) collective-permute-start(bf16[128,2048]{1,0:T(8,128)(2,1)} %param.16), channel_id=1, source_target_pairs={{0,2},{2,0},{1,3},{3,1},{4,6},{6,4},{5,7},{7,5},{8,10},{10,8},{9,1... | collective-permute-start | bytes 1572872 | tf_op jit(solution)/shard_map/ppermute | solution.py:25
  15.9 20.5 %collective-permute-start.8 = (bf16[128,2048]{1,0:T(8,128)(2,1)}, bf16[128,2048]{1,0:T(8,128)(2,1)S(1)}, u32[]{:S(2)}, u32[]{:S(2)}) collective-permute-start(bf16[128,2048]{1,0:T(8,128)(2,1)} %param.16), channel_id=1, source_target_pairs={{0,16},{16,0},{1,17},{17,1},{2,18},{18,2},{3,19},{19,3},{4,20},{20... | collective-permute-start | bytes 1572872 | tf_op jit(solution)/shard_map/ppermute | solution.py:21
  25.0 20.6 %collective-permute-start.1 = (bf16[128,2048]{1,0:T(8,128)(2,1)S(1)}, bf16[128,2048]{1,0:T(8,128)(2,1)S(1)}, u32[]{:S(2)}, u32[]{:S(2)}) collective-permute-start(bf16[128,2048]{1,0:T(8,128)(2,1)S(1)} %get-tuple-element.61), channel_id=1, source_target_pairs={{0,2},{2,0},{1,3},{3,1},{4,6},{6,4},{5,7},{7,5},{8,10},{10,8},{9,1... | collective-permute-start | bytes 1572872 | tf_op jit(solution)/shard_map/ppermute | solution.py:25
  25.0 22.7 %collective-permute-start = (bf16[128,2048]{1,0:T(8,128)(2,1)S(1)}, bf16[128,2048]{1,0:T(8,128)(2,1)S(1)}, u32[]{:S(2)}, u32[]{:S(2)}) collective-permute-start(bf16[128,2048]{1,0:T(8,128)(2,1)S(1)} %get-tuple-element.61), channel_id=1, source_target_pairs={{0,16},{16,0},{1,17},{17,1},{2,18},{18,2},{3,19},{19,3},{4,20},{20... | collective-permute-start | bytes 1572872 | tf_op jit(solution)/shard_map/ppermute | solution.py:21
  27.0 39.5 %all-to-all-start.1 = ((bf16[4,128,256]{2,1,0:T(8,128)(2,1)}), bf16[4,128,256]{2,1,0:T(8,128)(2,1)S(1)}, u32[]{:S(2)}, u32[]{:S(2)}) async-start(bf16[4,128,256]{2,1,0:T(8,128)(2,1)} %get-tuple-element.31), calls=%async_computation.1 | async-start | bytes 524288 | tf_op jit(solution)/shard_map/all_to_all | solution.py:89
  34.4 27.1 %collective-permute-start.11 = (bf16[64,2048]{1,0:T(8,128)(2,1)S(1)}, bf16[64,2048]{1,0:T(8,128)(2,1)S(1)}, u32[]{:S(2)}, u32[]{:S(2)}) collective-permute-start(bf16[64,2048]{1,0:T(8,128)(2,1)S(1)} %slice.506), channel_id=1, source_target_pairs={{0,16},{16,0},{1,17},{17,1},{2,18},{18,2},{3,19},{19,3},{4,20},{20... | collective-permute-start | bytes 786440 | tf_op jit(solution)/shard_map/ppermute | solution.py:21
  36.4 24.1 %collective-permute-start.10 = (bf16[64,2048]{1,0:T(8,128)(2,1)S(1)}, bf16[64,2048]{1,0:T(8,128)(2,1)S(1)}, u32[]{:S(2)}, u32[]{:S(2)}) collective-permute-start(bf16[64,2048]{1,0:T(8,128)(2,1)S(1)} %slice.505), channel_id=1, source_target_pairs={{0,2},{2,0},{1,3},{3,1},{4,6},{6,4},{5,7},{7,5},{8,10},{10,8},{9,1... | collective-permute-start | bytes 786440 | tf_op jit(solution)/shard_map/ppermute | solution.py:25
  60.5 29.2 %collective-permute-start.4 = (bf16[512,2048]{1,0:T(8,128)(2,1)}, bf16[512,2048]{1,0:T(8,128)(2,1)S(1)}, u32[]{:S(2)}, u32[]{:S(2)}) collective-permute-start(bf16[512,2048]{1,0:T(8,128)(2,1)} %get-tuple-element.137), channel_id=1, source_target_pairs={{0,1},{1,0},{2,3},{3,2},{4,5},{5,4},{6,7},{7,6},{8,9},{9,8},{10,11... | collective-permute-start | bytes 6291464 | tf_op jit(solution)/shard_map/ppermute | solution.py:29
  62.9 28.3 %collective-permute-start.12 = (bf16[512,2048]{1,0:T(8,128)(2,1)}, bf16[512,2048]{1,0:T(8,128)(2,1)}, u32[]{:S(2)}, u32[]{:S(2)}) collective-permute-start(bf16[512,2048]{1,0:T(8,128)(2,1)} %get-tuple-element.133), channel_id=1, source_target_pairs={{0,1},{1,0},{2,3},{3,2},{4,5},{5,4},{6,7},{7,6},{8,9},{9,8},{10,11... | collective-permute-start | bytes 6291464 | tf_op jit(solution)/shard_map/ppermute | solution.py:29
  66.5 22.3 %all-to-all-start.4 = ((bf16[4,128,768]{2,1,0:T(8,128)(2,1)}), bf16[4,128,768]{2,1,0:T(8,128)(2,1)S(1)}, u32[]{:S(2)}, u32[]{:S(2)}) async-start(bf16[4,128,768]{2,1,0:T(8,128)(2,1)} %get-tuple-element.34), calls=%async_computation.4 | async-start | bytes 1572864 | tf_op jit(solution)/shard_map/all_to_all | solution.py:89
  70.0 39.7 %all-gather.8.cloned.1.call-start = ((), (), s32[]{:S(2)}) async-start(), calls=%async_computation.16 | async-start | bytes 1310720 | tf_op jit(solution)/shard_map/all_gather | solution.py:94
  70.8 127.7 %all-gather.14.cloned.1.call-start = ((), (), s32[]{:S(2)}) async-start(), calls=%async_computation.19 | async-start | bytes 3932160 | tf_op jit(solution)/shard_map/all_gather | solution.py:94
  117.5 113.5 %all-gather.10.cloned.1.call-start = ((), (), s32[]{:S(2)}) async-start(), calls=%async_computation.17 | async-start | bytes 3932160 | tf_op jit(solution)/shard_map/all_gather | solution.py:94
  161.4 16.9 %collective-permute-start.18 = (bf16[128,2048]{1,0:T(8,128)(2,1)}, bf16[128,2048]{1,0:T(8,128)(2,1)}, u32[]{:S(2)}, u32[]{:S(2)}) collective-permute-start(bf16[128,2048]{1,0:T(8,128)(2,1)} %get-tuple-element.57), channel_id=1, source_target_pairs={{0,16},{16,0},{1,17},{17,1},{2,18},{18,2},{3,19},{19,3},{4,20},{20... | collective-permute-start | bytes 1572872 | tf_op jit(solution)/shard_map/ppermute | solution.py:21
  163.2 27.6 %all-to-all-start.3 = ((bf16[4,128,768]{2,1,0:T(8,128)(2,1)}), bf16[4,128,768]{2,1,0:T(8,128)(2,1)}, u32[]{:S(2)}, u32[]{:S(2)}) async-start(bf16[4,128,768]{2,1,0:T(8,128)(2,1)} %get-tuple-element.33), calls=%async_computation.3 | async-start | bytes 1572864 | tf_op jit(solution)/shard_map/all_to_all | solution.py:89
  167.4 127.2 %all-gather.12.cloned.1.call-start = ((), (), s32[]{:S(2)}) async-start(), calls=%async_computation.18 | async-start | bytes 3932160 | tf_op jit(solution)/shard_map/all_gather | solution.py:94
  190.8 235.9 %reduce-scatter.14.cloned.1.call-start = ((), (), s32[]{:S(2)}) async-start(), calls=%async_computation.24 | async-start | bytes 3932160 | tf_op jit(solution)/shard_map/reduce_scatter | solution.py:98
  216.3 218.3 %reduce-scatter.12.cloned.1.call-start = ((), (), s32[]{:S(2)}) async-start(), calls=%async_computation.23 | async-start | bytes 3932160 | tf_op jit(solution)/shard_map/reduce_scatter | solution.py:98
  319.0 163.6 %reduce-scatter.10.cloned.1.call-start = ((), (), s32[]{:S(2)}) async-start(), calls=%async_computation.22 | async-start | bytes 3932160 | tf_op jit(solution)/shard_map/reduce_scatter | solution.py:98
  361.7 192.7 %reduce-scatter.8.cloned.1.call-start = ((), (), s32[]{:S(2)}) async-start(), calls=%async_computation.21 | async-start | bytes 1310720 | tf_op jit(solution)/shard_map/reduce_scatter | solution.py:98
  444.2 40.8 %all-to-all-start.8 = ((bf16[4,128,768]{2,1,0:T(8,128)(2,1)}), bf16[4,128,768]{2,1,0:T(8,128)(2,1)S(1)}, u32[]{:S(2)}, u32[]{:S(2)}) async-start(bf16[4,128,768]{2,1,0:T(8,128)(2,1)} %bitcast.54), calls=%async_computation.12 | async-start | bytes 1572864 | tf_op jit(solution)/shard_map/all_to_all | solution.py:89
  452.2 105.9 %collective-permute-start.38 = (bf16[512,2048]{1,0:T(8,128)(2,1)}, bf16[512,2048]{1,0:T(8,128)(2,1)}, u32[]{:S(2)}, u32[]{:S(2)}) collective-permute-start(bf16[512,2048]{1,0:T(8,128)(2,1)} %convolution_convert_fusion.5), channel_id=1, source_target_pairs={{0,1},{1,0},{2,3},{3,2},{4,5},{5,4},{6,7},{7,6},{8,9},{9,8},{10,11... | collective-permute-start | bytes 6291464 | tf_op jit(solution)/shard_map/ppermute | solution.py:29
  488.4 134.7 %reduce-scatter.6.cloned.1.call-start = ((), (), s32[]{:S(2)}) async-start(), calls=%async_computation.20 | async-start | bytes 2621440 | tf_op jit(solution)/shard_map/reduce_scatter | solution.py:98
  495.3 20.3 %collective-permute-start.47 = (bf16[4,128,768]{2,1,0:T(8,128)(2,1)S(1)}, bf16[4,128,768]{2,1,0:T(8,128)(2,1)S(1)}, u32[]{:S(2)}, u32[]{:S(2)}) collective-permute-start(bf16[4,128,768]{2,1,0:T(8,128)(2,1)S(1)} %all-to-all-done.9.refs_4_), channel_id=1, source_target_pairs={{0,16},{16,0},{1,17},{17,1},{2,18},{18,2},{3,19},{19,3},{4,20},{20... | collective-permute-start | bytes 2359304 | tf_op jit(solution)/shard_map/ppermute | solution.py:21
  496.8 35.8 %collective-permute-start.46 = (bf16[4,128,768]{2,1,0:T(8,128)(2,1)S(1)}, bf16[4,128,768]{2,1,0:T(8,128)(2,1)}, u32[]{:S(2)}, u32[]{:S(2)}) collective-permute-start(bf16[4,128,768]{2,1,0:T(8,128)(2,1)S(1)} %all-to-all-done.8.refs_2_), channel_id=1, source_target_pairs={{0,16},{16,0},{1,17},{17,1},{2,18},{18,2},{3,19},{19,3},{4,20},{20... | collective-permute-start | bytes 2359304 | tf_op jit(solution)/shard_map/ppermute | solution.py:21
  500.1 48.9 %collective-permute-start.45 = (bf16[4,128,768]{2,1,0:T(8,128)(2,1)S(1)}, bf16[4,128,768]{2,1,0:T(8,128)(2,1)}, u32[]{:S(2)}, u32[]{:S(2)}) collective-permute-start(bf16[4,128,768]{2,1,0:T(8,128)(2,1)S(1)} %all-to-all-done.7.refs_0_), channel_id=1, source_target_pairs={{0,16},{16,0},{1,17},{17,1},{2,18},{18,2},{3,19},{19,3},{4,20},{20... | collective-permute-start | bytes 2359304 | tf_op jit(solution)/shard_map/ppermute | solution.py:21
  506.9 58.8 %collective-permute-start.33 = (bf16[512,2048]{1,0:T(8,128)(2,1)}, bf16[512,2048]{1,0:T(8,128)(2,1)}, u32[]{:S(2)}, u32[]{:S(2)}) collective-permute-start(bf16[512,2048]{1,0:T(8,128)(2,1)} %convolution_convert_fusion.6), channel_id=1, source_target_pairs={{0,1},{1,0},{2,3},{3,2},{4,5},{5,4},{6,7},{7,6},{8,9},{9,8},{10,11... | collective-permute-start | bytes 6291464 | tf_op jit(solution)/shard_map/ppermute | solution.py:29
  554.4 29.6 %all-to-all-start.6 = ((bf16[4,128,256]{2,1,0:T(8,128)(2,1)}), bf16[4,128,256]{2,1,0:T(8,128)(2,1)S(1)}, u32[]{:S(2)}, u32[]{:S(2)}) async-start(bf16[4,128,256]{2,1,0:T(8,128)(2,1)} %bitcast.198), calls=%async_computation.8 | async-start | bytes 524288 | tf_op jit(solution)/shard_map/all_to_all | solution.py:89
  562.1 22.4 %collective-permute-start.41 = (bf16[128,2048]{1,0:T(8,128)(2,1)S(1)}, bf16[128,2048]{1,0:T(8,128)(2,1)S(1)}, u32[]{:S(2)}, u32[]{:S(2)}) collective-permute-start(bf16[128,2048]{1,0:T(8,128)(2,1)S(1)} %pad_maximum_fusion.30), channel_id=1, source_target_pairs={{0,2},{2,0},{1,3},{3,1},{4,6},{6,4},{5,7},{7,5},{8,10},{10,8},{9,1... | collective-permute-start | bytes 1572872 | tf_op jit(solution)/shard_map/ppermute | solution.py:25
  582.3 23.7 %collective-permute-start.36 = (bf16[128,2048]{1,0:T(8,128)(2,1)}, bf16[128,2048]{1,0:T(8,128)(2,1)S(1)}, u32[]{:S(2)}, u32[]{:S(2)}) collective-permute-start(bf16[128,2048]{1,0:T(8,128)(2,1)} %pad_maximum_fusion.27), channel_id=1, source_target_pairs={{0,2},{2,0},{1,3},{3,1},{4,6},{6,4},{5,7},{7,5},{8,10},{10,8},{9,1... | collective-permute-start | bytes 1572872 | tf_op jit(solution)/shard_map/ppermute | solution.py:25
  584.0 54.0 %collective-permute-start.44 = (bf16[4,128,256]{2,1,0:T(8,128)(2,1)S(1)}, bf16[4,128,256]{2,1,0:T(8,128)(2,1)S(1)}, u32[]{:S(2)}, u32[]{:S(2)}) collective-permute-start(bf16[4,128,256]{2,1,0:T(8,128)(2,1)S(1)} %all-to-all-done.6.refs_2_), channel_id=1, source_target_pairs={{0,16},{16,0},{1,17},{17,1},{2,18},{18,2},{3,19},{19,3},{4,20},{20... | collective-permute-start | bytes 786440 | tf_op jit(solution)/shard_map/ppermute | solution.py:21
  (131 other events, 1327.0 us)
Sparse Core Ops, SparseCore 0:
  24.1 46.6 all-gather.5
  72.4 30.2 all-gather.7
  104.3 62.9 all-gather.13
  168.8 62.1 all-gather.9
  232.4 62.1 all-gather.11
  297.3 58.8 reduce-scatter.13
  359.1 60.2 reduce-scatter.11
  422.3 60.2 reduce-scatter.9
  485.0 27.1 reduce-scatter.7
  514.4 42.4 reduce-scatter.5

commit v3 on v2

v3 whole, which is shorter than its diff:
```python
import math

import jax
import jax.numpy as jnp
from jax import lax
from jax.experimental import pallas as pl
from jax.experimental.pallas import tpu as pltpu
from jax.sharding import Mesh
from jax.sharding import PartitionSpec as P

EPSILON = 1e-06
ROPE_BASE = 1000000.0
NEG_FILL = -1e30
F32 = jnp.float32
BF16 = jnp.bfloat16
SWAP = [(0, 1), (1, 0)]


def over_rep(v):
    return lax.ppermute(v, "rep", SWAP)


def over_mid(v):
    return lax.ppermute(v, "mid", SWAP)


def over_near(v):
    return lax.ppermute(v, "near", SWAP)


def plane_gather(own):
    half = own.shape[0] // 2
    from_rep = over_rep(own)
    from_mid = over_mid(own)
    top = over_mid(from_rep[:half])
    bottom = over_rep(from_mid[half:])
    mine = jnp.concatenate([own, from_rep, from_mid, top, bottom], 0)
    return jnp.concatenate([mine, over_near(mine)], 0)


def plane_scatter(partial, rows):
    half = rows // 2
    near = over_near(partial(4 * rows, 8 * rows).astype(BF16))
    part = partial(0, 4 * rows) + near.astype(F32)
    own, rep, mid, both = (part[i * rows : (i + 1) * rows] for i in range(4))
    first_rep = over_rep(jnp.concatenate([both[:half], rep[:half]], 0).astype(BF16))
    first_mid = over_mid(jnp.concatenate([both[half:], mid[half:]], 0).astype(BF16))
    last_mid = over_mid((mid[:half] + first_rep[:half].astype(F32)).astype(BF16))
    last_rep = over_rep((rep[half:] + first_mid[:half].astype(F32)).astype(BF16))
    top = own[:half] + first_rep[half:].astype(F32) + last_mid.astype(F32)
    bottom = own[half:] + last_rep.astype(F32) + first_mid[half:].astype(F32)
    return jnp.concatenate([top, bottom], 0)


def pick_columns(groups):
    side = lax.axis_index("rep").astype(jnp.int32).reshape(1)
    members = [m for group in groups for m in group]
    rows = members[0][0].shape[0]
    widths = [sum(n for _, _, n in group) for group in groups]

    def kernel(side_ref, *refs):
        sources = iter(refs[: len(members)])
        for group, out in zip(groups, refs[len(members) :]):
            at = 0
            for _, _, n in group:
                source = next(sources)
                for block in range(4):
                    out[block, :, at : at + n] = source[:, block * n : (block + 1) * n]
                at += n

    def half(start, n):
        return pl.BlockSpec((rows, 4 * n), lambda i, side_ref: (0, start // (4 * n) + side_ref[0]))

    return pl.pallas_call(
        kernel,
        grid_spec=pltpu.PrefetchScalarGridSpec(
            num_scalar_prefetch=1,
            grid=(1,),
            in_specs=[half(start, n) for _, start, n in members],
            out_specs=[pl.BlockSpec((4, rows, w), lambda i, side_ref: (0, 0, 0)) for w in widths],
        ),
        out_shape=[jax.ShapeDtypeStruct((4, rows, w), BF16) for w in widths],
        compiler_params=pltpu.CompilerParams(vmem_limit_bytes=20 << 20),
        name="pick_columns",
    )(side, *[m for m, _, _ in members])


def trade(blocks):
    return lax.all_to_all(blocks, ("mid", "near"), 0, 0)


def gather_rows(blocks):
    four, rows, n = blocks.shape
    return lax.all_gather(blocks.reshape(four * rows, n), "far", axis=0, tiled=True)


def queue_scatter(parts):
    return lax.psum_scatter(parts, "far", scatter_dimension=0, tiled=True)


def hand_out(mine):
    mine = trade(mine.reshape(4, mine.shape[0] // 4, -1))
    return (mine, over_rep(mine))


def spread(pairs, outs):
    side = lax.axis_index("rep").astype(jnp.int32).reshape(1)
    rows = pairs[0][0].shape[1]
    columns = [sum(8 * n for _, _, n in pieces) for pieces in outs]

    def kernel(side_ref, *refs):
        first = side_ref[0] == 0
        for out, pieces in zip(refs[2 * len(pairs) :], outs):
            at = 0
            for pair, start, n in pieces:
                own, other = refs[2 * pair], refs[2 * pair + 1]
                for block in range(4):
                    a = own[block, :, start : start + n].astype(F32)
                    b = other[block, :, start : start + n].astype(F32)
                    out[:, at + block * n : at + (block + 1) * n] = jnp.where(first, a, b)
                    out[:, at + (4 + block) * n : at + (5 + block) * n] = jnp.where(first, b, a)
                at += 8 * n

    return pl.pallas_call(
        kernel,
        in_specs=[pl.BlockSpec(memory_space=pltpu.SMEM)] + [pl.BlockSpec(memory_space=pltpu.VMEM)] * (2 * len(pairs)),
        out_specs=[pl.BlockSpec(memory_space=pltpu.VMEM)] * len(outs),
        out_shape=[jax.ShapeDtypeStruct((rows, c), F32) for c in columns],
        compiler_params=pltpu.CompilerParams(vmem_limit_bytes=40 << 20),
        name="spread",
    )(side, *[v for pair in pairs for v in pair])


def sum_everywhere(v, size):
    for axis in ("near", "mid", "rep"):
        v = v + lax.ppermute(v, axis, SWAP)
    if size & (size - 1):
        return lax.psum(v, "far")
    step = 1
    while step < size:
        v = v + lax.ppermute(v, "far", [(i, i ^ step) for i in range(size)])
        step *= 2
    return v


def after(*values):
    return lax.optimization_barrier(values)


def rope_tables(positions, half):
    freq = jnp.exp(jnp.arange(half, dtype=F32) * (-math.log(ROPE_BASE) / half))
    angles = positions.reshape(-1).astype(F32)[:, None] * freq
    cosine, sine = (jnp.cos(angles), jnp.sin(angles))
    return (jnp.concatenate([cosine, cosine], 1), jnp.concatenate([-sine, sine], 1))


def norm_back(grads, inputs, recip, gain, axes):
    normal = inputs * recip
    scaled = grads * gain
    gain_grad = jnp.sum(grads * normal, axis=axes)
    input_grad = recip * (scaled - normal * jnp.mean(scaled * normal, -1, keepdims=True))
    return (input_grad, gain_grad)


def dot(left, right):
    return jnp.dot(left, right, preferred_element_type=F32)


def contract_rows(left, right):
    return lax.dot_general(left, right, (((0,), (0,)), ((), ())), preferred_element_type=F32)


def contract_cols(left, right):
    return lax.dot_general(left, right, (((1,), (1,)), ((), ())), preferred_element_type=F32)


def swap_halves(v):
    half = v.shape[-1] // 2
    return jnp.concatenate([v[:, half:], v[:, :half]], -1)


def unit(u):
    recip = lax.rsqrt(jnp.mean(u * u, -1, keepdims=True) + EPSILON)
    return (u * recip, recip)


def sequence_state(proj_ref, cosine_ref, sine_ref, down_ref, across_ref, head):
    length = proj_ref.shape[0]
    later = lax.broadcasted_iota(jnp.int32, (length, length), 0)
    earlier = lax.broadcasted_iota(jnp.int32, (length, length), 1)
    mask = (down_ref[...] == across_ref[0]) & (earlier <= later)
    cosine, sine = cosine_ref[...], sine_ref[...]

    def turned(v):
        return v * cosine + swap_halves(v) * sine

    def turned_back(v):
        return v * cosine - swap_halves(v) * sine

    def columns(i):
        return proj_ref[:, i * head : (i + 1) * head]

    return (mask, turned, turned_back, columns)


def masked_scores(query, key, mask, head):
    return jnp.where(mask, contract_cols(query, key) * head ** (-0.5), NEG_FILL)


def attention_forward(proj, cosine, sine, down, across, q_gain, k_gain, heads, kv_heads):
    head = q_gain.shape[1]
    sequences, _, length = across.shape
    groups = heads // kv_heads

    def kernel(proj_ref, cosine_ref, sine_ref, down_ref, across_ref, q_gain_ref, k_gain_ref, out_ref):
        mask, turned, _, columns = sequence_state(proj_ref, cosine_ref, sine_ref, down_ref, across_ref, head)
        for kv in range(kv_heads):
            key = turned(unit(columns(heads + kv))[0] * k_gain_ref[...]).astype(BF16)
            value = columns(heads + kv_heads + kv).astype(BF16)
            for h in range(kv * groups, (kv + 1) * groups):
                query = turned(unit(columns(h))[0] * q_gain_ref[...]).astype(BF16)
                scores = masked_scores(query, key, mask, head)
                expo = jnp.exp(scores - jnp.max(scores, -1, keepdims=True))
                probs = (expo / jnp.sum(expo, -1, keepdims=True)).astype(BF16)
                out_ref[:, h * head : (h + 1) * head] = dot(probs, value).astype(BF16)

    row = lambda n: pl.BlockSpec((length, n), lambda i: (i, 0))
    fixed = pl.BlockSpec((1, head), lambda i: (0, 0))
    return pl.pallas_call(
        kernel,
        grid=(sequences,),
        in_specs=[row(proj.shape[1]), row(head), row(head), row(1)]
        + [pl.BlockSpec((1, 1, length), lambda i: (i, 0, 0)), fixed, fixed],
        out_specs=row(heads * head),
        out_shape=jax.ShapeDtypeStruct((proj.shape[0], heads * head), BF16),
        compiler_params=pltpu.CompilerParams(vmem_limit_bytes=6 << 20),
        name="attention_forward",
    )(proj, cosine, sine, down, across, q_gain, k_gain)


def attention_backward(proj, cosine, sine, down, across, q_gain, k_gain, attended, attended_grad, heads, kv_heads):
    head = q_gain.shape[1]
    sequences, _, length = across.shape
    groups = heads // kv_heads
    scale = head ** (-0.5)

    def kernel(
        proj_ref,
        cosine_ref,
        sine_ref,
        down_ref,
        across_ref,
        q_gain_ref,
        k_gain_ref,
        attended_ref,
        grad_ref,
        out_ref,
        gains_ref,
    ):
        mask, turned, turned_back, columns = sequence_state(
            proj_ref, cosine_ref, sine_ref, down_ref, across_ref, head
        )

        @pl.when(pl.program_id(0) == 0)
        def _():
            gains_ref[...] = jnp.zeros_like(gains_ref)

        def put(i, v):
            out_ref[:, i * head : (i + 1) * head] = v.astype(BF16)

        def norm_grad(i, grads, normal, recip, gain, row):
            scaled = grads * gain
            gains_ref[row : row + 1, :] += jnp.sum(grads * normal, 0, keepdims=True)
            put(i, recip * (scaled - normal * jnp.mean(scaled * normal, -1, keepdims=True)))

        for kv in range(kv_heads):
            key_unit, key_recip = unit(columns(heads + kv))
            key = turned(key_unit * k_gain_ref[...]).astype(BF16)
            value = columns(heads + kv_heads + kv).astype(BF16)
            grad_value = jnp.zeros((length, head), F32)
            grad_key = jnp.zeros((length, head), F32)
            for h in range(kv * groups, (kv + 1) * groups):
                query_unit, query_recip = unit(columns(h))
                query = turned(query_unit * q_gain_ref[...]).astype(BF16)
                scores = masked_scores(query, key, mask, head)
                top = jnp.max(scores, -1, keepdims=True)
                log_total = top + jnp.log(jnp.sum(jnp.exp(scores - top), -1, keepdims=True))
                probs = jnp.where(mask, jnp.exp(scores - log_total), 0.0)
                grad = grad_ref[:, h * head : (h + 1) * head]
                grad_value += contract_rows(probs.astype(BF16), grad)
                complete = attended_ref[:, h * head : (h + 1) * head].astype(F32)
                delta = jnp.sum(grad.astype(F32) * complete, -1, keepdims=True)
                grad_scores = (probs * (contract_cols(grad, value) - delta)).astype(BF16)
                grad_query = dot(grad_scores, key) * scale
                grad_key += contract_rows(grad_scores, query)
                norm_grad(h, turned_back(grad_query), query_unit, query_recip, q_gain_ref[...], 0)
            norm_grad(heads + kv, turned_back(grad_key * scale), key_unit, key_recip, k_gain_ref[...], 1)
            put(heads + kv_heads + kv, grad_value)

    row = lambda n: pl.BlockSpec((length, n), lambda i: (i, 0))
    fixed = pl.BlockSpec((1, head), lambda i: (0, 0))
    return pl.pallas_call(
        kernel,
        grid=(sequences,),
        in_specs=[row(proj.shape[1]), row(head), row(head), row(1)]
        + [pl.BlockSpec((1, 1, length), lambda i: (i, 0, 0)), fixed, fixed]
        + [row(heads * head), row(heads * head)],
        out_specs=[row(proj.shape[1]), pl.BlockSpec((8, head), lambda i: (0, 0))],
        out_shape=[jax.ShapeDtypeStruct(proj.shape, BF16), jax.ShapeDtypeStruct((8, head), F32)],
        compiler_params=pltpu.CompilerParams(vmem_limit_bytes=8 << 20),
        name="attention_backward",
    )(proj, cosine, sine, down, across, q_gain, k_gain, attended, attended_grad)


def plane_notes(own):
    pair = jnp.concatenate([own, over_near(own)], 0)
    four = jnp.concatenate([pair, over_mid(pair)], 0)
    eight = jnp.concatenate([four, over_rep(four)], 0)
    return jnp.concatenate([eight[i : i + 1] for i in (0, 4, 2, 6, 1, 5, 3, 7)], 0)


def build(far):
    def on_device(
        block_input,
        out_grad,
        segments,
        positions,
        attn_gain,
        mlp_gain,
        q_gain,
        k_gain,
        w_q,
        key_matrix,
        value_matrix,
        w_o,
        w_gate,
        w_up,
        w_down,
    ):
        head = q_gain.shape[0]
        heads = w_q.shape[1] // head // 8
        kv_heads = key_matrix.shape[1] // head // 8
        hidden = w_gate.shape[1]
        rows = w_q.shape[0]
        q_cols = heads * head
        k_cols = kv_heads * head
        part = hidden // 3 if hidden % 3072 == 0 else hidden
        chunks = [(start, part // 8) for start in range(0, hidden, part)]

        q_n, k_n, o_n = (w.shape[1] // 8 for w in (w_q, key_matrix, w_o))
        (attn_slot,) = pick_columns(
            [[(w_q, 0, q_n), (key_matrix, 0, k_n), (value_matrix, 0, k_n), (w_o, 0, o_n)]]
        )
        mlp_slots = pick_columns([[(w, start, n) for w in (w_gate, w_up, w_down)] for start, n in chunks])
        inputs = block_input.astype(F32)
        recip_attn = lax.rsqrt(jnp.mean(inputs * inputs, -1, keepdims=True) + EPSILON)
        normed_own = (inputs * recip_attn * attn_gain).astype(BF16)
        traded = [trade(slot) for slot in (attn_slot, *mlp_slots)]
        attn_weights, *mlp_weights = [gather_rows(v) for v in traded]
        qkv, w_o_cols = attn_weights[:, : q_n + 2 * k_n], attn_weights[:, q_n + 2 * k_n :]

        normed_rows = plane_gather(normed_own)
        grad_top = plane_gather(out_grad)
        notes = plane_notes(jnp.concatenate([segments, positions], 1))
        length = segments.shape[1]
        own_tokens = inputs.shape[0]
        tokens = normed_rows.shape[0]
        across = notes[:, None, :length]
        cosine, sine = rope_tables(notes[:, length:], head // 2)
        attention = (cosine, sine, across.reshape(tokens, 1), across, q_gain[None], k_gain[None])

        proj = dot(normed_rows, qkv)
        attended_rows = attention_forward(proj, *attention, heads, kv_heads)
        attended_rows, grad_top = lax.optimization_barrier((attended_rows, grad_top))
        mid = inputs + plane_scatter(lambda i, j: contract_cols(attended_rows[i:j], w_o_cols), own_tokens)
        recip_mlp = lax.rsqrt(jnp.mean(mid * mid, -1, keepdims=True) + EPSILON)
        mlp_in = plane_gather((mid * recip_mlp * mlp_gain).astype(BF16))

        acts, downs, owns, boths = [], [], [], []
        before = None
        for number, three in enumerate(mlp_weights):
            block = chunks[number][1]
            if number == 2:
                grad_top, owns[0] = after(grad_top, owns[0])
            weight = three[:, : 2 * block]
            pre = dot(mlp_in, weight)
            gate_pre, up_pre = pre[:, :block], pre[:, block:]
            sigma = jax.nn.sigmoid(gate_pre)
            silu_gate = gate_pre * sigma
            act = (silu_gate * up_pre).astype(BF16)
            grad_act = dot(grad_top, three[:, 2 * block :])
            grad_gate = (grad_act * up_pre * sigma * (1.0 + gate_pre * (1.0 - sigma))).astype(BF16)
            grad_up = (grad_act * silu_gate).astype(BF16)
            both = jnp.concatenate([grad_gate, grad_up], 1)
            own = jnp.concatenate([contract_rows(mlp_in, both), contract_rows(grad_top, act)], 1).astype(BF16)
            owns.append(own)
            boths.append(both)
            acts.append(act)
            downs.append(three[:, 2 * block :])
            if number < len(mlp_weights) - 1:
                part = contract_cols(both, weight)
                before = part if before is None else before + part
        grad_mlp_in = plane_scatter(
            lambda i, j: contract_cols(both[i:j], weight) + (0.0 if before is None else before[i:j]), own_tokens
        )
        grad_mid_part, mlp_gain_part = norm_back(grad_mlp_in, mid, recip_mlp, mlp_gain, 0)
        grad_mid = out_grad.astype(F32) + grad_mid_part
        mlp_rows = [queue_scatter(own) for own in owns[:-1]]
        grad_mid_b, owns[-1] = after(grad_mid.astype(BF16), owns[-1])
        grad_mid_b = plane_gather(grad_mid_b)
        act = jnp.concatenate(acts, 1)
        act, grad_mid_b = lax.optimization_barrier((act, grad_mid_b))
        down = jnp.concatenate(downs, 1)
        mlp_out = plane_scatter(lambda i, j: contract_cols(act[i:j], down), own_tokens)
        output = (mid + mlp_out).astype(BF16)
        attended_gradient = dot(grad_mid_b, w_o_cols).astype(BF16)
        own_o = contract_rows(grad_mid_b, attended_rows).astype(BF16)
        last_own = jnp.concatenate([owns[-1], own_o], 1)
        mlp_rows.append(queue_scatter(last_own))
        grad_qkv, head_gains = attention_backward(
            proj, *attention, attended_rows, attended_gradient, heads, kv_heads
        )
        own_qkv = contract_rows(normed_rows, grad_qkv).astype(BF16)
        mlp_grads = [hand_out(v) for v in mlp_rows[:-1]] + [None]
        grad_normed = plane_scatter(lambda i, j: contract_cols(grad_qkv[i:j], qkv), own_tokens)
        grad_in_part, attn_gain_part = norm_back(grad_normed, inputs, recip_attn, attn_gain, 0)
        grad_input = grad_mid + grad_in_part
        width = inputs.shape[1]
        sums = sum_everywhere(
            jnp.concatenate([attn_gain_part, mlp_gain_part, head_gains[0], head_gains[1]]).reshape(1, -1), far
        )[0]
        own_qkv, sums, grad_input, mlp_grads[:-1], mlp_rows[-1] = after(
            own_qkv, sums, grad_input, mlp_grads[:-1], mlp_rows[-1]
        )
        qkv_rows = queue_scatter(own_qkv)
        mlp_grads[-1] = hand_out(mlp_rows[-1])
        qkv_pair = hand_out(qkv_rows)
        last = len(chunks) - 1
        gate_pieces, up_pieces, down_pieces = ([(j, m * n, n) for j, (_, n) in enumerate(chunks)] for m in range(3))
        grad_w_gate, grad_w_up, grad_w_down, grad_w_o = spread(
            mlp_grads, [gate_pieces, up_pieces, down_pieces, [(last, 3 * chunks[last][1], o_n)]]
        )
        grad_w_q, grad_w_k, grad_w_v = spread([qkv_pair], [[(0, 0, q_n)], [(0, q_n, k_n)], [(0, q_n + k_n, k_n)]])
        return (
            output,
            grad_input,
            grad_w_q,
            grad_w_k,
            grad_w_v,
            grad_w_o,
            grad_w_gate,
            grad_w_up,
            grad_w_down,
            sums[:width],
            sums[width : 2 * width],
            sums[2 * width : 2 * width + head],
            sums[2 * width + head :],
        )

    return on_device


def solution(mesh):
    far = mesh.shape["shard"] // 4
    split = Mesh(mesh.devices.reshape(mesh.shape["rep"], far, 2, 2), ("rep", "far", "mid", "near"))
    tokens = P(("rep", "far", "mid", "near"), None)
    weights = P(("far", "mid", "near"), None)
    return jax.shard_map(
        build(far),
        mesh=split,
        in_specs=(tokens,) * 4 + (P(),) * 4 + (weights,) * 7,
        out_specs=(tokens,) * 2 + (weights,) * 7 + (P(),) * 4,
        check_vma=False,
    )
```

time: 669 us -> 593 us (0.89)
  waiting for transfers between devices: 287 us -> 257 us
  local copies, waits for them, and re-layouts: 77.5 us -> 58.2 us
  other arithmetic: 51.6 us -> 32.6 us
  Pallas kernels: 12.3 us -> 28.4 us
  starting transfers between devices: 99.1 us -> 86.5 us
  matrix products: 114 us -> 105 us
    reduce_scatter x5 -> x4, waiting for transfers between devices: 30 us -> 1.56 us  [queue_scatter(): return lax.psum_scatter(parts, 'far', scatter_dimension=0, tiled=True)]
    all_gather x5 -> x4, waiting for transfers between devices: 60.7 us -> 39.5 us  [gather_rows(): lax.all_gather(blocks.reshape(four * rows, n), 'far', axis=0, tiled=True)]
    pallas_call x0 -> x2, Pallas kernels: none -> 19.2 us  [the longest x1 11.2 us: attention_backward(): pl.pallas_call(kernel, grid=(sequences,), in_specs=[row(proj.shape[1]), r...]
    ppermute x17, waiting for transfers between devices: 62.3 us -> 71.6 us  [over_mid(): return lax.ppermute(v, 'mid', SWAP)]
    ppermute x22 -> x21, waiting for transfers between devices: 97.3 us -> 89.2 us  [over_rep(): return lax.ppermute(v, 'rep', SWAP)]
    ppermute x9, waiting for transfers between devices: 4.47 us -> 12.4 us  [over_near(): return lax.ppermute(v, 'near', SWAP)]
    all_to_all x10 -> x8, waiting for transfers between devices: 25.3 us -> 33.2 us  [trade(): return lax.all_to_all(blocks, ('mid', 'near'), 0, 0)]
    all_to_all x10 -> x8, starting transfers between devices: 37.4 us -> 30.1 us  [trade(): return lax.all_to_all(blocks, ('mid', 'near'), 0, 0)]
  transfers between devices with their start and end apart: 73 -> 68, of which waited for: 37 -> 43; matrix products, arithmetic and copies ran while one was open for 35% -> 31% of each run, Pallas kernels for 1% -> 4%
where the time goes in v3:
time: 593 us; the launch traced here: 584 us
  waiting for transfers between devices  257 us (43%)
  matrix products  105 us (18%)
  starting transfers between devices  86.5 us (15%)
  local copies, waits for them, and re-layouts  58.2 us (10%)
  other arithmetic  32.6 us (5%)
  Pallas kernels  28.4 us (5%)
  between operations  15.8 us (3%)
    ppermute x21, waiting for transfers between devices, over_rep(): return lax.ppermute(v, 'rep', SWAP)  89.2 us
    ppermute x17, waiting for transfers between devices, over_mid(): return lax.ppermute(v, 'mid', SWAP)  71.6 us
    dot_general x10, matrix products, contract_cols(): lax.dot_general(left, right, (((1,), (1,)), ((), ())), preferred_element_...  42.6 us
    all_gather x4, waiting for transfers between devices, gather_rows(): lax.all_gather(blocks.reshape(four * rows, n), 'far', axis=0, tiled=True)  39.5 us
    dot_general x8, matrix products, dot(): return jnp.dot(left, right, preferred_element_type=F32)  36.6 us
    all_to_all x8, waiting for transfers between devices, trade(): return lax.all_to_all(blocks, ('mid', 'near'), 0, 0)  33.2 us
    ppermute x21, starting transfers between devices, over_rep(): return lax.ppermute(v, 'rep', SWAP)  31.1 us
    all_to_all x8, starting transfers between devices, trade(): return lax.all_to_all(blocks, ('mid', 'near'), 0, 0)  30.1 us
  transfers between devices with their start and end apart: 68, of which 43 were waited for; matrix products, arithmetic and copies ran while one was open for 31% of the time, Pallas kernels for 4%

profile of v3, /device:TPU:0, one launch (start us, length us, event | category | flops | bytes accessed | tf_op | source)
XLA Modules:
  0.0 583.5 jit_solution(14178536413084776)
XLA Ops:
  20.8 7.9 %all-to-all-done = bf16[4,128,768]{2,1,0:T(8,128)(2,1)S(1)} async-done(((bf16[4,128,768]{2,1,0:T(8,128)(2,1)}), bf16[4,128,768]{2,1,0:T(8,128)(2,1)S(1)}, u32[]{:S(2)}, u32[]{:S(2)}) %all-to-all-start) | async-done | bytes 786464 | tf_op jit(solution)/shard_map/all_to_all | solution.py:89
  33.8 6.1 %collective-permute-done.9 = bf16[128,2048]{1,0:T(8,128)(2,1)S(1)} collective-permute-done((bf16[128,2048]{1,0:T(8,128)(2,1)S(1)}, bf16[128,2048]{1,0:T(8,128)(2,1)S(1)}, u32[]{:S(2)}, u32[]{:S(2)}) %collective-permute-start.9) | collective-permute-done | bytes 524320 | tf_op jit(solution)/shard_map/ppermute | solution.py:24
  42.2 9.0 %collective-permute-done.1 = bf16[128,2048]{1,0:T(8,128)(2,1)S(1)} collective-permute-done((bf16[128,2048]{1,0:T(8,128)(2,1)S(1)}, bf16[128,2048]{1,0:T(8,128)(2,1)S(1)}, u32[]{:S(2)}, u32[]{:S(2)}) %collective-permute-start.1) | collective-permute-done | bytes 524320 | tf_op jit(solution)/shard_map/ppermute | solution.py:24
  74.6 9.6 %collective-permute-done.6 = s32[2,256]{1,0:T(2,128)S(1)} collective-permute-done((s32[2,256]{1,0:T(2,128)S(1)}, s32[2,256]{1,0:T(2,128)S(1)}, u32[]{:S(2)}, u32[]{:S(2)}) %collective-permute-start.6) | collective-permute-done | bytes 2080 | tf_op jit(solution)/shard_map/ppermute | solution.py:24
  98.6 5.3 fusion.16.proj_ref
  103.9 8.0 %attention_forward.1.attended_ref = bf16[1024,256]{1,0:T(8,128)(2,1)S(1)} custom-call(f32[1024,512]{1,0:T(8,128)S(1)} %fusion.16.proj_ref, f32[1024,128]{1,0:T(8,128)S(1)} %get-tuple-element.175.cosine_ref, f32[1024,128]{1,0:T(8,128)S(1)} %get-tuple-element.176.sine_ref, s32[1024,1]{1,0:T(8,128)S(1)} %copy-done.3, s32[8,1,128]{2,1,0:T(1,128)S(1)} %bitcast.41, ...), custom_call_target="tpu_custom_call" | custom-call | tf_op jit(solution)/shard_map/attention_forward/pallas_call | solution.py:229
  133.4 8.2 %collective-permute-done.14 = bf16[128,2048]{1,0:T(8,128)(2,1)} collective-permute-done((bf16[128,2048]{1,0:T(8,128)(2,1)}, bf16[128,2048]{1,0:T(8,128)(2,1)}, u32[]{:S(2)}, u32[]{:S(2)}) %collective-permute-start.14) | collective-permute-done | bytes 524320 | tf_op jit(solution)/shard_map/ppermute | solution.py:20
  155.7 5.3 collective-permute-done.17
  172.5 6.5 %collective-permute-done.19 = bf16[128,2048]{1,0:T(8,128)(2,1)} collective-permute-done((bf16[128,2048]{1,0:T(8,128)(2,1)}, bf16[128,2048]{1,0:T(8,128)(2,1)}, u32[]{:S(2)}, u32[]{:S(2)}) %collective-permute-start.19) | collective-permute-done | bytes 524320 | tf_op jit(solution)/shard_map/ppermute | solution.py:24
  201.9 5.3 fusion.3
  222.1 5.2 fusion.7
  240.3 7.7 %fusion.5 = f32[1024,2048]{1,0:T(8,128)} fusion(bf16[2048,768]{1,0:T(8,128)(2,1)} %all-gather.7.cloned.1.call-done, bf16[1024,256]{0,1:T(8,128)(2,1)} %copy-done.62, bf16[1024,256]{0,1:T(8,128)(2,1)} %copy-done.61), kind=kOutput, calls=%fused_computation.27 | convolution fusion | flops 2149580800 | bytes 11534336 | tf_op jit(solution)/shard_map/dot_general | solution.py:174
  248.1 37.7 %all-gather.11.cloned.1.call-done = bf16[2048,768]{1,0:T(8,128)(2,1)} async-done(((bf16[512,768]{1,0:T(8,128)(2,1)}), bf16[2048,768]{1,0:T(8,128)(2,1)}) %all-gather.11.cloned.1.call-update) | async-done | bytes 3145744 | tf_op jit(solution)/shard_map/all_gather | solution.py:94
  285.8 5.4 fusion.11
  291.2 5.4 multiply_convert_fusion.2
  307.6 5.1 fusion.97
  318.1 8.8 %collective-permute-done.24 = bf16[128,2048]{1,0:T(8,128)(2,1)S(1)} collective-permute-done((bf16[128,2048]{1,0:T(8,128)(2,1)S(1)}, bf16[128,2048]{1,0:T(8,128)(2,1)S(1)}, u32[]{:S(2)}, u32[]{:S(2)}) %collective-permute-start.24) | collective-permute-done | bytes 524320 | tf_op jit(solution)/shard_map/ppermute | solution.py:20
  337.8 5.9 %collective-permute-done.27 = bf16[64,2048]{1,0:T(8,128)(2,1)S(1)} collective-permute-done((bf16[64,2048]{1,0:T(8,128)(2,1)S(1)}, bf16[64,2048]{1,0:T(8,128)(2,1)S(1)}, u32[]{:S(2)}, u32[]{:S(2)}) %collective-permute-start.27) | collective-permute-done | bytes 262176 | tf_op jit(solution)/shard_map/ppermute | solution.py:20
  348.5 9.2 %collective-permute-done.29 = bf16[128,2048]{1,0:T(8,128)(2,1)S(1)} collective-permute-done((bf16[128,2048]{1,0:T(8,128)(2,1)S(1)}, bf16[128,2048]{1,0:T(8,128)(2,1)S(1)}, u32[]{:S(2)}, u32[]{:S(2)}) %collective-permute-start.29) | collective-permute-done | bytes 524320 | tf_op jit(solution)/shard_map/ppermute | solution.py:24
  371.8 11.2 %attention_backward.1 = (bf16[1024,512]{1,0:T(8,128)(2,1)S(1)}, f32[8,128]{1,0:T(8,128)S(1)}) custom-call(f32[1024,512]{1,0:T(8,128)S(1)} %fusion.16.proj_ref, f32[1024,128]{1,0:T(8,128)S(1)} %get-tuple-element.175.cosine_ref, f32[1024,128]{1,0:T(8,128)S(1)} %get-tuple-element.176.sine_ref, s32[1024,1]{1,0:T(8,128)S(1)} %copy-done.4, ...), custom_call_target="tpu_custom_call" | custom-call | tf_op jit(solution)/shard_map/attention_backward/pallas_call | solution.py:302
  396.3 12.3 %collective-permute-done.39 = bf16[128,2048]{1,0:T(8,128)(2,1)S(1)} collective-permute-done((bf16[128,2048]{1,0:T(8,128)(2,1)S(1)}, bf16[128,2048]{1,0:T(8,128)(2,1)S(1)}, u32[]{:S(2)}, u32[]{:S(2)}) %collective-permute-start.39) | collective-permute-done | bytes 524320 | tf_op jit(solution)/shard_map/ppermute | solution.py:20
  410.2 6.5 %collective-permute-done.40 = bf16[64,2048]{1,0:T(8,128)(2,1)S(1)} collective-permute-done((bf16[64,2048]{1,0:T(8,128)(2,1)S(1)}, bf16[64,2048]{1,0:T(8,128)(2,1)S(1)}, u32[]{:S(2)}, u32[]{:S(2)}) %collective-permute-start.40) | collective-permute-done | bytes 262176 | tf_op jit(solution)/shard_map/ppermute | solution.py:24
  418.6 5.3 collective-permute-done.42
  440.0 5.3 convolution_convert_fusion.6
  455.5 5.9 %convolution_convert_fusion.3 = bf16[2048,512]{1,0:T(8,128)(2,1)} fusion(bf16[1024,2048]{1,0:T(8,128)(2,1)} %constant_dynamic-update-slice_fusion.5, bf16[1024,512]{1,0:T(8,128)(2,1)S(1)} %copy-done.18), kind=kOutput, calls=%fused_computation.16 | convolution fusion | flops 2148532224 | bytes 7340032 | tf_op jit(solution)/shard_map/dot_general | solution.py:170
  461.7 5.1 all-to-all-done.4.refs_0_
  481.7 16.4 %collective-permute-done.48.refs_1_ = bf16[4,128,768]{2,1,0:T(8,128)(2,1)S(1)} collective-permute-done((bf16[4,128,768]{2,1,0:T(8,128)(2,1)S(1)}, bf16[4,128,768]{2,1,0:T(8,128)(2,1)S(1)}, u32[]{:S(2)}, u32[]{:S(2)}) %collective-permute-start.48) | collective-permute-done | bytes 786464 | tf_op jit(solution)/shard_map/ppermute | solution.py:20
  506.7 10.6 %collective-permute-done.34 = bf16[128,2048]{1,0:T(8,128)(2,1)S(1)} collective-permute-done((bf16[128,2048]{1,0:T(8,128)(2,1)S(1)}, bf16[128,2048]{1,0:T(8,128)(2,1)S(1)}, u32[]{:S(2)}, u32[]{:S(2)}) %collective-permute-start.34) | collective-permute-done | bytes 524320 | tf_op jit(solution)/shard_map/ppermute | solution.py:20
  528.3 10.5 %all-to-all-done.7.refs_4_ = bf16[4,128,1024]{2,1,0:T(8,128)(2,1)S(1)} async-done(((bf16[4,128,1024]{2,1,0:T(8,128)(2,1)}), bf16[4,128,1024]{2,1,0:T(8,128)(2,1)S(1)}, u32[]{:S(2)}, u32[]{:S(2)}) %all-to-all-start.7) | async-done | bytes 1048608 | tf_op jit(solution)/shard_map/all_to_all | solution.py:89
  546.3 6.7 %all-to-all-done.6.refs_0_ = bf16[4,128,512]{2,1,0:T(8,128)(2,1)S(1)} async-done(((bf16[4,128,512]{2,1,0:T(8,128)(2,1)}), bf16[4,128,512]{2,1,0:T(8,128)(2,1)S(1)}, u32[]{:S(2)}, u32[]{:S(2)}) %all-to-all-start.6) | async-done | bytes 524320 | tf_op jit(solution)/shard_map/all_to_all | solution.py:89
  558.1 6.9 %collective-permute-done.51.refs_5_ = bf16[4,128,1024]{2,1,0:T(8,128)(2,1)} collective-permute-done((bf16[4,128,1024]{2,1,0:T(8,128)(2,1)S(1)}, bf16[4,128,1024]{2,1,0:T(8,128)(2,1)}, u32[]{:S(2)}, u32[]{:S(2)}) %collective-permute-start.51) | collective-permute-done | bytes 1048608 | tf_op jit(solution)/shard_map/ppermute | solution.py:20
  565.0 5.8 spread.3
  (377 shorter events, 297.4 us)
Async XLA Ops:
  12.2 16.6 %all-to-all-start = ((bf16[4,128,768]{2,1,0:T(8,128)(2,1)}), bf16[4,128,768]{2,1,0:T(8,128)(2,1)S(1)}, u32[]{:S(2)}, u32[]{:S(2)}) async-start(bf16[4,128,768]{2,1,0:T(8,128)(2,1)} %pick_columns.2), calls=%async_computation | async-start | bytes 1572864 | tf_op jit(solution)/shard_map/all_to_all | solution.py:89
  16.4 82.2 %all-gather.5.cloned.1.call-start = ((), (), s32[]{:S(2)}) async-start(), calls=%async_computation.12 | async-start | bytes 3932160 | tf_op jit(solution)/shard_map/all_gather | solution.py:94
  16.4 23.6 %collective-permute-start.9 = (bf16[128,2048]{1,0:T(8,128)(2,1)S(1)}, bf16[128,2048]{1,0:T(8,128)(2,1)S(1)}, u32[]{:S(2)}, u32[]{:S(2)}) collective-permute-start(bf16[128,2048]{1,0:T(8,128)(2,1)S(1)} %copy-done.34), channel_id=1, source_target_pairs={{0,2},{2,0},{1,3},{3,1},{4,6},{6,4},{5,7},{7,5},{8,10},{10,8},{9,1... | collective-permute-start | bytes 1572872 | tf_op jit(solution)/shard_map/ppermute | solution.py:24
  18.7 23.3 %collective-permute-start.8 = (bf16[128,2048]{1,0:T(8,128)(2,1)S(1)}, bf16[128,2048]{1,0:T(8,128)(2,1)S(1)}, u32[]{:S(2)}, u32[]{:S(2)}) collective-permute-start(bf16[128,2048]{1,0:T(8,128)(2,1)S(1)} %copy-done.34), channel_id=1, source_target_pairs={{0,16},{16,0},{1,17},{17,1},{2,18},{18,2},{3,19},{19,3},{4,20},{20... | collective-permute-start | bytes 1572872 | tf_op jit(solution)/shard_map/ppermute | solution.py:20
  30.6 20.6 %collective-permute-start.1 = (bf16[128,2048]{1,0:T(8,128)(2,1)S(1)}, bf16[128,2048]{1,0:T(8,128)(2,1)S(1)}, u32[]{:S(2)}, u32[]{:S(2)}) collective-permute-start(bf16[128,2048]{1,0:T(8,128)(2,1)S(1)} %get-tuple-element.80), channel_id=1, source_target_pairs={{0,2},{2,0},{1,3},{3,1},{4,6},{6,4},{5,7},{7,5},{8,10},{10,8},{9,1... | collective-permute-start | bytes 1572872 | tf_op jit(solution)/shard_map/ppermute | solution.py:24
  30.6 22.6 %collective-permute-start = (bf16[128,2048]{1,0:T(8,128)(2,1)S(1)}, bf16[128,2048]{1,0:T(8,128)(2,1)S(1)}, u32[]{:S(2)}, u32[]{:S(2)}) collective-permute-start(bf16[128,2048]{1,0:T(8,128)(2,1)S(1)} %get-tuple-element.80), channel_id=1, source_target_pairs={{0,16},{16,0},{1,17},{17,1},{2,18},{18,2},{3,19},{19,3},{4,20},{20... | collective-permute-start | bytes 1572872 | tf_op jit(solution)/shard_map/ppermute | solution.py:20
  40.0 24.2 %collective-permute-start.11 = (bf16[64,2048]{1,0:T(8,128)(2,1)S(1)}, bf16[64,2048]{1,0:T(8,128)(2,1)S(1)}, u32[]{:S(2)}, u32[]{:S(2)}) collective-permute-start(bf16[64,2048]{1,0:T(8,128)(2,1)S(1)} %slice.455), channel_id=1, source_target_pairs={{0,16},{16,0},{1,17},{17,1},{2,18},{18,2},{3,19},{19,3},{4,20},{20... | collective-permute-start | bytes 786440 | tf_op jit(solution)/shard_map/ppermute | solution.py:20
  42.0 21.2 %collective-permute-start.10 = (bf16[64,2048]{1,0:T(8,128)(2,1)S(1)}, bf16[64,2048]{1,0:T(8,128)(2,1)S(1)}, u32[]{:S(2)}, u32[]{:S(2)}) collective-permute-start(bf16[64,2048]{1,0:T(8,128)(2,1)S(1)} %slice.454), channel_id=1, source_target_pairs={{0,2},{2,0},{1,3},{3,1},{4,6},{6,4},{5,7},{7,5},{8,10},{10,8},{9,1... | collective-permute-start | bytes 786440 | tf_op jit(solution)/shard_map/ppermute | solution.py:24
  63.3 29.0 %collective-permute-start.4 = (bf16[512,2048]{1,0:T(8,128)(2,1)}, bf16[512,2048]{1,0:T(8,128)(2,1)}, u32[]{:S(2)}, u32[]{:S(2)}) collective-permute-start(bf16[512,2048]{1,0:T(8,128)(2,1)} %get-tuple-element.146), channel_id=1, source_target_pairs={{0,1},{1,0},{2,3},{3,2},{4,5},{5,4},{6,7},{7,6},{8,9},{9,8},{10,11... | collective-permute-start | bytes 6291464 | tf_op jit(solution)/shard_map/ppermute | solution.py:28
  65.6 29.8 %collective-permute-start.12 = (bf16[512,2048]{1,0:T(8,128)(2,1)}, bf16[512,2048]{1,0:T(8,128)(2,1)}, u32[]{:S(2)}, u32[]{:S(2)}) collective-permute-start(bf16[512,2048]{1,0:T(8,128)(2,1)} %get-tuple-element.142), channel_id=1, source_target_pairs={{0,1},{1,0},{2,3},{3,2},{4,5},{5,4},{6,7},{7,6},{8,9},{9,8},{10,11... | collective-permute-start | bytes 6291464 | tf_op jit(solution)/shard_map/ppermute | solution.py:28
  69.0 22.3 %all-to-all-start.2 = ((bf16[4,128,768]{2,1,0:T(8,128)(2,1)}), bf16[4,128,768]{2,1,0:T(8,128)(2,1)S(1)}, u32[]{:S(2)}, u32[]{:S(2)}) async-start(bf16[4,128,768]{2,1,0:T(8,128)(2,1)} %get-tuple-element.43), calls=%async_computation.2 | async-start | bytes 1572864 | tf_op jit(solution)/shard_map/all_to_all | solution.py:89
  72.5 129.4 %all-gather.9.cloned.1.call-start = ((), (), s32[]{:S(2)}) async-start(), calls=%async_computation.14 | async-start | bytes 3932160 | tf_op jit(solution)/shard_map/all_gather | solution.py:94
  116.0 15.9 %all-to-all-start.1 = ((bf16[4,128,768]{2,1,0:T(8,128)(2,1)}), bf16[4,128,768]{2,1,0:T(8,128)(2,1)}, u32[]{:S(2)}, u32[]{:S(2)}) async-start(bf16[4,128,768]{2,1,0:T(8,128)(2,1)} %copy-done.8), calls=%async_computation.1 | async-start | bytes 1572864 | tf_op jit(solution)/shard_map/all_to_all | solution.py:89
  120.2 101.9 %all-gather.7.cloned.1.call-start = ((), (), s32[]{:S(2)}) async-start(), calls=%async_computation.13 | async-start | bytes 3932160 | tf_op jit(solution)/shard_map/all_gather | solution.py:94
  165.4 17.0 %collective-permute-start.18 = (bf16[128,2048]{1,0:T(8,128)(2,1)}, bf16[128,2048]{1,0:T(8,128)(2,1)}, u32[]{:S(2)}, u32[]{:S(2)}) collective-permute-start(bf16[128,2048]{1,0:T(8,128)(2,1)} %get-tuple-element.76), channel_id=1, source_target_pairs={{0,16},{16,0},{1,17},{17,1},{2,18},{18,2},{3,19},{19,3},{4,20},{20... | collective-permute-start | bytes 1572872 | tf_op jit(solution)/shard_map/ppermute | solution.py:20
  167.1 27.1 %all-to-all-start.3 = ((bf16[4,128,768]{2,1,0:T(8,128)(2,1)}), bf16[4,128,768]{2,1,0:T(8,128)(2,1)}, u32[]{:S(2)}, u32[]{:S(2)}) async-start(bf16[4,128,768]{2,1,0:T(8,128)(2,1)} %copy-done.7), calls=%async_computation.3 | async-start | bytes 1572864 | tf_op jit(solution)/shard_map/all_to_all | solution.py:89
  171.3 114.4 %all-gather.11.cloned.1.call-start = ((), (), s32[]{:S(2)}) async-start(), calls=%async_computation.15 | async-start | bytes 3932160 | tf_op jit(solution)/shard_map/all_gather | solution.py:94
  194.3 237.8 %reduce-scatter.7.cloned.1.call-start = ((), (), s32[]{:S(2)}) async-start(), calls=%async_computation.17 | async-start | bytes 3932160 | tf_op jit(solution)/shard_map/reduce_scatter | solution.py:98
  219.8 225.4 %reduce-scatter.5.cloned.1.call-start = ((), (), s32[]{:S(2)}) async-start(), calls=%async_computation.16 | async-start | bytes 3932160 | tf_op jit(solution)/shard_map/reduce_scatter | solution.py:98
  303.1 195.8 %reduce-scatter.9.cloned.1.call-start = ((), (), s32[]{:S(2)}) async-start(), calls=%async_computation.18 | async-start | bytes 5242880 | tf_op jit(solution)/shard_map/reduce_scatter | solution.py:98
  316.6 15.1 %collective-permute-start.26 = (bf16[128,2048]{1,0:T(8,128)(2,1)S(1)}, bf16[128,2048]{1,0:T(8,128)(2,1)S(1)}, u32[]{:S(2)}, u32[]{:S(2)}) collective-permute-start(bf16[128,2048]{1,0:T(8,128)(2,1)S(1)} %pad_maximum_fusion.25), channel_id=1, source_target_pairs={{0,2},{2,0},{1,3},{3,1},{4,6},{6,4},{5,7},{7,5},{8,10},{10,8},{9,1... | collective-permute-start | bytes 1572872 | tf_op jit(solution)/shard_map/ppermute | solution.py:24
  434.4 17.2 %all-to-all-start.5 = ((bf16[4,128,768]{2,1,0:T(8,128)(2,1)}), bf16[4,128,768]{2,1,0:T(8,128)(2,1)S(1)}, u32[]{:S(2)}, u32[]{:S(2)}) async-start(bf16[4,128,768]{2,1,0:T(8,128)(2,1)} %bitcast.13), calls=%async_computation.7 | async-start | bytes 1572864 | tf_op jit(solution)/shard_map/all_to_all | solution.py:89
  445.3 53.7 %collective-permute-start.33 = (bf16[512,2048]{1,0:T(8,128)(2,1)}, bf16[512,2048]{1,0:T(8,128)(2,1)}, u32[]{:S(2)}, u32[]{:S(2)}) collective-permute-start(bf16[512,2048]{1,0:T(8,128)(2,1)} %convolution_convert_fusion.6), channel_id=1, source_target_pairs={{0,1},{1,0},{2,3},{3,2},{4,5},{5,4},{6,7},{7,6},{8,9},{9,8},{10,11... | collective-permute-start | bytes 6291464 | tf_op jit(solution)/shard_map/ppermute | solution.py:28
  449.9 17.2 %collective-permute-start.45 = (f32[1,4352]{1,0:T(1,128)S(1)}, f32[1,4352]{1,0:T(1,128)S(1)}, u32[]{:S(2)}, u32[]{:S(2)}) collective-permute-start(f32[1,4352]{1,0:T(1,128)S(1)} %add.205), channel_id=1, source_target_pairs={{0,16},{16,0},{1,17},{17,1},{2,18},{18,2},{3,19},{19,3},{4,20},{20... | collective-permute-start | bytes 52232 | tf_op jit(solution)/shard_map/ppermute | solution.py:136
  455.2 85.6 %reduce-scatter.11.cloned.1.call-start = ((), (), s32[]{:S(2)}) async-start(), calls=%async_computation.19 | async-start | bytes 2621440 | tf_op jit(solution)/shard_map/reduce_scatter | solution.py:98
  461.4 20.3 %collective-permute-start.49 = (bf16[4,128,768]{2,1,0:T(8,128)(2,1)S(1)}, bf16[4,128,768]{2,1,0:T(8,128)(2,1)S(1)}, u32[]{:S(2)}, u32[]{:S(2)}) collective-permute-start(bf16[4,128,768]{2,1,0:T(8,128)(2,1)S(1)} %all-to-all-done.5.refs_2_), channel_id=1, source_target_pairs={{0,16},{16,0},{1,17},{17,1},{2,18},{18,2},{3,19},{19,3},{4,20},{20... | collective-permute-start | bytes 2359304 | tf_op jit(solution)/shard_map/ppermute | solution.py:20
  466.8 31.3 %collective-permute-start.48 = (bf16[4,128,768]{2,1,0:T(8,128)(2,1)S(1)}, bf16[4,128,768]{2,1,0:T(8,128)(2,1)S(1)}, u32[]{:S(2)}, u32[]{:S(2)}) collective-permute-start(bf16[4,128,768]{2,1,0:T(8,128)(2,1)S(1)} %all-to-all-done.4.refs_0_), channel_id=1, source_target_pairs={{0,16},{16,0},{1,17},{17,1},{2,18},{18,2},{3,19},{19,3},{4,20},{20... | collective-permute-start | bytes 2359304 | tf_op jit(solution)/shard_map/ppermute | solution.py:20
  505.1 19.3 %collective-permute-start.36 = (bf16[128,2048]{1,0:T(8,128)(2,1)}, bf16[128,2048]{1,0:T(8,128)(2,1)}, u32[]{:S(2)}, u32[]{:S(2)}) collective-permute-start(bf16[128,2048]{1,0:T(8,128)(2,1)} %pad_maximum_fusion.27), channel_id=1, source_target_pairs={{0,2},{2,0},{1,3},{3,1},{4,6},{6,4},{5,7},{7,5},{8,10},{10,8},{9,1... | collective-permute-start | bytes 1572872 | tf_op jit(solution)/shard_map/ppermute | solution.py:24
  520.9 18.0 %all-to-all-start.7 = ((bf16[4,128,1024]{2,1,0:T(8,128)(2,1)}), bf16[4,128,1024]{2,1,0:T(8,128)(2,1)S(1)}, u32[]{:S(2)}, u32[]{:S(2)}) async-start(bf16[4,128,1024]{2,1,0:T(8,128)(2,1)} %bitcast.49), calls=%async_computation.11 | async-start | bytes 2097152 | tf_op jit(solution)/shard_map/all_to_all | solution.py:89
  528.0 16.3 %collective-permute-start.37 = (bf16[64,2048]{1,0:T(8,128)(2,1)S(1)}, bf16[64,2048]{1,0:T(8,128)(2,1)}, u32[]{:S(2)}, u32[]{:S(2)}) collective-permute-start(bf16[64,2048]{1,0:T(8,128)(2,1)S(1)} %get-tuple-element.84), channel_id=1, source_target_pairs={{0,16},{16,0},{1,17},{17,1},{2,18},{18,2},{3,19},{19,3},{4,20},{20... | collective-permute-start | bytes 786440 | tf_op jit(solution)/shard_map/ppermute | solution.py:20
  538.8 26.2 %collective-permute-start.51 = (bf16[4,128,1024]{2,1,0:T(8,128)(2,1)S(1)}, bf16[4,128,1024]{2,1,0:T(8,128)(2,1)}, u32[]{:S(2)}, u32[]{:S(2)}) collective-permute-start(bf16[4,128,1024]{2,1,0:T(8,128)(2,1)S(1)} %all-to-all-done.7.refs_4_), channel_id=1, source_target_pairs={{0,16},{16,0},{1,17},{17,1},{2,18},{18,2},{3,19},{19,3},{4,20},{20... | collective-permute-start | bytes 3145736 | tf_op jit(solution)/shard_map/ppermute | solution.py:20
  553.1 21.8 %collective-permute-start.50 = (bf16[4,128,512]{2,1,0:T(8,128)(2,1)S(1)}, bf16[4,128,512]{2,1,0:T(8,128)(2,1)S(1)}, u32[]{:S(2)}, u32[]{:S(2)}) collective-permute-start(bf16[4,128,512]{2,1,0:T(8,128)(2,1)S(1)} %all-to-all-done.6.refs_0_), channel_id=1, source_target_pairs={{0,16},{16,0},{1,17},{17,1},{2,18},{18,2},{3,19},{19,3},{4,20},{20... | collective-permute-start | bytes 1572872 | tf_op jit(solution)/shard_map/ppermute | solution.py:20
  (101 other events, 796.5 us)
Sparse Core Ops, SparseCore 0:
  29.8 64.2 all-gather.4
  96.2 62.1 all-gather.8
  160.0 62.1 all-gather.6
  223.6 62.1 all-gather.10
  288.5 58.8 reduce-scatter.6
  350.2 60.2 reduce-scatter.4
  412.8 77.5 reduce-scatter.8
  499.1 41.5 reduce-scatter.10

commit v4 on v3

--- a/solution.py
+++ b/solution.py
@@ -351,12 +351,18 @@
         (attn_slot,) = pick_columns(
             [[(w_q, 0, q_n), (key_matrix, 0, k_n), (value_matrix, 0, k_n), (w_o, 0, o_n)]]
         )
-        mlp_slots = pick_columns([[(w, start, n) for w in (w_gate, w_up, w_down)] for start, n in chunks])
+        mlp_slots = pick_columns(
+            [[(w, start, n) for start, n in part for w in (w_gate, w_up, w_down)] for part in (chunks[:-1], chunks[-1:]) if part]
+        )
         inputs = block_input.astype(F32)
         recip_attn = lax.rsqrt(jnp.mean(inputs * inputs, -1, keepdims=True) + EPSILON)
         normed_own = (inputs * recip_attn * attn_gain).astype(BF16)
         traded = [trade(slot) for slot in (attn_slot, *mlp_slots)]
-        attn_weights, *mlp_weights = [gather_rows(v) for v in traded]
+        attn_weights, *gathered = [gather_rows(v) for v in traded]
+        mlp_weights = []
+        for part in gathered:
+            step = 3 * chunks[0][1]
+            mlp_weights += [part[:, at : at + step] for at in range(0, part.shape[1], step)]
         qkv, w_o_cols = attn_weights[:, : q_n + 2 * k_n], attn_weights[:, q_n + 2 * k_n :]
 
         normed_rows = plane_gather(normed_own)
@@ -381,7 +387,7 @@
         for number, three in enumerate(mlp_weights):
             block = chunks[number][1]
             if number == 2:
-                grad_top, owns[0] = after(grad_top, owns[0])
+                three, owns[0] = after(three, owns[0])
             weight = three[:, : 2 * block]
             pre = dot(mlp_in, weight)
             gate_pre, up_pre = pre[:, :block], pre[:, block:]

time: 593 us -> 589 us (level)
  waiting for transfers between devices: 257 us -> 280 us
  matrix products: 105 us -> 94.7 us
  starting transfers between devices: 86.5 us -> 78.9 us
    ppermute x17, waiting for transfers between devices: 71.6 us -> 82.3 us  [over_mid(): return lax.ppermute(v, 'mid', SWAP)]
    dot_general x10, matrix products: 42.6 us -> 34.6 us  [contract_cols(): lax.dot_general(left, right, (((1,), (1,)), ((), ())), preferred_element_...]
    all_gather x4 -> x3, waiting for transfers between devices: 39.5 us -> 47 us  [gather_rows(): lax.all_gather(blocks.reshape(four * rows, n), 'far', axis=0, tiled=True)]
    all_to_all x8 -> x7, starting transfers between devices: 30.1 us -> 26 us  [trade(): return lax.all_to_all(blocks, ('mid', 'near'), 0, 0)]
    all_to_all x8 -> x7, waiting for transfers between devices: 33.2 us -> 30.4 us  [trade(): return lax.all_to_all(blocks, ('mid', 'near'), 0, 0)]
    unnamed x147 -> x143, local copies, waits for them, and re-layouts: 27.6 us -> 25.8 us
  transfers between devices with their start and end apart: 68 -> 66, of which waited for: 43 -> 40; matrix products, arithmetic and copies ran while one was open for 31% -> 28% of each run, Pallas kernels for 4% -> 5%
where the time goes in v4:
time: 589 us; the launch traced here: 579 us
  waiting for transfers between devices  280 us (48%)
  matrix products  94.7 us (16%)
  starting transfers between devices  78.9 us (13%)
  local copies, waits for them, and re-layouts  54.2 us (9%)
  Pallas kernels  28.7 us (5%)
  other arithmetic  27.3 us (5%)
  between operations  15.8 us (3%)
    ppermute x21, waiting for transfers between devices, over_rep(): return lax.ppermute(v, 'rep', SWAP)  94 us
    ppermute x17, waiting for transfers between devices, over_mid(): return lax.ppermute(v, 'mid', SWAP)  82.3 us
    all_gather x3, waiting for transfers between devices, gather_rows(): lax.all_gather(blocks.reshape(four * rows, n), 'far', axis=0, tiled=True)  47 us
    dot_general x10, matrix products, contract_cols(): lax.dot_general(left, right, (((1,), (1,)), ((), ())), preferred_element_...  34.6 us
    dot_general x8, matrix products, dot(): return jnp.dot(left, right, preferred_element_type=F32)  34.2 us
    all_to_all x7, waiting for transfers between devices, trade(): return lax.all_to_all(blocks, ('mid', 'near'), 0, 0)  30.4 us
    ppermute x21, starting transfers between devices, over_rep(): return lax.ppermute(v, 'rep', SWAP)  28.8 us
    all_to_all x7, starting transfers between devices, trade(): return lax.all_to_all(blocks, ('mid', 'near'), 0, 0)  26 us
  transfers between devices with their start and end apart: 66, of which 40 were waited for; matrix products, arithmetic and copies ran while one was open for 28% of the time, Pallas kernels for 5%

profile of v4, /device:TPU:0, one launch (start us, length us, event | category | flops | bytes accessed | tf_op | source)
XLA Modules:
  0.0 579.4 jit_solution(10591507970730406397)
XLA Ops:
  20.8 7.9 %all-to-all-done = bf16[4,128,768]{2,1,0:T(8,128)(2,1)S(1)} async-done(((bf16[4,128,768]{2,1,0:T(8,128)(2,1)}), bf16[4,128,768]{2,1,0:T(8,128)(2,1)S(1)}, u32[]{:S(2)}, u32[]{:S(2)}) %all-to-all-start) | async-done | bytes 786464 | tf_op jit(solution)/shard_map/all_to_all | solution.py:89
  33.9 6.1 %collective-permute-done.9 = bf16[128,2048]{1,0:T(8,128)(2,1)S(1)} collective-permute-done((bf16[128,2048]{1,0:T(8,128)(2,1)S(1)}, bf16[128,2048]{1,0:T(8,128)(2,1)S(1)}, u32[]{:S(2)}, u32[]{:S(2)}) %collective-permute-start.9) | collective-permute-done | bytes 524320 | tf_op jit(solution)/shard_map/ppermute | solution.py:24
  42.2 9.0 %collective-permute-done.1 = bf16[128,2048]{1,0:T(8,128)(2,1)S(1)} collective-permute-done((bf16[128,2048]{1,0:T(8,128)(2,1)S(1)}, bf16[128,2048]{1,0:T(8,128)(2,1)S(1)}, u32[]{:S(2)}, u32[]{:S(2)}) %collective-permute-start.1) | collective-permute-done | bytes 524320 | tf_op jit(solution)/shard_map/ppermute | solution.py:24
  74.1 18.0 %collective-permute-done.6 = s32[2,256]{1,0:T(2,128)S(1)} collective-permute-done((s32[2,256]{1,0:T(2,128)S(1)}, s32[2,256]{1,0:T(2,128)S(1)}, u32[]{:S(2)}, u32[]{:S(2)}) %collective-permute-start.6) | collective-permute-done | bytes 2080 | tf_op jit(solution)/shard_map/ppermute | solution.py:24
  106.8 6.0 %fusion.12.proj_ref = f32[1024,512]{1,0:T(8,128)S(1)} fusion(bf16[1024,2048]{1,0:T(8,128)(2,1)} %constant_dynamic-update-slice_fusion.5, bf16[2048,768]{1,0:T(8,128)(2,1)} %all-gather.4.cloned.1.call-done), kind=kOutput, calls=%fused_computation.34 | convolution fusion | flops 2147483648 | bytes 8388608 | tf_op jit(solution)/shard_map/dot_general | solution.py:166
  112.8 8.0 %attention_forward.1.attended_ref = bf16[1024,256]{1,0:T(8,128)(2,1)S(1)} custom-call(f32[1024,512]{1,0:T(8,128)S(1)} %fusion.12.proj_ref, f32[1024,128]{1,0:T(8,128)S(1)} %get-tuple-element.175.cosine_ref, f32[1024,128]{1,0:T(8,128)S(1)} %get-tuple-element.176.sine_ref, s32[1024,1]{1,0:T(8,128)S(1)} %copy-done.3, s32[8,1,128]{2,1,0:T(1,128)S(1)} %bitcast.40, ...), custom_call_target="tpu_custom_call" | custom-call | tf_op jit(solution)/shard_map/attention_forward/pallas_call | solution.py:229
  128.9 12.1 %collective-permute-done.14 = bf16[128,2048]{1,0:T(8,128)(2,1)S(1)} collective-permute-done((bf16[128,2048]{1,0:T(8,128)(2,1)S(1)}, bf16[128,2048]{1,0:T(8,128)(2,1)S(1)}, u32[]{:S(2)}, u32[]{:S(2)}) %collective-permute-start.14) | collective-permute-done | bytes 524320 | tf_op jit(solution)/shard_map/ppermute | solution.py:20
  142.6 6.5 %collective-permute-done.15 = bf16[64,2048]{1,0:T(8,128)(2,1)S(1)} collective-permute-done((bf16[64,2048]{1,0:T(8,128)(2,1)S(1)}, bf16[64,2048]{1,0:T(8,128)(2,1)S(1)}, u32[]{:S(2)}, u32[]{:S(2)}) %collective-permute-start.15) | collective-permute-done | bytes 262176 | tf_op jit(solution)/shard_map/ppermute | solution.py:24
  150.8 5.7 collective-permute-done.17
  165.9 8.2 %collective-permute-done.19 = bf16[128,2048]{1,0:T(8,128)(2,1)} collective-permute-done((bf16[128,2048]{1,0:T(8,128)(2,1)}, bf16[128,2048]{1,0:T(8,128)(2,1)}, u32[]{:S(2)}, u32[]{:S(2)}) %collective-permute-start.19) | collective-permute-done | bytes 524320 | tf_op jit(solution)/shard_map/ppermute | solution.py:24
  196.5 20.3 %all-gather.6.cloned.1.call-done = bf16[2048,1536]{1,0:T(8,128)(2,1)} async-done(((bf16[512,1536]{1,0:T(8,128)(2,1)}), bf16[2048,1536]{1,0:T(8,128)(2,1)}) %all-gather.6.cloned.1.call-update) | async-done | bytes 6291472 | tf_op jit(solution)/shard_map/all_gather | solution.py:94
  216.7 5.2 fusion.3
  235.5 5.2 fusion.7
  253.4 26.7 %all-gather.8.cloned.1.call-done = bf16[2048,768]{1,0:T(8,128)(2,1)} async-done(((bf16[512,768]{1,0:T(8,128)(2,1)}), bf16[2048,768]{1,0:T(8,128)(2,1)}) %all-gather.8.cloned.1.call-update) | async-done | bytes 3145744 | tf_op jit(solution)/shard_map/all_gather | solution.py:94
  287.0 5.3 multiply_convert_fusion.2
  305.3 5.1 fusion.98
  316.2 8.3 %collective-permute-done.24 = bf16[128,2048]{1,0:T(8,128)(2,1)S(1)} collective-permute-done((bf16[128,2048]{1,0:T(8,128)(2,1)S(1)}, bf16[128,2048]{1,0:T(8,128)(2,1)S(1)}, u32[]{:S(2)}, u32[]{:S(2)}) %collective-permute-start.24) | collective-permute-done | bytes 524320 | tf_op jit(solution)/shard_map/ppermute | solution.py:20
  335.9 5.7 collective-permute-done.27
  346.6 8.9 %collective-permute-done.29 = bf16[128,2048]{1,0:T(8,128)(2,1)S(1)} collective-permute-done((bf16[128,2048]{1,0:T(8,128)(2,1)S(1)}, bf16[128,2048]{1,0:T(8,128)(2,1)S(1)}, u32[]{:S(2)}, u32[]{:S(2)}) %collective-permute-start.29) | collective-permute-done | bytes 524320 | tf_op jit(solution)/shard_map/ppermute | solution.py:24
  369.7 11.2 %attention_backward.1 = (bf16[1024,512]{1,0:T(8,128)(2,1)S(1)}, f32[8,128]{1,0:T(8,128)S(1)}) custom-call(f32[1024,512]{1,0:T(8,128)S(1)} %fusion.12.proj_ref, f32[1024,128]{1,0:T(8,128)S(1)} %get-tuple-element.175.cosine_ref, f32[1024,128]{1,0:T(8,128)S(1)} %get-tuple-element.176.sine_ref, s32[1024,1]{1,0:T(8,128)S(1)} %copy-done.4, ...), custom_call_target="tpu_custom_call" | custom-call | tf_op jit(solution)/shard_map/attention_backward/pallas_call | solution.py:302
  394.2 12.3 %collective-permute-done.39 = bf16[128,2048]{1,0:T(8,128)(2,1)S(1)} collective-permute-done((bf16[128,2048]{1,0:T(8,128)(2,1)S(1)}, bf16[128,2048]{1,0:T(8,128)(2,1)S(1)}, u32[]{:S(2)}, u32[]{:S(2)}) %collective-permute-start.39) | collective-permute-done | bytes 524320 | tf_op jit(solution)/shard_map/ppermute | solution.py:20
  408.1 6.3 %collective-permute-done.40 = bf16[64,2048]{1,0:T(8,128)(2,1)S(1)} collective-permute-done((bf16[64,2048]{1,0:T(8,128)(2,1)S(1)}, bf16[64,2048]{1,0:T(8,128)(2,1)S(1)}, u32[]{:S(2)}, u32[]{:S(2)}) %collective-permute-start.40) | collective-permute-done | bytes 262176 | tf_op jit(solution)/shard_map/ppermute | solution.py:24
  416.4 5.1 collective-permute-done.42
  435.7 5.3 convolution_convert_fusion.6
  451.2 5.9 %convolution_convert_fusion.3 = bf16[2048,512]{1,0:T(8,128)(2,1)} fusion(bf16[1024,2048]{1,0:T(8,128)(2,1)} %constant_dynamic-update-slice_fusion.5, bf16[1024,512]{1,0:T(8,128)(2,1)S(1)} %copy-done.17), kind=kOutput, calls=%fused_computation.16 | convolution fusion | flops 2148532224 | bytes 7340032 | tf_op jit(solution)/shard_map/dot_general | solution.py:170
  457.4 5.1 all-to-all-done.3.refs_0_
  477.4 16.4 %collective-permute-done.48.refs_1_ = bf16[4,128,768]{2,1,0:T(8,128)(2,1)S(1)} collective-permute-done((bf16[4,128,768]{2,1,0:T(8,128)(2,1)S(1)}, bf16[4,128,768]{2,1,0:T(8,128)(2,1)S(1)}, u32[]{:S(2)}, u32[]{:S(2)}) %collective-permute-start.48) | collective-permute-done | bytes 786464 | tf_op jit(solution)/shard_map/ppermute | solution.py:20
  502.4 10.7 %collective-permute-done.34 = bf16[128,2048]{1,0:T(8,128)(2,1)S(1)} collective-permute-done((bf16[128,2048]{1,0:T(8,128)(2,1)S(1)}, bf16[128,2048]{1,0:T(8,128)(2,1)S(1)}, u32[]{:S(2)}, u32[]{:S(2)}) %collective-permute-start.34) | collective-permute-done | bytes 524320 | tf_op jit(solution)/shard_map/ppermute | solution.py:20
  524.1 10.6 %all-to-all-done.6.refs_4_ = bf16[4,128,1024]{2,1,0:T(8,128)(2,1)S(1)} async-done(((bf16[4,128,1024]{2,1,0:T(8,128)(2,1)}), bf16[4,128,1024]{2,1,0:T(8,128)(2,1)S(1)}, u32[]{:S(2)}, u32[]{:S(2)}) %all-to-all-start.6) | async-done | bytes 1048608 | tf_op jit(solution)/shard_map/all_to_all | solution.py:89
  542.1 6.7 %all-to-all-done.5.refs_0_ = bf16[4,128,512]{2,1,0:T(8,128)(2,1)S(1)} async-done(((bf16[4,128,512]{2,1,0:T(8,128)(2,1)}), bf16[4,128,512]{2,1,0:T(8,128)(2,1)S(1)}, u32[]{:S(2)}, u32[]{:S(2)}) %all-to-all-start.5) | async-done | bytes 524320 | tf_op jit(solution)/shard_map/all_to_all | solution.py:89
  553.8 7.0 %collective-permute-done.51.refs_5_ = bf16[4,128,1024]{2,1,0:T(8,128)(2,1)} collective-permute-done((bf16[4,128,1024]{2,1,0:T(8,128)(2,1)S(1)}, bf16[4,128,1024]{2,1,0:T(8,128)(2,1)}, u32[]{:S(2)}, u32[]{:S(2)}) %collective-permute-start.51) | collective-permute-done | bytes 1048608 | tf_op jit(solution)/shard_map/ppermute | solution.py:20
  560.8 5.8 %spread.3 = (f32[128,6144]{1,0:T(8,128)}, f32[128,6144]{1,0:T(8,128)}, f32[128,6144]{1,0:T(8,128)}, f32[128,2048]{1,0:T(8,128)}) custom-call(s32[1]{0:T(128)} %bitcast.side_ref, bf16[4,128,768]{2,1,0:T(8,128)(2,1)S(1)} %all-to-all-done.3.refs_0_, bf16[4,128,768]{2,1,0:T(8,128)(2,1)S(1)} %copy-done.11, bf16[4,128,768]{2,1,0:T(8,128)(2,1)S(1)} %all-to-all-done.4.refs_2_, ...), custom_call_target="tpu_custom_call" | custom-call | tf_op jit(solution)/shard_map/spread/pallas_call | solution.py:124
  (366 shorter events, 276.8 us)
Async XLA Ops:
  12.2 16.6 %all-to-all-start = ((bf16[4,128,768]{2,1,0:T(8,128)(2,1)}), bf16[4,128,768]{2,1,0:T(8,128)(2,1)S(1)}, u32[]{:S(2)}, u32[]{:S(2)}) async-start(bf16[4,128,768]{2,1,0:T(8,128)(2,1)} %pick_columns.2), calls=%async_computation | async-start | bytes 1572864 | tf_op jit(solution)/shard_map/all_to_all | solution.py:89
  16.4 90.4 %all-gather.4.cloned.1.call-start = ((), (), s32[]{:S(2)}) async-start(), calls=%async_computation.11 | async-start | bytes 3932160 | tf_op jit(solution)/shard_map/all_gather | solution.py:94
  16.4 23.6 %collective-permute-start.9 = (bf16[128,2048]{1,0:T(8,128)(2,1)S(1)}, bf16[128,2048]{1,0:T(8,128)(2,1)S(1)}, u32[]{:S(2)}, u32[]{:S(2)}) collective-permute-start(bf16[128,2048]{1,0:T(8,128)(2,1)S(1)} %copy-done.33), channel_id=1, source_target_pairs={{0,2},{2,0},{1,3},{3,1},{4,6},{6,4},{5,7},{7,5},{8,10},{10,8},{9,1... | collective-permute-start | bytes 1572872 | tf_op jit(solution)/shard_map/ppermute | solution.py:24
  18.7 23.3 %collective-permute-start.8 = (bf16[128,2048]{1,0:T(8,128)(2,1)S(1)}, bf16[128,2048]{1,0:T(8,128)(2,1)S(1)}, u32[]{:S(2)}, u32[]{:S(2)}) collective-permute-start(bf16[128,2048]{1,0:T(8,128)(2,1)S(1)} %copy-done.33), channel_id=1, source_target_pairs={{0,16},{16,0},{1,17},{17,1},{2,18},{18,2},{3,19},{19,3},{4,20},{20... | collective-permute-start | bytes 1572872 | tf_op jit(solution)/shard_map/ppermute | solution.py:20
  30.6 20.6 %collective-permute-start.1 = (bf16[128,2048]{1,0:T(8,128)(2,1)S(1)}, bf16[128,2048]{1,0:T(8,128)(2,1)S(1)}, u32[]{:S(2)}, u32[]{:S(2)}) collective-permute-start(bf16[128,2048]{1,0:T(8,128)(2,1)S(1)} %get-tuple-element.78), channel_id=1, source_target_pairs={{0,2},{2,0},{1,3},{3,1},{4,6},{6,4},{5,7},{7,5},{8,10},{10,8},{9,1... | collective-permute-start | bytes 1572872 | tf_op jit(solution)/shard_map/ppermute | solution.py:24
  30.6 22.6 %collective-permute-start = (bf16[128,2048]{1,0:T(8,128)(2,1)S(1)}, bf16[128,2048]{1,0:T(8,128)(2,1)S(1)}, u32[]{:S(2)}, u32[]{:S(2)}) collective-permute-start(bf16[128,2048]{1,0:T(8,128)(2,1)S(1)} %get-tuple-element.78), channel_id=1, source_target_pairs={{0,16},{16,0},{1,17},{17,1},{2,18},{18,2},{3,19},{19,3},{4,20},{20... | collective-permute-start | bytes 1572872 | tf_op jit(solution)/shard_map/ppermute | solution.py:20
  40.0 24.2 %collective-permute-start.11 = (bf16[64,2048]{1,0:T(8,128)(2,1)S(1)}, bf16[64,2048]{1,0:T(8,128)(2,1)S(1)}, u32[]{:S(2)}, u32[]{:S(2)}) collective-permute-start(bf16[64,2048]{1,0:T(8,128)(2,1)S(1)} %slice.461), channel_id=1, source_target_pairs={{0,16},{16,0},{1,17},{17,1},{2,18},{18,2},{3,19},{19,3},{4,20},{20... | collective-permute-start | bytes 786440 | tf_op jit(solution)/shard_map/ppermute | solution.py:20
  42.0 21.2 %collective-permute-start.10 = (bf16[64,2048]{1,0:T(8,128)(2,1)S(1)}, bf16[64,2048]{1,0:T(8,128)(2,1)S(1)}, u32[]{:S(2)}, u32[]{:S(2)}) collective-permute-start(bf16[64,2048]{1,0:T(8,128)(2,1)S(1)} %slice.460), channel_id=1, source_target_pairs={{0,2},{2,0},{1,3},{3,1},{4,6},{6,4},{5,7},{7,5},{8,10},{10,8},{9,1... | collective-permute-start | bytes 786440 | tf_op jit(solution)/shard_map/ppermute | solution.py:24
  63.3 37.1 %collective-permute-start.4 = (bf16[512,2048]{1,0:T(8,128)(2,1)}, bf16[512,2048]{1,0:T(8,128)(2,1)}, u32[]{:S(2)}, u32[]{:S(2)}) collective-permute-start(bf16[512,2048]{1,0:T(8,128)(2,1)} %get-tuple-element.146), channel_id=1, source_target_pairs={{0,1},{1,0},{2,3},{3,2},{4,5},{5,4},{6,7},{7,6},{8,9},{9,8},{10,11... | collective-permute-start | bytes 6291464 | tf_op jit(solution)/shard_map/ppermute | solution.py:28
  65.6 38.0 %collective-permute-start.12 = (bf16[512,2048]{1,0:T(8,128)(2,1)}, bf16[512,2048]{1,0:T(8,128)(2,1)}, u32[]{:S(2)}, u32[]{:S(2)}) collective-permute-start(bf16[512,2048]{1,0:T(8,128)(2,1)} %get-tuple-element.142), channel_id=1, source_target_pairs={{0,1},{1,0},{2,3},{3,2},{4,5},{5,4},{6,7},{7,6},{8,9},{9,8},{10,11... | collective-permute-start | bytes 6291464 | tf_op jit(solution)/shard_map/ppermute | solution.py:28
  68.4 30.8 %all-to-all-start.1 = ((bf16[4,128,1536]{2,1,0:T(8,128)(2,1)}), bf16[4,128,1536]{2,1,0:T(8,128)(2,1)S(1)}, u32[]{:S(2)}, u32[]{:S(2)}) async-start(bf16[4,128,1536]{2,1,0:T(8,128)(2,1)} %get-tuple-element.41), calls=%async_computation.1 | async-start | bytes 3145728 | tf_op jit(solution)/shard_map/all_to_all | solution.py:89
  72.0 144.7 %all-gather.6.cloned.1.call-start = ((), (), s32[]{:S(2)}) async-start(), calls=%async_computation.12 | async-start | bytes 7864320 | tf_op jit(solution)/shard_map/all_gather | solution.py:94
  72.1 20.0 %collective-permute-start.6 = (s32[2,256]{1,0:T(2,128)S(1)}, s32[2,256]{1,0:T(2,128)S(1)}, u32[]{:S(2)}, u32[]{:S(2)}) collective-permute-start(s32[2,256]{1,0:T(2,128)S(1)} %pad_add_fusion.1), channel_id=1, source_target_pairs={{0,2},{2,0},{1,3},{3,1},{4,6},{6,4},{5,7},{7,5},{8,10},{10,8},{9,1... | collective-permute-start | bytes 6152 | tf_op jit(solution)/shard_map/ppermute | solution.py:24
  158.9 15.2 %collective-permute-start.19 = (bf16[128,2048]{1,0:T(8,128)(2,1)}, bf16[128,2048]{1,0:T(8,128)(2,1)}, u32[]{:S(2)}, u32[]{:S(2)}) collective-permute-start(bf16[128,2048]{1,0:T(8,128)(2,1)} %get-tuple-element.74), channel_id=1, source_target_pairs={{0,2},{2,0},{1,3},{3,1},{4,6},{6,4},{5,7},{7,5},{8,10},{10,8},{9,1... | collective-permute-start | bytes 1572872 | tf_op jit(solution)/shard_map/ppermute | solution.py:24
  159.5 16.2 %collective-permute-start.18 = (bf16[128,2048]{1,0:T(8,128)(2,1)}, bf16[128,2048]{1,0:T(8,128)(2,1)}, u32[]{:S(2)}, u32[]{:S(2)}) collective-permute-start(bf16[128,2048]{1,0:T(8,128)(2,1)} %get-tuple-element.74), channel_id=1, source_target_pairs={{0,16},{16,0},{1,17},{17,1},{2,18},{18,2},{3,19},{19,3},{4,20},{20... | collective-permute-start | bytes 1572872 | tf_op jit(solution)/shard_map/ppermute | solution.py:20
  160.6 28.1 %all-to-all-start.2 = ((bf16[4,128,768]{2,1,0:T(8,128)(2,1)}), bf16[4,128,768]{2,1,0:T(8,128)(2,1)}, u32[]{:S(2)}, u32[]{:S(2)}) async-start(bf16[4,128,768]{2,1,0:T(8,128)(2,1)} %copy-done.7), calls=%async_computation.2 | async-start | bytes 1572864 | tf_op jit(solution)/shard_map/all_to_all | solution.py:89
  164.8 115.3 %all-gather.8.cloned.1.call-start = ((), (), s32[]{:S(2)}) async-start(), calls=%async_computation.13 | async-start | bytes 3932160 | tf_op jit(solution)/shard_map/all_gather | solution.py:94
  188.7 239.1 %reduce-scatter.7.cloned.1.call-start = ((), (), s32[]{:S(2)}) async-start(), calls=%async_computation.15 | async-start | bytes 3932160 | tf_op jit(solution)/shard_map/reduce_scatter | solution.py:98
  235.0 205.9 %reduce-scatter.5.cloned.1.call-start = ((), (), s32[]{:S(2)}) async-start(), calls=%async_computation.14 | async-start | bytes 3932160 | tf_op jit(solution)/shard_map/reduce_scatter | solution.py:98
  300.8 193.9 %reduce-scatter.9.cloned.1.call-start = ((), (), s32[]{:S(2)}) async-start(), calls=%async_computation.16 | async-start | bytes 5242880 | tf_op jit(solution)/shard_map/reduce_scatter | solution.py:98
  430.1 17.3 %all-to-all-start.4 = ((bf16[4,128,768]{2,1,0:T(8,128)(2,1)}), bf16[4,128,768]{2,1,0:T(8,128)(2,1)S(1)}, u32[]{:S(2)}, u32[]{:S(2)}) async-start(bf16[4,128,768]{2,1,0:T(8,128)(2,1)} %bitcast.12), calls=%async_computation.6 | async-start | bytes 1572864 | tf_op jit(solution)/shard_map/all_to_all | solution.py:89
  441.0 53.8 %collective-permute-start.33 = (bf16[512,2048]{1,0:T(8,128)(2,1)}, bf16[512,2048]{1,0:T(8,128)(2,1)}, u32[]{:S(2)}, u32[]{:S(2)}) collective-permute-start(bf16[512,2048]{1,0:T(8,128)(2,1)} %convolution_convert_fusion.6), channel_id=1, source_target_pairs={{0,1},{1,0},{2,3},{3,2},{4,5},{5,4},{6,7},{7,6},{8,9},{9,8},{10,11... | collective-permute-start | bytes 6291464 | tf_op jit(solution)/shard_map/ppermute | solution.py:28
  445.6 17.2 %collective-permute-start.45 = (f32[1,4352]{1,0:T(1,128)S(1)}, f32[1,4352]{1,0:T(1,128)S(1)}, u32[]{:S(2)}, u32[]{:S(2)}) collective-permute-start(f32[1,4352]{1,0:T(1,128)S(1)} %add.205), channel_id=1, source_target_pairs={{0,16},{16,0},{1,17},{17,1},{2,18},{18,2},{3,19},{19,3},{4,20},{20... | collective-permute-start | bytes 52232 | tf_op jit(solution)/shard_map/ppermute | solution.py:136
  447.4 15.1 %all-to-all-start.3 = ((bf16[4,128,768]{2,1,0:T(8,128)(2,1)}), bf16[4,128,768]{2,1,0:T(8,128)(2,1)S(1)}, u32[]{:S(2)}, u32[]{:S(2)}) async-start(bf16[4,128,768]{2,1,0:T(8,128)(2,1)} %bitcast.49), calls=%async_computation.4 | async-start | bytes 1572864 | tf_op jit(solution)/shard_map/all_to_all | solution.py:89
  450.9 85.6 %reduce-scatter.11.cloned.1.call-start = ((), (), s32[]{:S(2)}) async-start(), calls=%async_computation.17 | async-start | bytes 2621440 | tf_op jit(solution)/shard_map/reduce_scatter | solution.py:98
  457.1 20.3 %collective-permute-start.49 = (bf16[4,128,768]{2,1,0:T(8,128)(2,1)S(1)}, bf16[4,128,768]{2,1,0:T(8,128)(2,1)S(1)}, u32[]{:S(2)}, u32[]{:S(2)}) collective-permute-start(bf16[4,128,768]{2,1,0:T(8,128)(2,1)S(1)} %all-to-all-done.4.refs_2_), channel_id=1, source_target_pairs={{0,16},{16,0},{1,17},{17,1},{2,18},{18,2},{3,19},{19,3},{4,20},{20... | collective-permute-start | bytes 2359304 | tf_op jit(solution)/shard_map/ppermute | solution.py:20
  462.5 31.3 %collective-permute-start.48 = (bf16[4,128,768]{2,1,0:T(8,128)(2,1)S(1)}, bf16[4,128,768]{2,1,0:T(8,128)(2,1)S(1)}, u32[]{:S(2)}, u32[]{:S(2)}) collective-permute-start(bf16[4,128,768]{2,1,0:T(8,128)(2,1)S(1)} %all-to-all-done.3.refs_0_), channel_id=1, source_target_pairs={{0,16},{16,0},{1,17},{17,1},{2,18},{18,2},{3,19},{19,3},{4,20},{20... | collective-permute-start | bytes 2359304 | tf_op jit(solution)/shard_map/ppermute | solution.py:20
  500.8 19.4 %collective-permute-start.36 = (bf16[128,2048]{1,0:T(8,128)(2,1)}, bf16[128,2048]{1,0:T(8,128)(2,1)}, u32[]{:S(2)}, u32[]{:S(2)}) collective-permute-start(bf16[128,2048]{1,0:T(8,128)(2,1)} %pad_maximum_fusion.27), channel_id=1, source_target_pairs={{0,2},{2,0},{1,3},{3,1},{4,6},{6,4},{5,7},{7,5},{8,10},{10,8},{9,1... | collective-permute-start | bytes 1572872 | tf_op jit(solution)/shard_map/ppermute | solution.py:24
  516.7 18.0 %all-to-all-start.6 = ((bf16[4,128,1024]{2,1,0:T(8,128)(2,1)}), bf16[4,128,1024]{2,1,0:T(8,128)(2,1)S(1)}, u32[]{:S(2)}, u32[]{:S(2)}) async-start(bf16[4,128,1024]{2,1,0:T(8,128)(2,1)} %bitcast.47), calls=%async_computation.10 | async-start | bytes 2097152 | tf_op jit(solution)/shard_map/all_to_all | solution.py:89
  523.8 16.2 %collective-permute-start.37 = (bf16[64,2048]{1,0:T(8,128)(2,1)S(1)}, bf16[64,2048]{1,0:T(8,128)(2,1)}, u32[]{:S(2)}, u32[]{:S(2)}) collective-permute-start(bf16[64,2048]{1,0:T(8,128)(2,1)S(1)} %get-tuple-element.84), channel_id=1, source_target_pairs={{0,16},{16,0},{1,17},{17,1},{2,18},{18,2},{3,19},{19,3},{4,20},{20... | collective-permute-start | bytes 786440 | tf_op jit(solution)/shard_map/ppermute | solution.py:20
  534.7 26.2 %collective-permute-start.51 = (bf16[4,128,1024]{2,1,0:T(8,128)(2,1)S(1)}, bf16[4,128,1024]{2,1,0:T(8,128)(2,1)}, u32[]{:S(2)}, u32[]{:S(2)}) collective-permute-start(bf16[4,128,1024]{2,1,0:T(8,128)(2,1)S(1)} %all-to-all-done.6.refs_4_), channel_id=1, source_target_pairs={{0,16},{16,0},{1,17},{17,1},{2,18},{18,2},{3,19},{19,3},{4,20},{20... | collective-permute-start | bytes 3145736 | tf_op jit(solution)/shard_map/ppermute | solution.py:20
  548.8 21.9 %collective-permute-start.50 = (bf16[4,128,512]{2,1,0:T(8,128)(2,1)S(1)}, bf16[4,128,512]{2,1,0:T(8,128)(2,1)S(1)}, u32[]{:S(2)}, u32[]{:S(2)}) collective-permute-start(bf16[4,128,512]{2,1,0:T(8,128)(2,1)S(1)} %all-to-all-done.5.refs_0_), channel_id=1, source_target_pairs={{0,16},{16,0},{1,17},{17,1},{2,18},{18,2},{3,19},{19,3},{4,20},{20... | collective-permute-start | bytes 1572872 | tf_op jit(solution)/shard_map/ppermute | solution.py:20
  (97 other events, 752.8 us)
Sparse Core Ops, SparseCore 0:
  29.8 64.2 all-gather.3
  100.5 116.1 all-gather.5
  218.3 61.7 all-gather.7
  282.8 58.8 reduce-scatter.6
  344.5 60.2 reduce-scatter.4
  407.0 77.5 reduce-scatter.8
  494.9 41.5 reduce-scatter.10

commit v5 on v4

--- a/solution.py
+++ b/solution.py
@@ -58,15 +58,22 @@
     rows = members[0][0].shape[0]
     widths = [sum(n for _, _, n in group) for group in groups]
 
+    tile = math.gcd(rows, 16)
+
     def kernel(side_ref, *refs):
-        sources = iter(refs[: len(members)])
-        for group, out in zip(groups, refs[len(members) :]):
-            at = 0
-            for _, _, n in group:
-                source = next(sources)
-                for block in range(4):
-                    out[block, :, at : at + n] = source[:, block * n : (block + 1) * n]
-                at += n
+        def some(step, carry):
+            span = pl.ds(pl.multiple_of(step * tile, tile), tile)
+            sources = iter(refs[: len(members)])
+            for group, out in zip(groups, refs[len(members) :]):
+                at = 0
+                for _, _, n in group:
+                    source = next(sources)
+                    for block in range(4):
+                        out[block, span, at : at + n] = source[span, block * n : (block + 1) * n]
+                    at += n
+            return carry
+
+        lax.fori_loop(0, rows // tile, some, 0)
 
     def half(start, n):
         return pl.BlockSpec((rows, 4 * n), lambda i, side_ref: (0, start // (4 * n) + side_ref[0]))
@@ -99,7 +106,10 @@
 
 
 def hand_out(mine):
-    mine = trade(mine.reshape(4, mine.shape[0] // 4, -1))
+    return trade(mine.reshape(4, mine.shape[0] // 4, -1))
+
+
+def both_sides(mine):
     return (mine, over_rep(mine))
 
 
@@ -108,18 +118,26 @@
     rows = pairs[0][0].shape[1]
     columns = [sum(8 * n for _, _, n in pieces) for pieces in outs]
 
+    tile = math.gcd(rows, 16)
+
     def kernel(side_ref, *refs):
         first = side_ref[0] == 0
-        for out, pieces in zip(refs[2 * len(pairs) :], outs):
-            at = 0
-            for pair, start, n in pieces:
-                own, other = refs[2 * pair], refs[2 * pair + 1]
-                for block in range(4):
-                    a = own[block, :, start : start + n].astype(F32)
-                    b = other[block, :, start : start + n].astype(F32)
-                    out[:, at + block * n : at + (block + 1) * n] = jnp.where(first, a, b)
-                    out[:, at + (4 + block) * n : at + (5 + block) * n] = jnp.where(first, b, a)
-                at += 8 * n
+
+        def some(step, carry):
+            span = pl.ds(pl.multiple_of(step * tile, tile), tile)
+            for out, pieces in zip(refs[2 * len(pairs) :], outs):
+                at = 0
+                for pair, start, n in pieces:
+                    own, other = refs[2 * pair], refs[2 * pair + 1]
+                    for block in range(4):
+                        a = own[block, span, start : start + n].astype(F32)
+                        b = other[block, span, start : start + n].astype(F32)
+                        out[span, at + block * n : at + (block + 1) * n] = jnp.where(first, a, b)
+                        out[span, at + (4 + block) * n : at + (5 + block) * n] = jnp.where(first, b, a)
+                    at += 8 * n
+            return carry
+
+        lax.fori_loop(0, rows // tile, some, 0)
 
     return pl.pallas_call(
         kernel,
@@ -428,6 +446,8 @@
         )
         own_qkv = contract_rows(normed_rows, grad_qkv).astype(BF16)
         mlp_grads = [hand_out(v) for v in mlp_rows[:-1]] + [None]
+        if len(mlp_grads) > 1:
+            mlp_grads[0] = both_sides(mlp_grads[0])
         grad_normed = plane_scatter(lambda i, j: contract_cols(grad_qkv[i:j], qkv), own_tokens)
         grad_in_part, attn_gain_part = norm_back(grad_normed, inputs, recip_attn, attn_gain, 0)
         grad_input = grad_mid + grad_in_part
@@ -440,7 +460,9 @@
         )
         qkv_rows = queue_scatter(own_qkv)
         mlp_grads[-1] = hand_out(mlp_rows[-1])
-        qkv_pair = hand_out(qkv_rows)
+        mlp_grads = [v if isinstance(v, tuple) else both_sides(v) for v in mlp_grads]
+        qkv_rows, mlp_grads[1:-1] = after(qkv_rows, mlp_grads[1:-1])
+        qkv_pair = both_sides(hand_out(qkv_rows))
         last = len(chunks) - 1
         gate_pieces, up_pieces, down_pieces = ([(j, m * n, n) for j, (_, n) in enumerate(chunks)] for m in range(3))
         grad_w_gate, grad_w_up, grad_w_down, grad_w_o = spread(

time: 589 us -> 588 us (level)
    all_gather x3, waiting for transfers between devices: 47 us -> 65.3 us  [gather_rows(): lax.all_gather(blocks.reshape(four * rows, n), 'far', axis=0, tiled=True)]
    unnamed x143 -> x151, local copies, waits for them, and re-layouts: 25.8 us -> 25.3 us
  transfers between devices with their start and end apart: 66 -> 66, of which waited for: 40 -> 39; matrix products, arithmetic and copies ran while one was open for 28% -> 27% of each run, Pallas kernels for 5% -> 5%
where the time goes in v5:
time: 588 us; the launch traced here: 579 us
  waiting for transfers between devices  283 us (48%)
  matrix products  89.8 us (15%)
  starting transfers between devices  81.2 us (14%)
  local copies, waits for them, and re-layouts  52.4 us (9%)
  Pallas kernels  29.1 us (5%)
  other arithmetic  27.3 us (5%)
  between operations  15.9 us (3%)
    ppermute x21, waiting for transfers between devices, over_rep(): return lax.ppermute(v, 'rep', SWAP)  88.4 us
    ppermute x17, waiting for transfers between devices, over_mid(): return lax.ppermute(v, 'mid', SWAP)  81.2 us
    all_gather x3, waiting for transfers between devices, gather_rows(): lax.all_gather(blocks.reshape(four * rows, n), 'far', axis=0, tiled=True)  65.3 us
    ppermute x21, starting transfers between devices, over_rep(): return lax.ppermute(v, 'rep', SWAP)  33.2 us
    dot_general x10, matrix products, contract_cols(): lax.dot_general(left, right, (((1,), (1,)), ((), ())), preferred_element_...  32.2 us
    dot_general x8, matrix products, dot(): return jnp.dot(left, right, preferred_element_type=F32)  32.1 us
    all_to_all x7, starting transfers between devices, trade(): return lax.all_to_all(blocks, ('mid', 'near'), 0, 0)  26 us
    all_to_all x7, waiting for transfers between devices, trade(): return lax.all_to_all(blocks, ('mid', 'near'), 0, 0)  25.5 us
  transfers between devices with their start and end apart: 66, of which 39 were waited for; matrix products, arithmetic and copies ran while one was open for 27% of the time, Pallas kernels for 5%

profile of v5, /device:TPU:0, one launch (start us, length us, event | category | flops | bytes accessed | tf_op | source)
XLA Modules:
  0.0 578.5 jit_solution(15476910996903369983)
XLA Ops:
  20.9 7.9 %all-to-all-done = bf16[4,128,768]{2,1,0:T(8,128)(2,1)S(1)} async-done(((bf16[4,128,768]{2,1,0:T(8,128)(2,1)}), bf16[4,128,768]{2,1,0:T(8,128)(2,1)S(1)}, u32[]{:S(2)}, u32[]{:S(2)}) %all-to-all-start) | async-done | bytes 786464 | tf_op jit(solution)/shard_map/all_to_all | solution.py:96
  33.9 6.1 %collective-permute-done.9 = bf16[128,2048]{1,0:T(8,128)(2,1)S(1)} collective-permute-done((bf16[128,2048]{1,0:T(8,128)(2,1)S(1)}, bf16[128,2048]{1,0:T(8,128)(2,1)S(1)}, u32[]{:S(2)}, u32[]{:S(2)}) %collective-permute-start.9) | collective-permute-done | bytes 524320 | tf_op jit(solution)/shard_map/ppermute | solution.py:24
  42.3 9.0 %collective-permute-done.1 = bf16[128,2048]{1,0:T(8,128)(2,1)S(1)} collective-permute-done((bf16[128,2048]{1,0:T(8,128)(2,1)S(1)}, bf16[128,2048]{1,0:T(8,128)(2,1)S(1)}, u32[]{:S(2)}, u32[]{:S(2)}) %collective-permute-start.1) | collective-permute-done | bytes 524320 | tf_op jit(solution)/shard_map/ppermute | solution.py:24
  74.3 18.0 %collective-permute-done.6 = s32[2,256]{1,0:T(2,128)S(1)} collective-permute-done((s32[2,256]{1,0:T(2,128)S(1)}, s32[2,256]{1,0:T(2,128)S(1)}, u32[]{:S(2)}, u32[]{:S(2)}) %collective-permute-start.6) | collective-permute-done | bytes 2080 | tf_op jit(solution)/shard_map/ppermute | solution.py:24
  107.1 6.0 %fusion.12.proj_ref = f32[1024,512]{1,0:T(8,128)S(1)} fusion(bf16[1024,2048]{1,0:T(8,128)(2,1)} %constant_dynamic-update-slice_fusion.5, bf16[2048,768]{1,0:T(8,128)(2,1)} %all-gather.4.cloned.1.call-done), kind=kOutput, calls=%fused_computation.34 | convolution fusion | flops 2147483648 | bytes 8388608 | tf_op jit(solution)/shard_map/dot_general | solution.py:184
  113.1 8.0 %attention_forward.1.attended_ref = bf16[1024,256]{1,0:T(8,128)(2,1)S(1)} custom-call(f32[1024,512]{1,0:T(8,128)S(1)} %fusion.12.proj_ref, f32[1024,128]{1,0:T(8,128)S(1)} %get-tuple-element.179.cosine_ref, f32[1024,128]{1,0:T(8,128)S(1)} %get-tuple-element.180.sine_ref, s32[1024,1]{1,0:T(8,128)S(1)} %copy-done.3, s32[8,1,128]{2,1,0:T(1,128)S(1)} %bitcast.40, ...), custom_call_target="tpu_custom_call" | custom-call | tf_op jit(solution)/shard_map/attention_forward/pallas_call | solution.py:247
  129.2 12.1 %collective-permute-done.14 = bf16[128,2048]{1,0:T(8,128)(2,1)S(1)} collective-permute-done((bf16[128,2048]{1,0:T(8,128)(2,1)S(1)}, bf16[128,2048]{1,0:T(8,128)(2,1)S(1)}, u32[]{:S(2)}, u32[]{:S(2)}) %collective-permute-start.14) | collective-permute-done | bytes 524320 | tf_op jit(solution)/shard_map/ppermute | solution.py:20
  142.8 6.5 %collective-permute-done.15 = bf16[64,2048]{1,0:T(8,128)(2,1)S(1)} collective-permute-done((bf16[64,2048]{1,0:T(8,128)(2,1)S(1)}, bf16[64,2048]{1,0:T(8,128)(2,1)S(1)}, u32[]{:S(2)}, u32[]{:S(2)}) %collective-permute-start.15) | collective-permute-done | bytes 262176 | tf_op jit(solution)/shard_map/ppermute | solution.py:24
  151.0 5.7 collective-permute-done.17
  166.2 8.2 %collective-permute-done.19 = bf16[128,2048]{1,0:T(8,128)(2,1)} collective-permute-done((bf16[128,2048]{1,0:T(8,128)(2,1)}, bf16[128,2048]{1,0:T(8,128)(2,1)}, u32[]{:S(2)}, u32[]{:S(2)}) %collective-permute-start.19) | collective-permute-done | bytes 524320 | tf_op jit(solution)/shard_map/ppermute | solution.py:24
  196.7 20.2 %all-gather.6.cloned.1.call-done = bf16[2048,1536]{1,0:T(8,128)(2,1)} async-done(((bf16[512,1536]{1,0:T(8,128)(2,1)}), bf16[2048,1536]{1,0:T(8,128)(2,1)}) %all-gather.6.cloned.1.call-update) | async-done | bytes 6291472 | tf_op jit(solution)/shard_map/all_gather | solution.py:101
  216.9 5.2 fusion.7
  235.2 45.1 %all-gather.8.cloned.1.call-done = bf16[2048,768]{1,0:T(8,128)(2,1)} async-done(((bf16[512,768]{1,0:T(8,128)(2,1)}), bf16[2048,768]{1,0:T(8,128)(2,1)}) %all-gather.8.cloned.1.call-update) | async-done | bytes 3145744 | tf_op jit(solution)/shard_map/all_gather | solution.py:101
  287.7 5.1 multiply_convert_fusion.2
  295.2 5.1 multiply_convert_fusion.1
  316.5 5.1 fusion.98
  327.5 8.7 %collective-permute-done.24 = bf16[128,2048]{1,0:T(8,128)(2,1)S(1)} collective-permute-done((bf16[128,2048]{1,0:T(8,128)(2,1)S(1)}, bf16[128,2048]{1,0:T(8,128)(2,1)S(1)}, u32[]{:S(2)}, u32[]{:S(2)}) %collective-permute-start.24) | collective-permute-done | bytes 524320 | tf_op jit(solution)/shard_map/ppermute | solution.py:20
  347.5 6.0 %collective-permute-done.27 = bf16[64,2048]{1,0:T(8,128)(2,1)S(1)} collective-permute-done((bf16[64,2048]{1,0:T(8,128)(2,1)S(1)}, bf16[64,2048]{1,0:T(8,128)(2,1)S(1)}, u32[]{:S(2)}, u32[]{:S(2)}) %collective-permute-start.27) | collective-permute-done | bytes 262176 | tf_op jit(solution)/shard_map/ppermute | solution.py:20
  358.5 9.1 %collective-permute-done.29 = bf16[128,2048]{1,0:T(8,128)(2,1)S(1)} collective-permute-done((bf16[128,2048]{1,0:T(8,128)(2,1)S(1)}, bf16[128,2048]{1,0:T(8,128)(2,1)S(1)}, u32[]{:S(2)}, u32[]{:S(2)}) %collective-permute-start.29) | collective-permute-done | bytes 524320 | tf_op jit(solution)/shard_map/ppermute | solution.py:24
  381.9 11.2 %attention_backward.1 = (bf16[1024,512]{1,0:T(8,128)(2,1)S(1)}, f32[8,128]{1,0:T(8,128)S(1)}) custom-call(f32[1024,512]{1,0:T(8,128)S(1)} %fusion.12.proj_ref, f32[1024,128]{1,0:T(8,128)S(1)} %get-tuple-element.179.cosine_ref, f32[1024,128]{1,0:T(8,128)S(1)} %get-tuple-element.180.sine_ref, s32[1024,1]{1,0:T(8,128)S(1)} %copy-done.4, ...), custom_call_target="tpu_custom_call" | custom-call | tf_op jit(solution)/shard_map/attention_backward/pallas_call | solution.py:320
  405.7 12.4 %collective-permute-done.39 = bf16[128,2048]{1,0:T(8,128)(2,1)S(1)} collective-permute-done((bf16[128,2048]{1,0:T(8,128)(2,1)S(1)}, bf16[128,2048]{1,0:T(8,128)(2,1)S(1)}, u32[]{:S(2)}, u32[]{:S(2)}) %collective-permute-start.39) | collective-permute-done | bytes 524320 | tf_op jit(solution)/shard_map/ppermute | solution.py:20
  419.8 6.4 %collective-permute-done.40 = bf16[64,2048]{1,0:T(8,128)(2,1)S(1)} collective-permute-done((bf16[64,2048]{1,0:T(8,128)(2,1)S(1)}, bf16[64,2048]{1,0:T(8,128)(2,1)S(1)}, u32[]{:S(2)}, u32[]{:S(2)}) %collective-permute-start.40) | collective-permute-done | bytes 262176 | tf_op jit(solution)/shard_map/ppermute | solution.py:24
  427.9 5.6 collective-permute-done.42
  449.7 5.9 %convolution_convert_fusion.3 = bf16[2048,512]{1,0:T(8,128)(2,1)} fusion(bf16[1024,2048]{1,0:T(8,128)(2,1)} %constant_dynamic-update-slice_fusion.5, bf16[1024,512]{1,0:T(8,128)(2,1)S(1)} %copy-done.17), kind=kOutput, calls=%fused_computation.16 | convolution fusion | flops 2148532224 | bytes 7340032 | tf_op jit(solution)/shard_map/dot_general | solution.py:188
  465.2 6.4 %collective-permute-done.46 = f32[1,4352]{1,0:T(1,128)S(1)} collective-permute-done((f32[1,4352]{1,0:T(1,128)S(1)}, f32[1,4352]{1,0:T(1,128)S(1)}, u32[]{:S(2)}, u32[]{:S(2)}) %collective-permute-start.46) | collective-permute-done | bytes 17440 | tf_op jit(solution)/shard_map/ppermute | solution.py:159
  478.2 6.2 %collective-permute-done.48.refs_1_ = bf16[4,128,768]{2,1,0:T(8,128)(2,1)S(1)} collective-permute-done((bf16[4,128,768]{2,1,0:T(8,128)(2,1)S(1)}, bf16[4,128,768]{2,1,0:T(8,128)(2,1)S(1)}, u32[]{:S(2)}, u32[]{:S(2)}) %collective-permute-start.48) | collective-permute-done | bytes 786464 | tf_op jit(solution)/shard_map/ppermute | solution.py:20
  493.4 9.9 %collective-permute-done.34 = bf16[128,2048]{1,0:T(8,128)(2,1)S(1)} collective-permute-done((bf16[128,2048]{1,0:T(8,128)(2,1)S(1)}, bf16[128,2048]{1,0:T(8,128)(2,1)S(1)}, u32[]{:S(2)}, u32[]{:S(2)}) %collective-permute-start.34) | collective-permute-done | bytes 524320 | tf_op jit(solution)/shard_map/ppermute | solution.py:20
  515.8 9.2 %all-to-all-done.6.refs_4_ = bf16[4,128,1024]{2,1,0:T(8,128)(2,1)S(1)} async-done(((bf16[4,128,1024]{2,1,0:T(8,128)(2,1)}), bf16[4,128,1024]{2,1,0:T(8,128)(2,1)S(1)}, u32[]{:S(2)}, u32[]{:S(2)}) %all-to-all-start.6) | async-done | bytes 1048608 | tf_op jit(solution)/shard_map/all_to_all | solution.py:96
  538.7 5.6 all-to-all-done.5.refs_0_
  549.3 9.8 %collective-permute-done.51.refs_5_ = bf16[4,128,1024]{2,1,0:T(8,128)(2,1)} collective-permute-done((bf16[4,128,1024]{2,1,0:T(8,128)(2,1)S(1)}, bf16[4,128,1024]{2,1,0:T(8,128)(2,1)}, u32[]{:S(2)}, u32[]{:S(2)}) %collective-permute-start.51) | collective-permute-done | bytes 1048608 | tf_op jit(solution)/shard_map/ppermute | solution.py:20
  559.1 5.9 %spread.3 = (f32[128,6144]{1,0:T(8,128)}, f32[128,6144]{1,0:T(8,128)}, f32[128,6144]{1,0:T(8,128)}, f32[128,2048]{1,0:T(8,128)}) custom-call(s32[1]{0:T(128)} %bitcast.side_ref, bf16[4,128,768]{2,1,0:T(8,128)(2,1)S(1)} %all-to-all-done.3.refs_0_, bf16[4,128,768]{2,1,0:T(8,128)(2,1)S(1)} %copy-done.9, bf16[4,128,768]{2,1,0:T(8,128)(2,1)S(1)} %all-to-all-done.4.refs_2_, ...), custom_call_target="tpu_custom_call" | custom-call | tf_op jit(solution)/shard_map/spread/pallas_call | solution.py:142
  565.1 4.7 collective-permute-done.50.refs_1_
  (375 shorter events, 266.3 us)
Async XLA Ops:
  12.2 16.6 %all-to-all-start = ((bf16[4,128,768]{2,1,0:T(8,128)(2,1)}), bf16[4,128,768]{2,1,0:T(8,128)(2,1)S(1)}, u32[]{:S(2)}, u32[]{:S(2)}) async-start(bf16[4,128,768]{2,1,0:T(8,128)(2,1)} %pick_columns.2), calls=%async_computation | async-start | bytes 1572864 | tf_op jit(solution)/shard_map/all_to_all | solution.py:96
  16.5 90.6 %all-gather.4.cloned.1.call-start = ((), (), s32[]{:S(2)}) async-start(), calls=%async_computation.11 | async-start | bytes 3932160 | tf_op jit(solution)/shard_map/all_gather | solution.py:101
  16.5 23.6 %collective-permute-start.9 = (bf16[128,2048]{1,0:T(8,128)(2,1)S(1)}, bf16[128,2048]{1,0:T(8,128)(2,1)S(1)}, u32[]{:S(2)}, u32[]{:S(2)}) collective-permute-start(bf16[128,2048]{1,0:T(8,128)(2,1)S(1)} %copy-done.34), channel_id=1, source_target_pairs={{0,2},{2,0},{1,3},{3,1},{4,6},{6,4},{5,7},{7,5},{8,10},{10,8},{9,1... | collective-permute-start | bytes 1572872 | tf_op jit(solution)/shard_map/ppermute | solution.py:24
  18.8 23.3 %collective-permute-start.8 = (bf16[128,2048]{1,0:T(8,128)(2,1)S(1)}, bf16[128,2048]{1,0:T(8,128)(2,1)S(1)}, u32[]{:S(2)}, u32[]{:S(2)}) collective-permute-start(bf16[128,2048]{1,0:T(8,128)(2,1)S(1)} %copy-done.34), channel_id=1, source_target_pairs={{0,16},{16,0},{1,17},{17,1},{2,18},{18,2},{3,19},{19,3},{4,20},{20... | collective-permute-start | bytes 1572872 | tf_op jit(solution)/shard_map/ppermute | solution.py:20
  30.7 20.6 %collective-permute-start.1 = (bf16[128,2048]{1,0:T(8,128)(2,1)S(1)}, bf16[128,2048]{1,0:T(8,128)(2,1)S(1)}, u32[]{:S(2)}, u32[]{:S(2)}) collective-permute-start(bf16[128,2048]{1,0:T(8,128)(2,1)S(1)} %get-tuple-element.82), channel_id=1, source_target_pairs={{0,2},{2,0},{1,3},{3,1},{4,6},{6,4},{5,7},{7,5},{8,10},{10,8},{9,1... | collective-permute-start | bytes 1572872 | tf_op jit(solution)/shard_map/ppermute | solution.py:24
  30.7 22.6 %collective-permute-start = (bf16[128,2048]{1,0:T(8,128)(2,1)S(1)}, bf16[128,2048]{1,0:T(8,128)(2,1)S(1)}, u32[]{:S(2)}, u32[]{:S(2)}) collective-permute-start(bf16[128,2048]{1,0:T(8,128)(2,1)S(1)} %get-tuple-element.82), channel_id=1, source_target_pairs={{0,16},{16,0},{1,17},{17,1},{2,18},{18,2},{3,19},{19,3},{4,20},{20... | collective-permute-start | bytes 1572872 | tf_op jit(solution)/shard_map/ppermute | solution.py:20
  40.1 24.3 %collective-permute-start.11 = (bf16[64,2048]{1,0:T(8,128)(2,1)S(1)}, bf16[64,2048]{1,0:T(8,128)(2,1)S(1)}, u32[]{:S(2)}, u32[]{:S(2)}) collective-permute-start(bf16[64,2048]{1,0:T(8,128)(2,1)S(1)} %slice.461), channel_id=1, source_target_pairs={{0,16},{16,0},{1,17},{17,1},{2,18},{18,2},{3,19},{19,3},{4,20},{20... | collective-permute-start | bytes 786440 | tf_op jit(solution)/shard_map/ppermute | solution.py:20
  42.1 21.2 %collective-permute-start.10 = (bf16[64,2048]{1,0:T(8,128)(2,1)S(1)}, bf16[64,2048]{1,0:T(8,128)(2,1)S(1)}, u32[]{:S(2)}, u32[]{:S(2)}) collective-permute-start(bf16[64,2048]{1,0:T(8,128)(2,1)S(1)} %slice.460), channel_id=1, source_target_pairs={{0,2},{2,0},{1,3},{3,1},{4,6},{6,4},{5,7},{7,5},{8,10},{10,8},{9,1... | collective-permute-start | bytes 786440 | tf_op jit(solution)/shard_map/ppermute | solution.py:24
  63.3 37.3 %collective-permute-start.4 = (bf16[512,2048]{1,0:T(8,128)(2,1)}, bf16[512,2048]{1,0:T(8,128)(2,1)}, u32[]{:S(2)}, u32[]{:S(2)}) collective-permute-start(bf16[512,2048]{1,0:T(8,128)(2,1)} %get-tuple-element.150), channel_id=1, source_target_pairs={{0,1},{1,0},{2,3},{3,2},{4,5},{5,4},{6,7},{7,6},{8,9},{9,8},{10,11... | collective-permute-start | bytes 6291464 | tf_op jit(solution)/shard_map/ppermute | solution.py:28
  65.7 38.1 %collective-permute-start.12 = (bf16[512,2048]{1,0:T(8,128)(2,1)}, bf16[512,2048]{1,0:T(8,128)(2,1)}, u32[]{:S(2)}, u32[]{:S(2)}) collective-permute-start(bf16[512,2048]{1,0:T(8,128)(2,1)} %get-tuple-element.146), channel_id=1, source_target_pairs={{0,1},{1,0},{2,3},{3,2},{4,5},{5,4},{6,7},{7,6},{8,9},{9,8},{10,11... | collective-permute-start | bytes 6291464 | tf_op jit(solution)/shard_map/ppermute | solution.py:28
  68.6 30.8 %all-to-all-start.1 = ((bf16[4,128,1536]{2,1,0:T(8,128)(2,1)}), bf16[4,128,1536]{2,1,0:T(8,128)(2,1)S(1)}, u32[]{:S(2)}, u32[]{:S(2)}) async-start(bf16[4,128,1536]{2,1,0:T(8,128)(2,1)} %get-tuple-element.43), calls=%async_computation.1 | async-start | bytes 3145728 | tf_op jit(solution)/shard_map/all_to_all | solution.py:96
  72.2 144.7 %all-gather.6.cloned.1.call-start = ((), (), s32[]{:S(2)}) async-start(), calls=%async_computation.12 | async-start | bytes 7864320 | tf_op jit(solution)/shard_map/all_gather | solution.py:101
  72.3 20.0 %collective-permute-start.6 = (s32[2,256]{1,0:T(2,128)S(1)}, s32[2,256]{1,0:T(2,128)S(1)}, u32[]{:S(2)}, u32[]{:S(2)}) collective-permute-start(s32[2,256]{1,0:T(2,128)S(1)} %pad_add_fusion.1), channel_id=1, source_target_pairs={{0,2},{2,0},{1,3},{3,1},{4,6},{6,4},{5,7},{7,5},{8,10},{10,8},{9,1... | collective-permute-start | bytes 6152 | tf_op jit(solution)/shard_map/ppermute | solution.py:24
  159.2 15.2 %collective-permute-start.19 = (bf16[128,2048]{1,0:T(8,128)(2,1)}, bf16[128,2048]{1,0:T(8,128)(2,1)}, u32[]{:S(2)}, u32[]{:S(2)}) collective-permute-start(bf16[128,2048]{1,0:T(8,128)(2,1)} %get-tuple-element.78), channel_id=1, source_target_pairs={{0,2},{2,0},{1,3},{3,1},{4,6},{6,4},{5,7},{7,5},{8,10},{10,8},{9,1... | collective-permute-start | bytes 1572872 | tf_op jit(solution)/shard_map/ppermute | solution.py:24
  159.8 16.2 %collective-permute-start.18 = (bf16[128,2048]{1,0:T(8,128)(2,1)}, bf16[128,2048]{1,0:T(8,128)(2,1)}, u32[]{:S(2)}, u32[]{:S(2)}) collective-permute-start(bf16[128,2048]{1,0:T(8,128)(2,1)} %get-tuple-element.78), channel_id=1, source_target_pairs={{0,16},{16,0},{1,17},{17,1},{2,18},{18,2},{3,19},{19,3},{4,20},{20... | collective-permute-start | bytes 1572872 | tf_op jit(solution)/shard_map/ppermute | solution.py:20
  160.9 28.1 %all-to-all-start.2 = ((bf16[4,128,768]{2,1,0:T(8,128)(2,1)}), bf16[4,128,768]{2,1,0:T(8,128)(2,1)}, u32[]{:S(2)}, u32[]{:S(2)}) async-start(bf16[4,128,768]{2,1,0:T(8,128)(2,1)} %copy-done.7), calls=%async_computation.2 | async-start | bytes 1572864 | tf_op jit(solution)/shard_map/all_to_all | solution.py:96
  165.1 115.2 %all-gather.8.cloned.1.call-start = ((), (), s32[]{:S(2)}) async-start(), calls=%async_computation.13 | async-start | bytes 3932160 | tf_op jit(solution)/shard_map/all_gather | solution.py:101
  189.0 254.2 %reduce-scatter.5.cloned.1.call-start = ((), (), s32[]{:S(2)}) async-start(), calls=%async_computation.14 | async-start | bytes 3932160 | tf_op jit(solution)/shard_map/reduce_scatter | solution.py:105
  280.3 175.3 %reduce-scatter.7.cloned.1.call-start = ((), (), s32[]{:S(2)}) async-start(), calls=%async_computation.15 | async-start | bytes 3932160 | tf_op jit(solution)/shard_map/reduce_scatter | solution.py:105
  316.4 168.3 %reduce-scatter.9.cloned.1.call-start = ((), (), s32[]{:S(2)}) async-start(), calls=%async_computation.16 | async-start | bytes 5242880 | tf_op jit(solution)/shard_map/reduce_scatter | solution.py:105
  325.9 15.5 %collective-permute-start.26 = (bf16[128,2048]{1,0:T(8,128)(2,1)S(1)}, bf16[128,2048]{1,0:T(8,128)(2,1)S(1)}, u32[]{:S(2)}, u32[]{:S(2)}) collective-permute-start(bf16[128,2048]{1,0:T(8,128)(2,1)S(1)} %pad_maximum_fusion.25), channel_id=1, source_target_pairs={{0,2},{2,0},{1,3},{3,1},{4,6},{6,4},{5,7},{7,5},{8,10},{10,8},{9,1... | collective-permute-start | bytes 1572872 | tf_op jit(solution)/shard_map/ppermute | solution.py:24
  443.1 41.6 %collective-permute-start.33 = (bf16[512,2048]{1,0:T(8,128)(2,1)}, bf16[512,2048]{1,0:T(8,128)(2,1)}, u32[]{:S(2)}, u32[]{:S(2)}) collective-permute-start(bf16[512,2048]{1,0:T(8,128)(2,1)} %convolution_convert_fusion.6), channel_id=1, source_target_pairs={{0,1},{1,0},{2,3},{3,2},{4,5},{5,4},{6,7},{7,6},{8,9},{9,8},{10,11... | collective-permute-start | bytes 6291464 | tf_op jit(solution)/shard_map/ppermute | solution.py:28
  449.1 16.0 %collective-permute-start.45 = (f32[1,4352]{1,0:T(1,128)S(1)}, f32[1,4352]{1,0:T(1,128)S(1)}, u32[]{:S(2)}, u32[]{:S(2)}) collective-permute-start(f32[1,4352]{1,0:T(1,128)S(1)} %add.205), channel_id=1, source_target_pairs={{0,16},{16,0},{1,17},{17,1},{2,18},{18,2},{3,19},{19,3},{4,20},{20... | collective-permute-start | bytes 52232 | tf_op jit(solution)/shard_map/ppermute | solution.py:154
  460.7 17.5 %all-to-all-start.4 = ((bf16[4,128,768]{2,1,0:T(8,128)(2,1)}), bf16[4,128,768]{2,1,0:T(8,128)(2,1)S(1)}, u32[]{:S(2)}, u32[]{:S(2)}) async-start(bf16[4,128,768]{2,1,0:T(8,128)(2,1)} %bitcast.12), calls=%async_computation.6 | async-start | bytes 1572864 | tf_op jit(solution)/shard_map/all_to_all | solution.py:96
  464.2 67.8 %reduce-scatter.11.cloned.1.call-start = ((), (), s32[]{:S(2)}) async-start(), calls=%async_computation.17 | async-start | bytes 2621440 | tf_op jit(solution)/shard_map/reduce_scatter | solution.py:105
  464.5 20.0 %collective-permute-start.48 = (bf16[4,128,768]{2,1,0:T(8,128)(2,1)S(1)}, bf16[4,128,768]{2,1,0:T(8,128)(2,1)S(1)}, u32[]{:S(2)}, u32[]{:S(2)}) collective-permute-start(bf16[4,128,768]{2,1,0:T(8,128)(2,1)S(1)} %all-to-all-done.3.refs_0_), channel_id=1, source_target_pairs={{0,16},{16,0},{1,17},{17,1},{2,18},{18,2},{3,19},{19,3},{4,20},{20... | collective-permute-start | bytes 2359304 | tf_op jit(solution)/shard_map/ppermute | solution.py:20
  491.9 20.1 %collective-permute-start.36 = (bf16[128,2048]{1,0:T(8,128)(2,1)}, bf16[128,2048]{1,0:T(8,128)(2,1)}, u32[]{:S(2)}, u32[]{:S(2)}) collective-permute-start(bf16[128,2048]{1,0:T(8,128)(2,1)} %pad_maximum_fusion.27), channel_id=1, source_target_pairs={{0,2},{2,0},{1,3},{3,1},{4,6},{6,4},{5,7},{7,5},{8,10},{10,8},{9,1... | collective-permute-start | bytes 1572872 | tf_op jit(solution)/shard_map/ppermute | solution.py:24
  507.0 18.0 %all-to-all-start.6 = ((bf16[4,128,1024]{2,1,0:T(8,128)(2,1)}), bf16[4,128,1024]{2,1,0:T(8,128)(2,1)S(1)}, u32[]{:S(2)}, u32[]{:S(2)}) async-start(bf16[4,128,1024]{2,1,0:T(8,128)(2,1)} %bitcast.47), calls=%async_computation.10 | async-start | bytes 2097152 | tf_op jit(solution)/shard_map/all_to_all | solution.py:96
  510.5 20.4 %collective-permute-start.49 = (bf16[4,128,768]{2,1,0:T(8,128)(2,1)S(1)}, bf16[4,128,768]{2,1,0:T(8,128)(2,1)S(1)}, u32[]{:S(2)}, u32[]{:S(2)}) collective-permute-start(bf16[4,128,768]{2,1,0:T(8,128)(2,1)S(1)} %all-to-all-done.4.refs_2_), channel_id=1, source_target_pairs={{0,16},{16,0},{1,17},{17,1},{2,18},{18,2},{3,19},{19,3},{4,20},{20... | collective-permute-start | bytes 2359304 | tf_op jit(solution)/shard_map/ppermute | solution.py:20
  514.5 22.2 %collective-permute-start.37 = (bf16[64,2048]{1,0:T(8,128)(2,1)}, bf16[64,2048]{1,0:T(8,128)(2,1)}, u32[]{:S(2)}, u32[]{:S(2)}) collective-permute-start(bf16[64,2048]{1,0:T(8,128)(2,1)} %get-tuple-element.88), channel_id=1, source_target_pairs={{0,16},{16,0},{1,17},{17,1},{2,18},{18,2},{3,19},{19,3},{4,20},{20... | collective-permute-start | bytes 786440 | tf_op jit(solution)/shard_map/ppermute | solution.py:20
  524.9 34.2 %collective-permute-start.51 = (bf16[4,128,1024]{2,1,0:T(8,128)(2,1)S(1)}, bf16[4,128,1024]{2,1,0:T(8,128)(2,1)}, u32[]{:S(2)}, u32[]{:S(2)}) collective-permute-start(bf16[4,128,1024]{2,1,0:T(8,128)(2,1)S(1)} %all-to-all-done.6.refs_4_), channel_id=1, source_target_pairs={{0,16},{16,0},{1,17},{17,1},{2,18},{18,2},{3,19},{19,3},{4,20},{20... | collective-permute-start | bytes 3145736 | tf_op jit(solution)/shard_map/ppermute | solution.py:20
  544.3 25.4 %collective-permute-start.50 = (bf16[4,128,512]{2,1,0:T(8,128)(2,1)S(1)}, bf16[4,128,512]{2,1,0:T(8,128)(2,1)S(1)}, u32[]{:S(2)}, u32[]{:S(2)}) collective-permute-start(bf16[4,128,512]{2,1,0:T(8,128)(2,1)S(1)} %all-to-all-done.5.refs_0_), channel_id=1, source_target_pairs={{0,16},{16,0},{1,17},{17,1},{2,18},{18,2},{3,19},{19,3},{4,20},{20... | collective-permute-start | bytes 1572872 | tf_op jit(solution)/shard_map/ppermute | solution.py:20
  (101 other events, 788.7 us)
Sparse Core Ops, SparseCore 0:
  29.8 64.2 all-gather.3
  100.7 116.1 all-gather.5
  218.5 61.7 all-gather.7
  283.0 58.8 reduce-scatter.4
  344.7 60.2 reduce-scatter.6
  407.1 77.5 reduce-scatter.8
  487.7 44.3 reduce-scatter.10

commit v6 on v5

--- a/solution.py
+++ b/solution.py
@@ -433,10 +433,6 @@
         grad_mid_b, owns[-1] = after(grad_mid.astype(BF16), owns[-1])
         grad_mid_b = plane_gather(grad_mid_b)
         act = jnp.concatenate(acts, 1)
-        act, grad_mid_b = lax.optimization_barrier((act, grad_mid_b))
-        down = jnp.concatenate(downs, 1)
-        mlp_out = plane_scatter(lambda i, j: contract_cols(act[i:j], down), own_tokens)
-        output = (mid + mlp_out).astype(BF16)
         attended_gradient = dot(grad_mid_b, w_o_cols).astype(BF16)
         own_o = contract_rows(grad_mid_b, attended_rows).astype(BF16)
         last_own = jnp.concatenate([owns[-1], own_o], 1)
@@ -460,6 +456,10 @@
         )
         qkv_rows = queue_scatter(own_qkv)
         mlp_grads[-1] = hand_out(mlp_rows[-1])
+        act, mlp_grads[-1] = after(act, mlp_grads[-1])
+        down = jnp.concatenate(downs, 1)
+        mlp_out = plane_scatter(lambda i, j: contract_cols(act[i:j], down), own_tokens)
+        output = (mid + mlp_out).astype(BF16)
         mlp_grads = [v if isinstance(v, tuple) else both_sides(v) for v in mlp_grads]
         qkv_rows, mlp_grads[1:-1] = after(qkv_rows, mlp_grads[1:-1])
         qkv_pair = both_sides(hand_out(qkv_rows))

time: 588 us -> 613 us (1.043)
  waiting for transfers between devices: 283 us -> 311 us
    ppermute x21, waiting for transfers between devices: 88.4 us -> 95.9 us  [over_rep(): return lax.ppermute(v, 'rep', SWAP)]
    reduce_scatter x4, waiting for transfers between devices: 0.47 us -> 7.95 us  [queue_scatter(): return lax.psum_scatter(parts, 'far', scatter_dimension=0, tiled=True)]
    ppermute x17, waiting for transfers between devices: 81.2 us -> 88.2 us  [over_mid(): return lax.ppermute(v, 'mid', SWAP)]
    unnamed x151 -> x143, local copies, waits for them, and re-layouts: 25.3 us -> 25.1 us
  transfers between devices with their start and end apart: 66 -> 66, of which waited for: 39 -> 42; matrix products, arithmetic and copies ran while one was open for 27% -> 25% of each run, Pallas kernels for 5% -> 4%
where the time goes in v6:
time: 613 us; the launch traced here: 604 us
  waiting for transfers between devices  311 us (51%)
  matrix products  92.4 us (15%)
  starting transfers between devices  77 us (13%)
  local copies, waits for them, and re-layouts  54.7 us (9%)
  Pallas kernels  29.1 us (5%)
  other arithmetic  23.2 us (4%)
  between operations  15.8 us (3%)
    ppermute x21, waiting for transfers between devices, over_rep(): return lax.ppermute(v, 'rep', SWAP)  95.9 us
    ppermute x17, waiting for transfers between devices, over_mid(): return lax.ppermute(v, 'mid', SWAP)  88.2 us
    all_gather x3, waiting for transfers between devices, gather_rows(): lax.all_gather(blocks.reshape(four * rows, n), 'far', axis=0, tiled=True)  65.4 us
    dot_general x10, matrix products, contract_cols(): lax.dot_general(left, right, (((1,), (1,)), ((), ())), preferred_element_...  34.8 us
    ppermute x21, starting transfers between devices, over_rep(): return lax.ppermute(v, 'rep', SWAP)  32.2 us
    dot_general x8, matrix products, dot(): return jnp.dot(left, right, preferred_element_type=F32)  32.1 us
    all_to_all x7, starting transfers between devices, trade(): return lax.all_to_all(blocks, ('mid', 'near'), 0, 0)  26 us
    dot_general x8, matrix products, contract_rows(): lax.dot_general(left, right, (((0,), (0,)), ((), ())), preferred_element_...  25.5 us
  transfers between devices with their start and end apart: 66, of which 42 were waited for; matrix products, arithmetic and copies ran while one was open for 25% of the time, Pallas kernels for 4%

profile of v6, /device:TPU:0, one launch (start us, length us, event | category | flops | bytes accessed | tf_op | source)
XLA Modules:
  0.0 603.6 jit_solution(15090142829677831647)
XLA Ops:
  20.9 7.9 %all-to-all-done = bf16[4,128,768]{2,1,0:T(8,128)(2,1)S(1)} async-done(((bf16[4,128,768]{2,1,0:T(8,128)(2,1)}), bf16[4,128,768]{2,1,0:T(8,128)(2,1)S(1)}, u32[]{:S(2)}, u32[]{:S(2)}) %all-to-all-start) | async-done | bytes 786464 | tf_op jit(solution)/shard_map/all_to_all | solution.py:96
  33.9 6.1 %collective-permute-done.9 = bf16[128,2048]{1,0:T(8,128)(2,1)S(1)} collective-permute-done((bf16[128,2048]{1,0:T(8,128)(2,1)S(1)}, bf16[128,2048]{1,0:T(8,128)(2,1)S(1)}, u32[]{:S(2)}, u32[]{:S(2)}) %collective-permute-start.9) | collective-permute-done | bytes 524320 | tf_op jit(solution)/shard_map/ppermute | solution.py:24
  42.3 9.0 %collective-permute-done.1 = bf16[128,2048]{1,0:T(8,128)(2,1)S(1)} collective-permute-done((bf16[128,2048]{1,0:T(8,128)(2,1)S(1)}, bf16[128,2048]{1,0:T(8,128)(2,1)S(1)}, u32[]{:S(2)}, u32[]{:S(2)}) %collective-permute-start.1) | collective-permute-done | bytes 524320 | tf_op jit(solution)/shard_map/ppermute | solution.py:24
  74.3 18.0 %collective-permute-done.6 = s32[2,256]{1,0:T(2,128)S(1)} collective-permute-done((s32[2,256]{1,0:T(2,128)S(1)}, s32[2,256]{1,0:T(2,128)S(1)}, u32[]{:S(2)}, u32[]{:S(2)}) %collective-permute-start.6) | collective-permute-done | bytes 2080 | tf_op jit(solution)/shard_map/ppermute | solution.py:24
  107.0 6.0 fusion.12.proj_ref
  113.1 8.0 %attention_forward.1.attended_ref = bf16[1024,256]{1,0:T(8,128)(2,1)S(1)} custom-call(f32[1024,512]{1,0:T(8,128)S(1)} %fusion.12.proj_ref, f32[1024,128]{1,0:T(8,128)S(1)} %get-tuple-element.179.cosine_ref, f32[1024,128]{1,0:T(8,128)S(1)} %get-tuple-element.180.sine_ref, s32[1024,1]{1,0:T(8,128)S(1)} %copy-done.3, s32[8,1,128]{2,1,0:T(1,128)S(1)} %bitcast.40, ...), custom_call_target="tpu_custom_call" | custom-call | tf_op jit(solution)/shard_map/attention_forward/pallas_call | solution.py:247
  129.1 12.1 %collective-permute-done.14 = bf16[128,2048]{1,0:T(8,128)(2,1)S(1)} collective-permute-done((bf16[128,2048]{1,0:T(8,128)(2,1)S(1)}, bf16[128,2048]{1,0:T(8,128)(2,1)S(1)}, u32[]{:S(2)}, u32[]{:S(2)}) %collective-permute-start.14) | collective-permute-done | bytes 524320 | tf_op jit(solution)/shard_map/ppermute | solution.py:20
  142.8 6.5 %collective-permute-done.15 = bf16[64,2048]{1,0:T(8,128)(2,1)S(1)} collective-permute-done((bf16[64,2048]{1,0:T(8,128)(2,1)S(1)}, bf16[64,2048]{1,0:T(8,128)(2,1)S(1)}, u32[]{:S(2)}, u32[]{:S(2)}) %collective-permute-start.15) | collective-permute-done | bytes 262176 | tf_op jit(solution)/shard_map/ppermute | solution.py:24
  151.0 5.7 collective-permute-done.17
  166.2 8.2 %collective-permute-done.19 = bf16[128,2048]{1,0:T(8,128)(2,1)} collective-permute-done((bf16[128,2048]{1,0:T(8,128)(2,1)}, bf16[128,2048]{1,0:T(8,128)(2,1)}, u32[]{:S(2)}, u32[]{:S(2)}) %collective-permute-start.19) | collective-permute-done | bytes 524320 | tf_op jit(solution)/shard_map/ppermute | solution.py:24
  196.6 20.3 %all-gather.6.cloned.1.call-done = bf16[2048,1536]{1,0:T(8,128)(2,1)} async-done(((bf16[512,1536]{1,0:T(8,128)(2,1)}), bf16[2048,1536]{1,0:T(8,128)(2,1)}) %all-gather.6.cloned.1.call-update) | async-done | bytes 6291472 | tf_op jit(solution)/shard_map/all_gather | solution.py:101
  216.9 5.2 fusion.7
  235.2 45.1 %all-gather.8.cloned.1.call-done = bf16[2048,768]{1,0:T(8,128)(2,1)} async-done(((bf16[512,768]{1,0:T(8,128)(2,1)}), bf16[2048,768]{1,0:T(8,128)(2,1)}) %all-gather.8.cloned.1.call-update) | async-done | bytes 3145744 | tf_op jit(solution)/shard_map/all_gather | solution.py:101
  327.5 8.7 %collective-permute-done.24 = bf16[128,2048]{1,0:T(8,128)(2,1)S(1)} collective-permute-done((bf16[128,2048]{1,0:T(8,128)(2,1)S(1)}, bf16[128,2048]{1,0:T(8,128)(2,1)S(1)}, u32[]{:S(2)}, u32[]{:S(2)}) %collective-permute-start.24) | collective-permute-done | bytes 524320 | tf_op jit(solution)/shard_map/ppermute | solution.py:20
  347.5 6.0 collective-permute-done.27
  358.5 9.1 %collective-permute-done.29 = bf16[128,2048]{1,0:T(8,128)(2,1)S(1)} collective-permute-done((bf16[128,2048]{1,0:T(8,128)(2,1)S(1)}, bf16[128,2048]{1,0:T(8,128)(2,1)S(1)}, u32[]{:S(2)}, u32[]{:S(2)}) %collective-permute-start.29) | collective-permute-done | bytes 524320 | tf_op jit(solution)/shard_map/ppermute | solution.py:24
  381.9 11.2 %attention_backward.1 = (bf16[1024,512]{1,0:T(8,128)(2,1)S(1)}, f32[8,128]{1,0:T(8,128)S(1)}) custom-call(f32[1024,512]{1,0:T(8,128)S(1)} %fusion.12.proj_ref, f32[1024,128]{1,0:T(8,128)S(1)} %get-tuple-element.179.cosine_ref, f32[1024,128]{1,0:T(8,128)S(1)} %get-tuple-element.180.sine_ref, s32[1024,1]{1,0:T(8,128)S(1)} %copy-done.4, ...), custom_call_target="tpu_custom_call" | custom-call | tf_op jit(solution)/shard_map/attention_backward/pallas_call | solution.py:320
  405.7 12.4 %collective-permute-done.34 = bf16[128,2048]{1,0:T(8,128)(2,1)S(1)} collective-permute-done((bf16[128,2048]{1,0:T(8,128)(2,1)S(1)}, bf16[128,2048]{1,0:T(8,128)(2,1)S(1)}, u32[]{:S(2)}, u32[]{:S(2)}) %collective-permute-start.34) | collective-permute-done | bytes 524320 | tf_op jit(solution)/shard_map/ppermute | solution.py:20
  419.8 6.5 %collective-permute-done.35 = bf16[64,2048]{1,0:T(8,128)(2,1)S(1)} collective-permute-done((bf16[64,2048]{1,0:T(8,128)(2,1)S(1)}, bf16[64,2048]{1,0:T(8,128)(2,1)S(1)}, u32[]{:S(2)}, u32[]{:S(2)}) %collective-permute-start.35) | collective-permute-done | bytes 262176 | tf_op jit(solution)/shard_map/ppermute | solution.py:24
  427.9 5.7 collective-permute-done.37
  443.7 5.9 convolution_convert_fusion.3
  458.9 6.6 %collective-permute-done.41 = f32[1,4352]{1,0:T(1,128)S(1)} collective-permute-done((f32[1,4352]{1,0:T(1,128)S(1)}, f32[1,4352]{1,0:T(1,128)S(1)}, u32[]{:S(2)}, u32[]{:S(2)}) %collective-permute-start.41) | collective-permute-done | bytes 17440 | tf_op jit(solution)/shard_map/ppermute | solution.py:159
  472.4 5.9 collective-permute-done.43.refs_1_
  478.3 6.5 %reduce-scatter.9.cloned.1.call-done = bf16[512,1024]{0,1:T(8,128)(2,1)} async-done(((bf16[2048,1024]{0,1:T(8,128)(2,1)}), bf16[512,1024]{0,1:T(8,128)(2,1)}) %reduce-scatter.9.cloned.1.call-update) | async-done | bytes 1048592 | tf_op jit(solution)/shard_map/reduce_scatter | solution.py:105
  497.6 7.4 %all-to-all-done.5.refs_4_ = bf16[4,128,1024]{2,1,0:T(8,128)(2,1)S(1)} async-done(((bf16[4,128,1024]{2,1,0:T(8,128)(2,1)}), bf16[4,128,1024]{2,1,0:T(8,128)(2,1)S(1)}, u32[]{:S(2)}, u32[]{:S(2)}) %all-to-all-start.5) | async-done | bytes 1048608 | tf_op jit(solution)/shard_map/all_to_all | solution.py:96
  505.0 5.3 convolution_convert_fusion.5
  522.2 12.6 %collective-permute-done.45 = bf16[128,2048]{1,0:T(8,128)(2,1)S(1)} collective-permute-done((bf16[128,2048]{1,0:T(8,128)(2,1)S(1)}, bf16[128,2048]{1,0:T(8,128)(2,1)S(1)}, u32[]{:S(2)}, u32[]{:S(2)}) %collective-permute-start.45) | collective-permute-done | bytes 524320 | tf_op jit(solution)/shard_map/ppermute | solution.py:20
  535.6 6.2 %collective-permute-done.46 = bf16[64,2048]{1,0:T(8,128)(2,1)S(1)} collective-permute-done((bf16[64,2048]{1,0:T(8,128)(2,1)S(1)}, bf16[64,2048]{1,0:T(8,128)(2,1)S(1)}, u32[]{:S(2)}, u32[]{:S(2)}) %collective-permute-start.46) | collective-permute-done | bytes 262176 | tf_op jit(solution)/shard_map/ppermute | solution.py:24
  544.1 7.5 %collective-permute-done.49.refs_3_ = bf16[4,128,768]{2,1,0:T(8,128)(2,1)S(1)} collective-permute-done((bf16[4,128,768]{2,1,0:T(8,128)(2,1)S(1)}, bf16[4,128,768]{2,1,0:T(8,128)(2,1)S(1)}, u32[]{:S(2)}, u32[]{:S(2)}) %collective-permute-start.49) | collective-permute-done | bytes 786464 | tf_op jit(solution)/shard_map/ppermute | solution.py:20
  560.1 6.2 %all-to-all-done.6.refs_0_ = bf16[4,128,512]{2,1,0:T(8,128)(2,1)S(1)} async-done(((bf16[4,128,512]{2,1,0:T(8,128)(2,1)}), bf16[4,128,512]{2,1,0:T(8,128)(2,1)S(1)}, u32[]{:S(2)}, u32[]{:S(2)}) %all-to-all-start.6) | async-done | bytes 524320 | tf_op jit(solution)/shard_map/all_to_all | solution.py:96
  571.3 12.8 %collective-permute-done.51.refs_5_ = bf16[4,128,1024]{2,1,0:T(8,128)(2,1)} collective-permute-done((bf16[4,128,1024]{2,1,0:T(8,128)(2,1)S(1)}, bf16[4,128,1024]{2,1,0:T(8,128)(2,1)}, u32[]{:S(2)}, u32[]{:S(2)}) %collective-permute-start.51) | collective-permute-done | bytes 1048608 | tf_op jit(solution)/shard_map/ppermute | solution.py:20
  584.1 5.9 spread.3
  (367 shorter events, 281.2 us)
Async XLA Ops:
  12.2 16.6 %all-to-all-start = ((bf16[4,128,768]{2,1,0:T(8,128)(2,1)}), bf16[4,128,768]{2,1,0:T(8,128)(2,1)S(1)}, u32[]{:S(2)}, u32[]{:S(2)}) async-start(bf16[4,128,768]{2,1,0:T(8,128)(2,1)} %pick_columns.2), calls=%async_computation | async-start | bytes 1572864 | tf_op jit(solution)/shard_map/all_to_all | solution.py:96
  16.5 90.6 %all-gather.4.cloned.1.call-start = ((), (), s32[]{:S(2)}) async-start(), calls=%async_computation.11 | async-start | bytes 3932160 | tf_op jit(solution)/shard_map/all_gather | solution.py:101
  16.5 23.6 %collective-permute-start.9 = (bf16[128,2048]{1,0:T(8,128)(2,1)S(1)}, bf16[128,2048]{1,0:T(8,128)(2,1)S(1)}, u32[]{:S(2)}, u32[]{:S(2)}) collective-permute-start(bf16[128,2048]{1,0:T(8,128)(2,1)S(1)} %copy-done.34), channel_id=1, source_target_pairs={{0,2},{2,0},{1,3},{3,1},{4,6},{6,4},{5,7},{7,5},{8,10},{10,8},{9,1... | collective-permute-start | bytes 1572872 | tf_op jit(solution)/shard_map/ppermute | solution.py:24
  18.8 23.3 %collective-permute-start.8 = (bf16[128,2048]{1,0:T(8,128)(2,1)S(1)}, bf16[128,2048]{1,0:T(8,128)(2,1)S(1)}, u32[]{:S(2)}, u32[]{:S(2)}) collective-permute-start(bf16[128,2048]{1,0:T(8,128)(2,1)S(1)} %copy-done.34), channel_id=1, source_target_pairs={{0,16},{16,0},{1,17},{17,1},{2,18},{18,2},{3,19},{19,3},{4,20},{20... | collective-permute-start | bytes 1572872 | tf_op jit(solution)/shard_map/ppermute | solution.py:20
  30.7 20.6 %collective-permute-start.1 = (bf16[128,2048]{1,0:T(8,128)(2,1)S(1)}, bf16[128,2048]{1,0:T(8,128)(2,1)S(1)}, u32[]{:S(2)}, u32[]{:S(2)}) collective-permute-start(bf16[128,2048]{1,0:T(8,128)(2,1)S(1)} %get-tuple-element.82), channel_id=1, source_target_pairs={{0,2},{2,0},{1,3},{3,1},{4,6},{6,4},{5,7},{7,5},{8,10},{10,8},{9,1... | collective-permute-start | bytes 1572872 | tf_op jit(solution)/shard_map/ppermute | solution.py:24
  30.7 22.6 %collective-permute-start = (bf16[128,2048]{1,0:T(8,128)(2,1)S(1)}, bf16[128,2048]{1,0:T(8,128)(2,1)S(1)}, u32[]{:S(2)}, u32[]{:S(2)}) collective-permute-start(bf16[128,2048]{1,0:T(8,128)(2,1)S(1)} %get-tuple-element.82), channel_id=1, source_target_pairs={{0,16},{16,0},{1,17},{17,1},{2,18},{18,2},{3,19},{19,3},{4,20},{20... | collective-permute-start | bytes 1572872 | tf_op jit(solution)/shard_map/ppermute | solution.py:20
  40.1 24.2 %collective-permute-start.11 = (bf16[64,2048]{1,0:T(8,128)(2,1)S(1)}, bf16[64,2048]{1,0:T(8,128)(2,1)S(1)}, u32[]{:S(2)}, u32[]{:S(2)}) collective-permute-start(bf16[64,2048]{1,0:T(8,128)(2,1)S(1)} %slice.461), channel_id=1, source_target_pairs={{0,16},{16,0},{1,17},{17,1},{2,18},{18,2},{3,19},{19,3},{4,20},{20... | collective-permute-start | bytes 786440 | tf_op jit(solution)/shard_map/ppermute | solution.py:20
  42.1 21.2 %collective-permute-start.10 = (bf16[64,2048]{1,0:T(8,128)(2,1)S(1)}, bf16[64,2048]{1,0:T(8,128)(2,1)S(1)}, u32[]{:S(2)}, u32[]{:S(2)}) collective-permute-start(bf16[64,2048]{1,0:T(8,128)(2,1)S(1)} %slice.460), channel_id=1, source_target_pairs={{0,2},{2,0},{1,3},{3,1},{4,6},{6,4},{5,7},{7,5},{8,10},{10,8},{9,1... | collective-permute-start | bytes 786440 | tf_op jit(solution)/shard_map/ppermute | solution.py:24
  63.3 37.3 %collective-permute-start.4 = (bf16[512,2048]{1,0:T(8,128)(2,1)}, bf16[512,2048]{1,0:T(8,128)(2,1)}, u32[]{:S(2)}, u32[]{:S(2)}) collective-permute-start(bf16[512,2048]{1,0:T(8,128)(2,1)} %get-tuple-element.150), channel_id=1, source_target_pairs={{0,1},{1,0},{2,3},{3,2},{4,5},{5,4},{6,7},{7,6},{8,9},{9,8},{10,11... | collective-permute-start | bytes 6291464 | tf_op jit(solution)/shard_map/ppermute | solution.py:28
  65.7 38.1 %collective-permute-start.12 = (bf16[512,2048]{1,0:T(8,128)(2,1)}, bf16[512,2048]{1,0:T(8,128)(2,1)}, u32[]{:S(2)}, u32[]{:S(2)}) collective-permute-start(bf16[512,2048]{1,0:T(8,128)(2,1)} %get-tuple-element.146), channel_id=1, source_target_pairs={{0,1},{1,0},{2,3},{3,2},{4,5},{5,4},{6,7},{7,6},{8,9},{9,8},{10,11... | collective-permute-start | bytes 6291464 | tf_op jit(solution)/shard_map/ppermute | solution.py:28
  68.6 30.8 %all-to-all-start.1 = ((bf16[4,128,1536]{2,1,0:T(8,128)(2,1)}), bf16[4,128,1536]{2,1,0:T(8,128)(2,1)S(1)}, u32[]{:S(2)}, u32[]{:S(2)}) async-start(bf16[4,128,1536]{2,1,0:T(8,128)(2,1)} %get-tuple-element.43), calls=%async_computation.1 | async-start | bytes 3145728 | tf_op jit(solution)/shard_map/all_to_all | solution.py:96
  72.2 144.7 %all-gather.6.cloned.1.call-start = ((), (), s32[]{:S(2)}) async-start(), calls=%async_computation.12 | async-start | bytes 7864320 | tf_op jit(solution)/shard_map/all_gather | solution.py:101
  72.3 20.0 %collective-permute-start.6 = (s32[2,256]{1,0:T(2,128)S(1)}, s32[2,256]{1,0:T(2,128)S(1)}, u32[]{:S(2)}, u32[]{:S(2)}) collective-permute-start(s32[2,256]{1,0:T(2,128)S(1)} %pad_add_fusion.1), channel_id=1, source_target_pairs={{0,2},{2,0},{1,3},{3,1},{4,6},{6,4},{5,7},{7,5},{8,10},{10,8},{9,1... | collective-permute-start | bytes 6152 | tf_op jit(solution)/shard_map/ppermute | solution.py:24
  159.1 15.2 %collective-permute-start.19 = (bf16[128,2048]{1,0:T(8,128)(2,1)}, bf16[128,2048]{1,0:T(8,128)(2,1)}, u32[]{:S(2)}, u32[]{:S(2)}) collective-permute-start(bf16[128,2048]{1,0:T(8,128)(2,1)} %get-tuple-element.78), channel_id=1, source_target_pairs={{0,2},{2,0},{1,3},{3,1},{4,6},{6,4},{5,7},{7,5},{8,10},{10,8},{9,1... | collective-permute-start | bytes 1572872 | tf_op jit(solution)/shard_map/ppermute | solution.py:24
  159.7 16.2 %collective-permute-start.18 = (bf16[128,2048]{1,0:T(8,128)(2,1)}, bf16[128,2048]{1,0:T(8,128)(2,1)}, u32[]{:S(2)}, u32[]{:S(2)}) collective-permute-start(bf16[128,2048]{1,0:T(8,128)(2,1)} %get-tuple-element.78), channel_id=1, source_target_pairs={{0,16},{16,0},{1,17},{17,1},{2,18},{18,2},{3,19},{19,3},{4,20},{20... | collective-permute-start | bytes 1572872 | tf_op jit(solution)/shard_map/ppermute | solution.py:20
  160.8 28.1 %all-to-all-start.2 = ((bf16[4,128,768]{2,1,0:T(8,128)(2,1)}), bf16[4,128,768]{2,1,0:T(8,128)(2,1)}, u32[]{:S(2)}, u32[]{:S(2)}) async-start(bf16[4,128,768]{2,1,0:T(8,128)(2,1)} %copy-done.7), calls=%async_computation.2 | async-start | bytes 1572864 | tf_op jit(solution)/shard_map/all_to_all | solution.py:96
  165.0 115.3 %all-gather.8.cloned.1.call-start = ((), (), s32[]{:S(2)}) async-start(), calls=%async_computation.13 | async-start | bytes 3932160 | tf_op jit(solution)/shard_map/all_gather | solution.py:101
  188.9 248.5 %reduce-scatter.5.cloned.1.call-start = ((), (), s32[]{:S(2)}) async-start(), calls=%async_computation.14 | async-start | bytes 3932160 | tf_op jit(solution)/shard_map/reduce_scatter | solution.py:105
  280.4 169.2 %reduce-scatter.7.cloned.1.call-start = ((), (), s32[]{:S(2)}) async-start(), calls=%async_computation.15 | async-start | bytes 3932160 | tf_op jit(solution)/shard_map/reduce_scatter | solution.py:105
  316.5 168.3 %reduce-scatter.9.cloned.1.call-start = ((), (), s32[]{:S(2)}) async-start(), calls=%async_computation.16 | async-start | bytes 5242880 | tf_op jit(solution)/shard_map/reduce_scatter | solution.py:105
  326.0 15.5 %collective-permute-start.26 = (bf16[128,2048]{1,0:T(8,128)(2,1)S(1)}, bf16[128,2048]{1,0:T(8,128)(2,1)S(1)}, u32[]{:S(2)}, u32[]{:S(2)}) collective-permute-start(bf16[128,2048]{1,0:T(8,128)(2,1)S(1)} %pad_maximum_fusion.25), channel_id=1, source_target_pairs={{0,2},{2,0},{1,3},{3,1},{4,6},{6,4},{5,7},{7,5},{8,10},{10,8},{9,1... | collective-permute-start | bytes 1572872 | tf_op jit(solution)/shard_map/ppermute | solution.py:24
  439.7 15.1 %all-to-all-start.3 = ((bf16[4,128,768]{2,1,0:T(8,128)(2,1)}), bf16[4,128,768]{2,1,0:T(8,128)(2,1)S(1)}, u32[]{:S(2)}, u32[]{:S(2)}) async-start(bf16[4,128,768]{2,1,0:T(8,128)(2,1)} %bitcast.11), calls=%async_computation.4 | async-start | bytes 1572864 | tf_op jit(solution)/shard_map/all_to_all | solution.py:96
  443.3 15.5 %collective-permute-start.40 = (f32[1,4352]{1,0:T(1,128)S(1)}, f32[1,4352]{1,0:T(1,128)S(1)}, u32[]{:S(2)}, u32[]{:S(2)}) collective-permute-start(f32[1,4352]{1,0:T(1,128)S(1)} %add.197), channel_id=1, source_target_pairs={{0,16},{16,0},{1,17},{17,1},{2,18},{18,2},{3,19},{19,3},{4,20},{20... | collective-permute-start | bytes 52232 | tf_op jit(solution)/shard_map/ppermute | solution.py:154
  454.8 17.6 %all-to-all-start.4 = ((bf16[4,128,768]{2,1,0:T(8,128)(2,1)}), bf16[4,128,768]{2,1,0:T(8,128)(2,1)S(1)}, u32[]{:S(2)}, u32[]{:S(2)}) async-start(bf16[4,128,768]{2,1,0:T(8,128)(2,1)} %bitcast.12), calls=%async_computation.6 | async-start | bytes 1572864 | tf_op jit(solution)/shard_map/all_to_all | solution.py:96
  458.3 19.9 %collective-permute-start.43 = (bf16[4,128,768]{2,1,0:T(8,128)(2,1)S(1)}, bf16[4,128,768]{2,1,0:T(8,128)(2,1)S(1)}, u32[]{:S(2)}, u32[]{:S(2)}) collective-permute-start(bf16[4,128,768]{2,1,0:T(8,128)(2,1)S(1)} %all-to-all-done.3.refs_0_), channel_id=1, source_target_pairs={{0,16},{16,0},{1,17},{17,1},{2,18},{18,2},{3,19},{19,3},{4,20},{20... | collective-permute-start | bytes 2359304 | tf_op jit(solution)/shard_map/ppermute | solution.py:20
  487.0 18.0 %all-to-all-start.5 = ((bf16[4,128,1024]{2,1,0:T(8,128)(2,1)}), bf16[4,128,1024]{2,1,0:T(8,128)(2,1)S(1)}, u32[]{:S(2)}, u32[]{:S(2)}) async-start(bf16[4,128,1024]{2,1,0:T(8,128)(2,1)} %bitcast.47), calls=%async_computation.8 | async-start | bytes 2097152 | tf_op jit(solution)/shard_map/all_to_all | solution.py:96
  490.5 63.4 %reduce-scatter.11.cloned.1.call-start = ((), (), s32[]{:S(2)}) async-start(), calls=%async_computation.17 | async-start | bytes 2621440 | tf_op jit(solution)/shard_map/reduce_scatter | solution.py:105
  519.9 14.8 %collective-permute-start.45 = (bf16[128,2048]{1,0:T(8,128)(2,1)S(1)}, bf16[128,2048]{1,0:T(8,128)(2,1)S(1)}, u32[]{:S(2)}, u32[]{:S(2)}) collective-permute-start(bf16[128,2048]{1,0:T(8,128)(2,1)S(1)} %pad_maximum_fusion.28), channel_id=1, source_target_pairs={{0,16},{16,0},{1,17},{17,1},{2,18},{18,2},{3,19},{19,3},{4,20},{20... | collective-permute-start | bytes 1572872 | tf_op jit(solution)/shard_map/ppermute | solution.py:20
  521.5 30.2 %collective-permute-start.49 = (bf16[4,128,768]{2,1,0:T(8,128)(2,1)S(1)}, bf16[4,128,768]{2,1,0:T(8,128)(2,1)S(1)}, u32[]{:S(2)}, u32[]{:S(2)}) collective-permute-start(bf16[4,128,768]{2,1,0:T(8,128)(2,1)S(1)} %all-to-all-done.4.refs_2_), channel_id=1, source_target_pairs={{0,16},{16,0},{1,17},{17,1},{2,18},{18,2},{3,19},{19,3},{4,20},{20... | collective-permute-start | bytes 2359304 | tf_op jit(solution)/shard_map/ppermute | solution.py:20
  542.7 25.1 %collective-permute-start.48 = (bf16[64,2048]{1,0:T(8,128)(2,1)S(1)}, bf16[64,2048]{1,0:T(8,128)(2,1)}, u32[]{:S(2)}, u32[]{:S(2)}) collective-permute-start(bf16[64,2048]{1,0:T(8,128)(2,1)S(1)} %get-tuple-element.86), channel_id=1, source_target_pairs={{0,16},{16,0},{1,17},{17,1},{2,18},{18,2},{3,19},{19,3},{4,20},{20... | collective-permute-start | bytes 786440 | tf_op jit(solution)/shard_map/ppermute | solution.py:20
  558.1 26.1 %collective-permute-start.51 = (bf16[4,128,1024]{2,1,0:T(8,128)(2,1)S(1)}, bf16[4,128,1024]{2,1,0:T(8,128)(2,1)}, u32[]{:S(2)}, u32[]{:S(2)}) collective-permute-start(bf16[4,128,1024]{2,1,0:T(8,128)(2,1)S(1)} %all-to-all-done.5.refs_4_), channel_id=1, source_target_pairs={{0,16},{16,0},{1,17},{17,1},{2,18},{18,2},{3,19},{19,3},{4,20},{20... | collective-permute-start | bytes 3145736 | tf_op jit(solution)/shard_map/ppermute | solution.py:20
  566.3 28.6 %collective-permute-start.50 = (bf16[4,128,512]{2,1,0:T(8,128)(2,1)S(1)}, bf16[4,128,512]{2,1,0:T(8,128)(2,1)S(1)}, u32[]{:S(2)}, u32[]{:S(2)}) collective-permute-start(bf16[4,128,512]{2,1,0:T(8,128)(2,1)S(1)} %all-to-all-done.6.refs_0_), channel_id=1, source_target_pairs={{0,16},{16,0},{1,17},{17,1},{2,18},{18,2},{3,19},{19,3},{4,20},{20... | collective-permute-start | bytes 1572872 | tf_op jit(solution)/shard_map/ppermute | solution.py:20
  (97 other events, 742.3 us)
Sparse Core Ops, SparseCore 0:
  29.8 64.2 all-gather.3
  100.7 116.1 all-gather.5
  218.5 61.7 all-gather.7
  283.1 58.8 reduce-scatter.4
  344.7 60.2 reduce-scatter.6
  407.2 77.5 reduce-scatter.8
  510.4 43.5 reduce-scatter.10

commit v7 on v5

--- a/solution.py
+++ b/solution.py
@@ -405,7 +405,7 @@
         for number, three in enumerate(mlp_weights):
             block = chunks[number][1]
             if number == 2:
-                three, owns[0] = after(three, owns[0])
+                three, owns[0], acts[-1] = after(three, owns[0], acts[-1])
             weight = three[:, : 2 * block]
             pre = dot(mlp_in, weight)
             gate_pre, up_pre = pre[:, :block], pre[:, block:]

time: 588 us -> 601 us (1.022)
  blocking collectives: 0 us -> 14.8 us
  local copies, waits for them, and re-layouts: 52.4 us -> 45.6 us
  matrix products: 89.8 us -> 96.5 us
    all_to_all x0 -> x1, blocking collectives: none -> 14.8 us  [trade(): return lax.all_to_all(blocks, ('mid', 'near'), 0, 0)]
    ppermute x17, waiting for transfers between devices: 81.2 us -> 70.1 us  [over_mid(): return lax.ppermute(v, 'mid', SWAP)]
    ppermute x17, starting transfers between devices: 17.5 us -> 26.8 us  [over_mid(): return lax.ppermute(v, 'mid', SWAP)]
    reduce_scatter x4, waiting for transfers between devices: 0.47 us -> 8.01 us  [queue_scatter(): return lax.psum_scatter(parts, 'far', scatter_dimension=0, tiled=True)]
    ppermute x21, starting transfers between devices: 33.2 us -> 26.4 us  [over_rep(): return lax.ppermute(v, 'rep', SWAP)]
    all_gather x3, waiting for transfers between devices: 65.3 us -> 71.7 us  [gather_rows(): lax.all_gather(blocks.reshape(four * rows, n), 'far', axis=0, tiled=True)]
    all_to_all x7 -> x6, starting transfers between devices: 26 us -> 22 us  [trade(): return lax.all_to_all(blocks, ('mid', 'near'), 0, 0)]
    unnamed x151 -> x149, local copies, waits for them, and re-layouts: 25.3 us -> 22.5 us
  transfers between devices with their start and end apart: 66 -> 65, of which waited for: 39 -> 38; matrix products, arithmetic and copies ran while one was open for 27% -> 27% of each run, Pallas kernels for 5% -> 5%
where the time goes in v7:
time: 601 us; the launch traced here: 592 us
  waiting for transfers between devices  283 us (47%)
  matrix products  96.5 us (16%)
  starting transfers between devices  80.6 us (13%)
  local copies, waits for them, and re-layouts  45.6 us (8%)
  Pallas kernels  29.1 us (5%)
  other arithmetic  27.2 us (5%)
  between operations  15.6 us (3%)
  blocking collectives  14.8 us (2%)
    ppermute x21, waiting for transfers between devices, over_rep(): return lax.ppermute(v, 'rep', SWAP)  92.5 us
    all_gather x3, waiting for transfers between devices, gather_rows(): lax.all_gather(blocks.reshape(four * rows, n), 'far', axis=0, tiled=True)  71.7 us
    ppermute x17, waiting for transfers between devices, over_mid(): return lax.ppermute(v, 'mid', SWAP)  70.1 us
    dot_general x10, matrix products, contract_cols(): lax.dot_general(left, right, (((1,), (1,)), ((), ())), preferred_element_...  36.5 us
    dot_general x8, matrix products, dot(): return jnp.dot(left, right, preferred_element_type=F32)  34.3 us
    all_to_all x6, waiting for transfers between devices, trade(): return lax.all_to_all(blocks, ('mid', 'near'), 0, 0)  27 us
    ppermute x17, starting transfers between devices, over_mid(): return lax.ppermute(v, 'mid', SWAP)  26.8 us
    ppermute x21, starting transfers between devices, over_rep(): return lax.ppermute(v, 'rep', SWAP)  26.4 us
  transfers between devices with their start and end apart: 65, of which 38 were waited for; matrix products, arithmetic and copies ran while one was open for 27% of the time, Pallas kernels for 5%

profile of v7, /device:TPU:0, one launch (start us, length us, event | category | flops | bytes accessed | tf_op | source)
XLA Modules:
  0.0 592.0 jit_solution(3370312472633050813)
XLA Ops:
  24.1 8.4 %all-to-all-done = bf16[4,128,768]{2,1,0:T(8,128)(2,1)S(1)} async-done(((bf16[4,128,768]{2,1,0:T(8,128)(2,1)}), bf16[4,128,768]{2,1,0:T(8,128)(2,1)S(1)}, u32[]{:S(2)}, u32[]{:S(2)}) %all-to-all-start) | async-done | bytes 786464 | tf_op jit(solution)/shard_map/all_to_all | solution.py:96
  37.4 6.3 %collective-permute-done.1 = bf16[128,2048]{1,0:T(8,128)(2,1)S(1)} collective-permute-done((bf16[128,2048]{1,0:T(8,128)(2,1)S(1)}, bf16[128,2048]{1,0:T(8,128)(2,1)S(1)}, u32[]{:S(2)}, u32[]{:S(2)}) %collective-permute-start.1) | collective-permute-done | bytes 524320 | tf_op jit(solution)/shard_map/ppermute | solution.py:24
  67.7 18.1 %collective-permute-done.6 = s32[2,256]{1,0:T(2,128)S(1)} collective-permute-done((s32[2,256]{1,0:T(2,128)S(1)}, s32[2,256]{1,0:T(2,128)S(1)}, u32[]{:S(2)}, u32[]{:S(2)}) %collective-permute-start.6) | collective-permute-done | bytes 2080 | tf_op jit(solution)/shard_map/ppermute | solution.py:24
  98.2 5.2 fusion.12.proj_ref
  103.5 8.0 %attention_forward.1.attended_ref = bf16[1024,256]{1,0:T(8,128)(2,1)S(1)} custom-call(f32[1024,512]{1,0:T(8,128)S(1)} %fusion.12.proj_ref, f32[1024,128]{1,0:T(8,128)S(1)} %get-tuple-element.181.cosine_ref, f32[1024,128]{1,0:T(8,128)S(1)} %get-tuple-element.182.sine_ref, s32[1024,1]{1,0:T(8,128)S(1)} %copy-done.3, s32[8,1,128]{2,1,0:T(1,128)S(1)} %bitcast.40, ...), custom_call_target="tpu_custom_call" | custom-call | tf_op jit(solution)/shard_map/attention_forward/pallas_call | solution.py:247
  125.7 11.3 %collective-permute-done.14 = bf16[128,2048]{1,0:T(8,128)(2,1)S(1)} collective-permute-done((bf16[128,2048]{1,0:T(8,128)(2,1)S(1)}, bf16[128,2048]{1,0:T(8,128)(2,1)S(1)}, u32[]{:S(2)}, u32[]{:S(2)}) %collective-permute-start.14) | collective-permute-done | bytes 524320 | tf_op jit(solution)/shard_map/ppermute | solution.py:20
  138.2 6.5 %collective-permute-done.15 = bf16[64,2048]{1,0:T(8,128)(2,1)S(1)} collective-permute-done((bf16[64,2048]{1,0:T(8,128)(2,1)S(1)}, bf16[64,2048]{1,0:T(8,128)(2,1)S(1)}, u32[]{:S(2)}, u32[]{:S(2)}) %collective-permute-start.15) | collective-permute-done | bytes 262176 | tf_op jit(solution)/shard_map/ppermute | solution.py:24
  146.1 5.6 collective-permute-done.17
  155.9 8.7 %collective-permute-done.19 = bf16[128,2048]{1,0:T(8,128)(2,1)S(1)} collective-permute-done((bf16[128,2048]{1,0:T(8,128)(2,1)S(1)}, bf16[128,2048]{1,0:T(8,128)(2,1)S(1)}, u32[]{:S(2)}, u32[]{:S(2)}) %collective-permute-start.19) | collective-permute-done | bytes 524320 | tf_op jit(solution)/shard_map/ppermute | solution.py:24
  175.0 14.8 %all_to_all.35 = bf16[4,128,768]{2,1,0:T(8,128)(2,1)} all-to-all(bf16[4,128,768]{2,1,0:T(8,128)(2,1)S(1)} %copy-done.8), channel_id=1, replica_groups=mesh['rep'=2,'far'=4,'mid'=2,'near'=2] {'mid','near'}, dimensions={0} | all-to-all | bytes 1572864 | tf_op jit(solution)/shard_map/all_to_all | solution.py:96
  193.4 37.2 %all-gather.6.cloned.1.call-done = bf16[2048,1536]{1,0:T(8,128)(2,1)} async-done(((bf16[512,1536]{1,0:T(8,128)(2,1)}), bf16[2048,1536]{1,0:T(8,128)(2,1)}) %all-gather.6.cloned.1.call-update) | async-done | bytes 6291472 | tf_op jit(solution)/shard_map/all_gather | solution.py:101
  230.6 5.2 fusion.7
  248.9 5.2 fusion.3
  254.1 5.3 multiply_convert_fusion.1
  259.4 34.5 %all-gather.8.cloned.1.call-done = bf16[2048,768]{1,0:T(8,128)(2,1)} async-done(((bf16[512,768]{1,0:T(8,128)(2,1)}), bf16[2048,768]{1,0:T(8,128)(2,1)}) %all-gather.8.cloned.1.call-update) | async-done | bytes 3145744 | tf_op jit(solution)/shard_map/all_gather | solution.py:101
  301.1 4.9 multiply_convert_fusion.2
  322.8 5.1 fusion.98
  333.7 8.7 %collective-permute-done.24 = bf16[128,2048]{1,0:T(8,128)(2,1)S(1)} collective-permute-done((bf16[128,2048]{1,0:T(8,128)(2,1)S(1)}, bf16[128,2048]{1,0:T(8,128)(2,1)S(1)}, u32[]{:S(2)}, u32[]{:S(2)}) %collective-permute-start.24) | collective-permute-done | bytes 524320 | tf_op jit(solution)/shard_map/ppermute | solution.py:20
  353.7 6.1 %collective-permute-done.27 = bf16[64,2048]{1,0:T(8,128)(2,1)S(1)} collective-permute-done((bf16[64,2048]{1,0:T(8,128)(2,1)S(1)}, bf16[64,2048]{1,0:T(8,128)(2,1)S(1)}, u32[]{:S(2)}, u32[]{:S(2)}) %collective-permute-start.27) | collective-permute-done | bytes 262176 | tf_op jit(solution)/shard_map/ppermute | solution.py:20
  364.8 9.2 %collective-permute-done.29 = bf16[128,2048]{1,0:T(8,128)(2,1)S(1)} collective-permute-done((bf16[128,2048]{1,0:T(8,128)(2,1)S(1)}, bf16[128,2048]{1,0:T(8,128)(2,1)S(1)}, u32[]{:S(2)}, u32[]{:S(2)}) %collective-permute-start.29) | collective-permute-done | bytes 524320 | tf_op jit(solution)/shard_map/ppermute | solution.py:24
  388.3 11.2 %attention_backward.1 = (bf16[1024,512]{1,0:T(8,128)(2,1)S(1)}, f32[8,128]{1,0:T(8,128)S(1)}) custom-call(f32[1024,512]{1,0:T(8,128)S(1)} %fusion.12.proj_ref, f32[1024,128]{1,0:T(8,128)S(1)} %get-tuple-element.181.cosine_ref, f32[1024,128]{1,0:T(8,128)S(1)} %get-tuple-element.182.sine_ref, s32[1024,1]{1,0:T(8,128)S(1)} %copy-done.4, ...), custom_call_target="tpu_custom_call" | custom-call | tf_op jit(solution)/shard_map/attention_backward/pallas_call | solution.py:320
  412.1 12.4 %collective-permute-done.39 = bf16[128,2048]{1,0:T(8,128)(2,1)S(1)} collective-permute-done((bf16[128,2048]{1,0:T(8,128)(2,1)S(1)}, bf16[128,2048]{1,0:T(8,128)(2,1)S(1)}, u32[]{:S(2)}, u32[]{:S(2)}) %collective-permute-start.39) | collective-permute-done | bytes 524320 | tf_op jit(solution)/shard_map/ppermute | solution.py:20
  426.1 6.3 %collective-permute-done.40 = bf16[64,2048]{1,0:T(8,128)(2,1)S(1)} collective-permute-done((bf16[64,2048]{1,0:T(8,128)(2,1)S(1)}, bf16[64,2048]{1,0:T(8,128)(2,1)S(1)}, u32[]{:S(2)}, u32[]{:S(2)}) %collective-permute-start.40) | collective-permute-done | bytes 262176 | tf_op jit(solution)/shard_map/ppermute | solution.py:24
  434.1 5.5 collective-permute-done.42
  455.8 5.9 convolution_convert_fusion.3
  481.9 8.6 %collective-permute-done.48.refs_1_ = bf16[4,128,768]{2,1,0:T(8,128)(2,1)S(1)} collective-permute-done((bf16[4,128,768]{2,1,0:T(8,128)(2,1)S(1)}, bf16[4,128,768]{2,1,0:T(8,128)(2,1)S(1)}, u32[]{:S(2)}, u32[]{:S(2)}) %collective-permute-start.48) | collective-permute-done | bytes 786464 | tf_op jit(solution)/shard_map/ppermute | solution.py:20
  490.5 7.8 %reduce-scatter.9.cloned.1.call-done = bf16[512,1024]{0,1:T(8,128)(2,1)} async-done(((bf16[2048,1024]{0,1:T(8,128)(2,1)}), bf16[512,1024]{0,1:T(8,128)(2,1)}) %reduce-scatter.9.cloned.1.call-update) | async-done | bytes 1048592 | tf_op jit(solution)/shard_map/reduce_scatter | solution.py:105
  507.0 9.9 %collective-permute-done.34 = bf16[128,2048]{1,0:T(8,128)(2,1)S(1)} collective-permute-done((bf16[128,2048]{1,0:T(8,128)(2,1)S(1)}, bf16[128,2048]{1,0:T(8,128)(2,1)S(1)}, u32[]{:S(2)}, u32[]{:S(2)}) %collective-permute-start.34) | collective-permute-done | bytes 524320 | tf_op jit(solution)/shard_map/ppermute | solution.py:20
  529.4 9.2 %all-to-all-done.6.refs_4_ = bf16[4,128,1024]{2,1,0:T(8,128)(2,1)S(1)} async-done(((bf16[4,128,1024]{2,1,0:T(8,128)(2,1)}), bf16[4,128,1024]{2,1,0:T(8,128)(2,1)S(1)}, u32[]{:S(2)}, u32[]{:S(2)}) %all-to-all-start.6) | async-done | bytes 1048608 | tf_op jit(solution)/shard_map/all_to_all | solution.py:96
  552.4 5.6 all-to-all-done.5.refs_0_
  563.0 9.8 %collective-permute-done.51.refs_5_ = bf16[4,128,1024]{2,1,0:T(8,128)(2,1)} collective-permute-done((bf16[4,128,1024]{2,1,0:T(8,128)(2,1)S(1)}, bf16[4,128,1024]{2,1,0:T(8,128)(2,1)}, u32[]{:S(2)}, u32[]{:S(2)}) %collective-permute-start.51) | collective-permute-done | bytes 1048608 | tf_op jit(solution)/shard_map/ppermute | solution.py:20
  572.8 5.9 %spread.3 = (f32[128,6144]{1,0:T(8,128)}, f32[128,6144]{1,0:T(8,128)}, f32[128,6144]{1,0:T(8,128)}, f32[128,2048]{1,0:T(8,128)}) custom-call(s32[1]{0:T(128)} %bitcast.side_ref, bf16[4,128,768]{2,1,0:T(8,128)(2,1)S(1)} %all-to-all-done.3.refs_0_, bf16[4,128,768]{2,1,0:T(8,128)(2,1)S(1)} %copy-done.10, bf16[4,128,768]{2,1,0:T(8,128)(2,1)S(1)} %all-to-all-done.4.refs_2_, ...), custom_call_target="tpu_custom_call" | custom-call | tf_op jit(solution)/shard_map/spread/pallas_call | solution.py:142
  (371 shorter events, 263.9 us)
Async XLA Ops:
  7.2 27.4 %collective-permute-start.9 = (bf16[128,2048]{1,0:T(8,128)(2,1)}, bf16[128,2048]{1,0:T(8,128)(2,1)S(1)}, u32[]{:S(2)}, u32[]{:S(2)}) collective-permute-start(bf16[128,2048]{1,0:T(8,128)(2,1)} %param.16), channel_id=1, source_target_pairs={{0,2},{2,0},{1,3},{3,1},{4,6},{6,4},{5,7},{7,5},{8,10},{10,8},{9,1... | collective-permute-start | bytes 1572872 | tf_op jit(solution)/shard_map/ppermute | solution.py:24
  10.2 25.0 %collective-permute-start.8 = (bf16[128,2048]{1,0:T(8,128)(2,1)}, bf16[128,2048]{1,0:T(8,128)(2,1)S(1)}, u32[]{:S(2)}, u32[]{:S(2)}) collective-permute-start(bf16[128,2048]{1,0:T(8,128)(2,1)} %param.16), channel_id=1, source_target_pairs={{0,16},{16,0},{1,17},{17,1},{2,18},{18,2},{3,19},{19,3},{4,20},{20... | collective-permute-start | bytes 1572872 | tf_op jit(solution)/shard_map/ppermute | solution.py:20
  16.7 15.7 %all-to-all-start = ((bf16[4,128,768]{2,1,0:T(8,128)(2,1)}), bf16[4,128,768]{2,1,0:T(8,128)(2,1)S(1)}, u32[]{:S(2)}, u32[]{:S(2)}) async-start(bf16[4,128,768]{2,1,0:T(8,128)(2,1)} %pick_columns.2), calls=%async_computation | async-start | bytes 1572864 | tf_op jit(solution)/shard_map/all_to_all | solution.py:96
  20.4 77.8 %all-gather.4.cloned.1.call-start = ((), (), s32[]{:S(2)}) async-start(), calls=%async_computation.11 | async-start | bytes 3932160 | tf_op jit(solution)/shard_map/all_gather | solution.py:101
  21.6 22.1 %collective-permute-start.1 = (bf16[128,2048]{1,0:T(8,128)(2,1)S(1)}, bf16[128,2048]{1,0:T(8,128)(2,1)S(1)}, u32[]{:S(2)}, u32[]{:S(2)}) collective-permute-start(bf16[128,2048]{1,0:T(8,128)(2,1)S(1)} %get-tuple-element.84), channel_id=1, source_target_pairs={{0,2},{2,0},{1,3},{3,1},{4,6},{6,4},{5,7},{7,5},{8,10},{10,8},{9,1... | collective-permute-start | bytes 1572872 | tf_op jit(solution)/shard_map/ppermute | solution.py:24
  23.6 20.8 %collective-permute-start = (bf16[128,2048]{1,0:T(8,128)(2,1)S(1)}, bf16[128,2048]{1,0:T(8,128)(2,1)}, u32[]{:S(2)}, u32[]{:S(2)}) collective-permute-start(bf16[128,2048]{1,0:T(8,128)(2,1)S(1)} %get-tuple-element.84), channel_id=1, source_target_pairs={{0,16},{16,0},{1,17},{17,1},{2,18},{18,2},{3,19},{19,3},{4,20},{20... | collective-permute-start | bytes 1572872 | tf_op jit(solution)/shard_map/ppermute | solution.py:20
  34.6 22.4 %collective-permute-start.11 = (bf16[64,2048]{1,0:T(8,128)(2,1)S(1)}, bf16[64,2048]{1,0:T(8,128)(2,1)S(1)}, u32[]{:S(2)}, u32[]{:S(2)}) collective-permute-start(bf16[64,2048]{1,0:T(8,128)(2,1)S(1)} %slice.461), channel_id=1, source_target_pairs={{0,16},{16,0},{1,17},{17,1},{2,18},{18,2},{3,19},{19,3},{4,20},{20... | collective-permute-start | bytes 786440 | tf_op jit(solution)/shard_map/ppermute | solution.py:20
  35.2 20.8 %collective-permute-start.10 = (bf16[64,2048]{1,0:T(8,128)(2,1)S(1)}, bf16[64,2048]{1,0:T(8,128)(2,1)S(1)}, u32[]{:S(2)}, u32[]{:S(2)}) collective-permute-start(bf16[64,2048]{1,0:T(8,128)(2,1)S(1)} %slice.460), channel_id=1, source_target_pairs={{0,2},{2,0},{1,3},{3,1},{4,6},{6,4},{5,7},{7,5},{8,10},{10,8},{9,1... | collective-permute-start | bytes 786440 | tf_op jit(solution)/shard_map/ppermute | solution.py:24
  56.0 36.8 %collective-permute-start.4 = (bf16[512,2048]{1,0:T(8,128)(2,1)}, bf16[512,2048]{1,0:T(8,128)(2,1)S(1)}, u32[]{:S(2)}, u32[]{:S(2)}) collective-permute-start(bf16[512,2048]{1,0:T(8,128)(2,1)} %get-tuple-element.152), channel_id=1, source_target_pairs={{0,1},{1,0},{2,3},{3,2},{4,5},{5,4},{6,7},{7,6},{8,9},{9,8},{10,11... | collective-permute-start | bytes 6291464 | tf_op jit(solution)/shard_map/ppermute | solution.py:28
  58.3 34.7 %collective-permute-start.12 = (bf16[512,2048]{1,0:T(8,128)(2,1)}, bf16[512,2048]{1,0:T(8,128)(2,1)}, u32[]{:S(2)}, u32[]{:S(2)}) collective-permute-start(bf16[512,2048]{1,0:T(8,128)(2,1)} %get-tuple-element.148), channel_id=1, source_target_pairs={{0,1},{1,0},{2,3},{3,2},{4,5},{5,4},{6,7},{7,6},{8,9},{9,8},{10,11... | collective-permute-start | bytes 6291464 | tf_op jit(solution)/shard_map/ppermute | solution.py:28
  61.3 54.2 %all-to-all-start.1 = ((bf16[4,128,1536]{2,1,0:T(8,128)(2,1)}), bf16[4,128,1536]{2,1,0:T(8,128)(2,1)}, u32[]{:S(2)}, u32[]{:S(2)}) async-start(bf16[4,128,1536]{2,1,0:T(8,128)(2,1)} %get-tuple-element.44), calls=%async_computation.1 | async-start | bytes 3145728 | tf_op jit(solution)/shard_map/all_to_all | solution.py:96
  65.6 164.9 %all-gather.6.cloned.1.call-start = ((), (), s32[]{:S(2)}) async-start(), calls=%async_computation.12 | async-start | bytes 7864320 | tf_op jit(solution)/shard_map/all_gather | solution.py:101
  65.7 20.1 %collective-permute-start.6 = (s32[2,256]{1,0:T(2,128)S(1)}, s32[2,256]{1,0:T(2,128)S(1)}, u32[]{:S(2)}, u32[]{:S(2)}) collective-permute-start(s32[2,256]{1,0:T(2,128)S(1)} %pad_add_fusion.1), channel_id=1, source_target_pairs={{0,2},{2,0},{1,3},{3,1},{4,6},{6,4},{5,7},{7,5},{8,10},{10,8},{9,1... | collective-permute-start | bytes 6152 | tf_op jit(solution)/shard_map/ppermute | solution.py:24
  115.5 178.4 %all-gather.8.cloned.1.call-start = ((), (), s32[]{:S(2)}) async-start(), calls=%async_computation.13 | async-start | bytes 3932160 | tf_op jit(solution)/shard_map/all_gather | solution.py:101
  175.0 15.1 %collective-permute-start.22 = (bf16[512,2048]{1,0:T(8,128)(2,1)}, bf16[512,2048]{1,0:T(8,128)(2,1)}, u32[]{:S(2)}, u32[]{:S(2)}) collective-permute-start(bf16[512,2048]{1,0:T(8,128)(2,1)} %get-tuple-element.144), channel_id=1, source_target_pairs={{0,1},{1,0},{2,3},{3,2},{4,5},{5,4},{6,7},{7,6},{8,9},{9,8},{10,11... | collective-permute-start | bytes 6291464 | tf_op jit(solution)/shard_map/ppermute | solution.py:28
  189.9 259.5 %reduce-scatter.5.cloned.1.call-start = ((), (), s32[]{:S(2)}) async-start(), calls=%async_computation.14 | async-start | bytes 3932160 | tf_op jit(solution)/shard_map/reduce_scatter | solution.py:105
  293.9 167.8 %reduce-scatter.7.cloned.1.call-start = ((), (), s32[]{:S(2)}) async-start(), calls=%async_computation.15 | async-start | bytes 3932160 | tf_op jit(solution)/shard_map/reduce_scatter | solution.py:105
  322.7 175.6 %reduce-scatter.9.cloned.1.call-start = ((), (), s32[]{:S(2)}) async-start(), calls=%async_computation.16 | async-start | bytes 5242880 | tf_op jit(solution)/shard_map/reduce_scatter | solution.py:105
  328.1 14.3 %collective-permute-start.24 = (bf16[128,2048]{1,0:T(8,128)(2,1)S(1)}, bf16[128,2048]{1,0:T(8,128)(2,1)S(1)}, u32[]{:S(2)}, u32[]{:S(2)}) collective-permute-start(bf16[128,2048]{1,0:T(8,128)(2,1)S(1)} %pad_maximum_fusion.24), channel_id=1, source_target_pairs={{0,16},{16,0},{1,17},{17,1},{2,18},{18,2},{3,19},{19,3},{4,20},{20... | collective-permute-start | bytes 1572872 | tf_op jit(solution)/shard_map/ppermute | solution.py:20
  332.2 15.4 %collective-permute-start.26 = (bf16[128,2048]{1,0:T(8,128)(2,1)S(1)}, bf16[128,2048]{1,0:T(8,128)(2,1)S(1)}, u32[]{:S(2)}, u32[]{:S(2)}) collective-permute-start(bf16[128,2048]{1,0:T(8,128)(2,1)S(1)} %pad_maximum_fusion.25), channel_id=1, source_target_pairs={{0,2},{2,0},{1,3},{3,1},{4,6},{6,4},{5,7},{7,5},{8,10},{10,8},{9,1... | collective-permute-start | bytes 1572872 | tf_op jit(solution)/shard_map/ppermute | solution.py:24
  449.2 49.2 %collective-permute-start.33 = (bf16[512,2048]{1,0:T(8,128)(2,1)}, bf16[512,2048]{1,0:T(8,128)(2,1)}, u32[]{:S(2)}, u32[]{:S(2)}) collective-permute-start(bf16[512,2048]{1,0:T(8,128)(2,1)} %convolution_convert_fusion.6), channel_id=1, source_target_pairs={{0,1},{1,0},{2,3},{3,2},{4,5},{5,4},{6,7},{7,6},{8,9},{9,8},{10,11... | collective-permute-start | bytes 6291464 | tf_op jit(solution)/shard_map/ppermute | solution.py:28
  451.7 15.1 %all-to-all-start.3 = ((bf16[4,128,768]{2,1,0:T(8,128)(2,1)}), bf16[4,128,768]{2,1,0:T(8,128)(2,1)S(1)}, u32[]{:S(2)}, u32[]{:S(2)}) async-start(bf16[4,128,768]{2,1,0:T(8,128)(2,1)} %bitcast.11), calls=%async_computation.4 | async-start | bytes 1572864 | tf_op jit(solution)/shard_map/all_to_all | solution.py:96
  455.2 16.0 %collective-permute-start.45 = (f32[1,4352]{1,0:T(1,128)S(1)}, f32[1,4352]{1,0:T(1,128)S(1)}, u32[]{:S(2)}, u32[]{:S(2)}) collective-permute-start(f32[1,4352]{1,0:T(1,128)S(1)} %add.205), channel_id=1, source_target_pairs={{0,16},{16,0},{1,17},{17,1},{2,18},{18,2},{3,19},{19,3},{4,20},{20... | collective-permute-start | bytes 52232 | tf_op jit(solution)/shard_map/ppermute | solution.py:154
  466.8 15.1 %all-to-all-start.4 = ((bf16[4,128,768]{2,1,0:T(8,128)(2,1)}), bf16[4,128,768]{2,1,0:T(8,128)(2,1)S(1)}, u32[]{:S(2)}, u32[]{:S(2)}) async-start(bf16[4,128,768]{2,1,0:T(8,128)(2,1)} %bitcast.12), calls=%async_computation.6 | async-start | bytes 1572864 | tf_op jit(solution)/shard_map/all_to_all | solution.py:96
  470.3 75.4 %reduce-scatter.11.cloned.1.call-start = ((), (), s32[]{:S(2)}) async-start(), calls=%async_computation.17 | async-start | bytes 2621440 | tf_op jit(solution)/shard_map/reduce_scatter | solution.py:105
  470.6 20.0 %collective-permute-start.48 = (bf16[4,128,768]{2,1,0:T(8,128)(2,1)S(1)}, bf16[4,128,768]{2,1,0:T(8,128)(2,1)S(1)}, u32[]{:S(2)}, u32[]{:S(2)}) collective-permute-start(bf16[4,128,768]{2,1,0:T(8,128)(2,1)S(1)} %all-to-all-done.3.refs_0_), channel_id=1, source_target_pairs={{0,16},{16,0},{1,17},{17,1},{2,18},{18,2},{3,19},{19,3},{4,20},{20... | collective-permute-start | bytes 2359304 | tf_op jit(solution)/shard_map/ppermute | solution.py:20
  505.5 20.1 %collective-permute-start.36 = (bf16[128,2048]{1,0:T(8,128)(2,1)}, bf16[128,2048]{1,0:T(8,128)(2,1)}, u32[]{:S(2)}, u32[]{:S(2)}) collective-permute-start(bf16[128,2048]{1,0:T(8,128)(2,1)} %pad_maximum_fusion.27), channel_id=1, source_target_pairs={{0,2},{2,0},{1,3},{3,1},{4,6},{6,4},{5,7},{7,5},{8,10},{10,8},{9,1... | collective-permute-start | bytes 1572872 | tf_op jit(solution)/shard_map/ppermute | solution.py:24
  520.6 18.0 %all-to-all-start.6 = ((bf16[4,128,1024]{2,1,0:T(8,128)(2,1)}), bf16[4,128,1024]{2,1,0:T(8,128)(2,1)S(1)}, u32[]{:S(2)}, u32[]{:S(2)}) async-start(bf16[4,128,1024]{2,1,0:T(8,128)(2,1)} %bitcast.46), calls=%async_computation.10 | async-start | bytes 2097152 | tf_op jit(solution)/shard_map/all_to_all | solution.py:96
  524.2 20.4 %collective-permute-start.49 = (bf16[4,128,768]{2,1,0:T(8,128)(2,1)S(1)}, bf16[4,128,768]{2,1,0:T(8,128)(2,1)S(1)}, u32[]{:S(2)}, u32[]{:S(2)}) collective-permute-start(bf16[4,128,768]{2,1,0:T(8,128)(2,1)S(1)} %all-to-all-done.4.refs_2_), channel_id=1, source_target_pairs={{0,16},{16,0},{1,17},{17,1},{2,18},{18,2},{3,19},{19,3},{4,20},{20... | collective-permute-start | bytes 2359304 | tf_op jit(solution)/shard_map/ppermute | solution.py:20
  528.1 22.2 %collective-permute-start.37 = (bf16[64,2048]{1,0:T(8,128)(2,1)}, bf16[64,2048]{1,0:T(8,128)(2,1)}, u32[]{:S(2)}, u32[]{:S(2)}) collective-permute-start(bf16[64,2048]{1,0:T(8,128)(2,1)} %get-tuple-element.90), channel_id=1, source_target_pairs={{0,16},{16,0},{1,17},{17,1},{2,18},{18,2},{3,19},{19,3},{4,20},{20... | collective-permute-start | bytes 786440 | tf_op jit(solution)/shard_map/ppermute | solution.py:20
  538.6 34.2 %collective-permute-start.51 = (bf16[4,128,1024]{2,1,0:T(8,128)(2,1)S(1)}, bf16[4,128,1024]{2,1,0:T(8,128)(2,1)}, u32[]{:S(2)}, u32[]{:S(2)}) collective-permute-start(bf16[4,128,1024]{2,1,0:T(8,128)(2,1)S(1)} %all-to-all-done.6.refs_4_), channel_id=1, source_target_pairs={{0,16},{16,0},{1,17},{17,1},{2,18},{18,2},{3,19},{19,3},{4,20},{20... | collective-permute-start | bytes 3145736 | tf_op jit(solution)/shard_map/ppermute | solution.py:20
  557.9 25.5 %collective-permute-start.50 = (bf16[4,128,512]{2,1,0:T(8,128)(2,1)S(1)}, bf16[4,128,512]{2,1,0:T(8,128)(2,1)S(1)}, u32[]{:S(2)}, u32[]{:S(2)}) collective-permute-start(bf16[4,128,512]{2,1,0:T(8,128)(2,1)S(1)} %all-to-all-done.5.refs_0_), channel_id=1, source_target_pairs={{0,16},{16,0},{1,17},{17,1},{2,18},{18,2},{3,19},{19,3},{4,20},{20... | collective-permute-start | bytes 1572872 | tf_op jit(solution)/shard_map/ppermute | solution.py:20
  (99 other events, 784.5 us)
Sparse Core Ops, SparseCore 0:
  33.5 64.3 all-gather.3
  115.7 114.8 all-gather.5
  232.1 61.7 all-gather.7
  296.6 58.8 reduce-scatter.4
  358.3 60.2 reduce-scatter.6
  420.8 77.5 reduce-scatter.8
  501.3 44.3 reduce-scatter.10
